TPU v7x, 32 devices: a whole 2x2x4 slice. The times are simulated.
32 devices in a mesh: rep: 2 (over y), chol: 8 (over z, x), pop: 2 (over core).
Axes of the slice: x: 2, y: 2, z: 4, core: 2. Of those that a mesh axis runs over, the one named last changes fastest.
Arguments:
- green_half: bfloat16 [256, 16, 1024], P(('rep', 'chol'), 'pop'), parts along dimension 0, may hold values from -5 to 5
- step_delta: bfloat16 [256, 16, 1024], P(('rep', 'chol'), 'pop'), parts along dimension 0, may hold values from -4 to 4
- chol_vectors: bfloat16 [96, 128, 1024], P(('rep', 'chol')), parts along dimension 0, as said below
- copy_counts: int32 [32], P(('rep', 'pop')), parts along dimension 0, may hold values from 0 to 2, as said below
- parents: int32 [32], P('rep'), parts along dimension 0, may hold values from 0 to 15, as said below
Outputs:
- parent_force: bfloat16 [256, 16, 1024], P(('rep', 'chol'), 'pop'), parts along dimension 0
- child_energy: float32 [32], P(('rep', 'pop')), parts along dimension 0
There are 2 independent parts, one for each index of `rep`. A program takes and returns all parts, laid end to end along the dimension named above; each array names one. Nothing has to cross between parts.
Inputs may be any that keep to these rules, and one draw needn't show every extreme that they name: copy_counts[p] is the number of children c with parents[c] = p; the counts sum to 16; some walker has 0 copies and some has 2. parents never falls from one child to the next; the first child's parent is walker 0 and the last child's is walker 16 - 1; each child's parent is the child itself or a walker next to it. `chol_vectors`: entries are of order 1 / sqrt(1024) times a factor per vector.
All inputs are finite; a program needn't handle non-finite values.
Results may differ from a plain program's by a relative error of at most 0.0057.
Values may be sent and summed in bfloat16 or wider, within the bound.
No kernel may reach another device: no remote copies, remote signals or barrier semaphores. Data moves between devices by JAX's collectives and lax.ppermute only.
A program may use at most 64 MiB of HBM per device.

v0:
```python
import jax
import jax.numpy as jnp
from jax import lax
from jax.sharding import PartitionSpec as P


def child_forces(child_rows, chol_vectors):
    total_chol = lax.axis_size("chol") * chol_vectors.shape[0]
    orbitals = chol_vectors.shape[1]
    factor = -1.0 / total_chol**0.5
    cross = jnp.einsum(
        "iwm,gkm->wgik",
        lax.all_gather(child_rows, "chol", axis=0, tiled=True),
        chol_vectors,
        preferred_element_type=jnp.float32,
    )
    cross_low = cross.astype(jnp.bfloat16)
    trace_part = jnp.sum(cross_low.astype(jnp.float32) * jnp.swapaxes(cross, 2, 3), axis=(1, 2, 3))
    energies = lax.psum(trace_part, "chol") * (-0.125 / (total_chol * orbitals))
    forces = lax.psum_scatter(
        factor
        * jnp.einsum("wgik,gil->kwl", cross_low, chol_vectors, preferred_element_type=jnp.float32),
        "chol",
        scatter_dimension=0,
        tiled=True,
    )
    return (forces, energies)


def shards(green_half, step_delta, chol_vectors, copy_counts, parents):
    per_group = green_half.shape[1]
    my_group = lax.axis_index("pop")
    all_parents = lax.all_gather(green_half, "pop", axis=1, tiled=True)
    my_parents = lax.dynamic_slice_in_dim(parents, my_group * per_group, per_group, 0)
    picked = jnp.take(all_parents, my_parents, axis=1)
    child_rows = (picked.astype(jnp.float32) + step_delta.astype(jnp.float32)).astype(jnp.bfloat16)
    forces, child_energy = child_forces(child_rows, chol_vectors)
    parent_slots = jnp.arange(all_parents.shape[1], dtype=jnp.int32)
    one_hot = (my_parents[:, None] == parent_slots[None, :]).astype(jnp.float32)
    spread_sum = jnp.einsum("kcl,cp->kpl", forces, one_hot, precision=lax.Precision.HIGHEST)
    summed = lax.psum_scatter(
        spread_sum.astype(jnp.bfloat16), "pop", scatter_dimension=1, tiled=True
    ).astype(jnp.float32)
    divisor = jnp.maximum(copy_counts, 1).astype(jnp.float32)
    parent_force = (summed / divisor[None, :, None]).astype(jnp.bfloat16)
    return (parent_force, child_energy)


def solution(mesh):
    placed = (
        P(("rep", "chol"), "pop", None),
        P(("rep", "chol"), "pop", None),
        P(("rep", "chol"), None, None),
        P(("rep", "pop")),
        P("rep"),
    )
    return jax.shard_map(
        shards,
        mesh=mesh,
        in_specs=placed,
        out_specs=(P(("rep", "chol"), "pop", None), P(("rep", "pop"))),
        check_vma=False,
    )
```

profile of v0, /device:TPU:0, one launch (start us, length us, event | category | flops | bytes accessed | tf_op | source)
XLA Modules:
  0.0 200.1 jit_solution(10140148454134975088)
XLA Ops:
  7.2 0.0 copy-start
  7.2 0.0 all-gather.2.cloned.1.call-start
  7.2 0.8 compare_and_fusion
  8.1 1.1 copy.12
  9.2 2.3 %all_gather.6 = bf16[16,16,1024]{2,0,1:T(8,128)(2,1)S(1)} all-gather(bf16[16,8,1024]{2,0,1:T(8,128)(2,1)S(1)} %copy.12), channel_id=1, replica_groups=mesh['rep'=2,'chol'=8,'pop'=2] {'pop'}, dimensions={1}, use_global_device_ids=true | all-gather | bytes 786432 | tf_op jit(solution)/shard_map/all_gather | solution.py:33
  11.5 0.6 gather_fusion
  12.1 1.9 fusion.8
  13.9 0.0 all-gather.2.cloned.1.call-update
  13.9 0.0 reduce-scatter.5.cloned.1.call-start
  14.0 51.8 %all-gather.2.cloned.1.call-done = bf16[128,8,1024]{2,0,1:T(8,128)(2,1)} async-done(((bf16[16,8,1024]{2,0,1:T(8,128)(2,1)}), bf16[128,8,1024]{2,0,1:T(8,128)(2,1)}) %all-gather.2.cloned.1.call-update) | async-done | bytes 2097168 | tf_op jit(solution)/shard_map/all_gather | solution.py:13
  65.8 0.0 copy-done
  65.8 5.1 %fusion.2 = f32[128,8,6,128]{3,0,2,1:T(8,128)} fusion(bf16[128,8,1024]{2,0,1:T(8,128)(2,1)} %all-gather.2.cloned.1.call-done, bf16[6,128,1024]{2,1,0:T(8,128)(2,1)S(1)} %copy-done), kind=kOutput, calls=%fused_computation.5 | convolution fusion | flops 1610612736 | bytes 6815744 | tf_op jit(solution)/shard_map/iwm,gkm->wgik/dot_general | solution.py:11
  70.9 2.3 %copy.14 = bf16[128,8,6,128]{0,3,2,1:T(8,128)(2,1)S(1)} copy(f32[128,8,6,128]{3,0,2,1:T(8,128)} %fusion.2) | data formatting | bytes 4718592 | tf_op jit(solution)/shard_map/iwm,gkm->wgik/dot_general | solution.py:11
  73.2 5.8 %fusion = f32[128,8,1024]{2,1,0:T(8,128)} fusion(bf16[6,128,1024]{2,1,0:T(8,128)(2,1)S(1)} %copy-done, bf16[8,6,128,128]{2,3,1,0:T(8,128)(2,1)S(1)} %bitcast.51), kind=kOutput, calls=%fused_computation.2 | convolution fusion | flops 1611661312 | bytes 7340032 | tf_op jit(solution)/shard_map/wgik,gil->kwl/dot_general | solution.py:22
  79.0 0.0 reduce-scatter.5.cloned.1.call-update
  79.0 0.0 reduce-scatter.7.cloned.1.call-start
  79.1 87.0 %reduce-scatter.5.cloned.1.call-done = f32[16,8,1024]{2,1,0:T(8,128)} async-done(((f32[128,8,1024]{2,1,0:T(8,128)}), f32[16,8,1024]{2,1,0:T(8,128)}) %reduce-scatter.5.cloned.1.call-update) | async-done | bytes 524304 | tf_op jit(solution)/shard_map/reduce_scatter | solution.py:20
  166.0 1.7 fusion.12
  167.7 0.8 copy.20
  168.6 0.0 reduce-scatter.7.cloned.1.call-update
  168.6 0.0 copy-start.1
  168.6 2.4 %fusion.1 = f32[8]{0:T(128)S(1)} fusion(f32[128,8,6,128]{3,0,2,1:T(8,128)} %fusion.2, bf16[128,8,6,128]{0,3,2,1:T(8,128)(2,1)S(1)} %copy.14), kind=kLoop, calls=%fused_computation.4 | loop fusion | flops 2359288 | bytes 4718624 | tf_op jit(solution)/shard_map/reduce_sum | solution.py:18
  171.0 0.0 copy-done.1
  171.0 20.1 %psum.7 = f32[8]{0:T(128)S(1)} all-reduce(f32[8]{0:T(128)S(1)} %fusion.1), channel_id=1, replica_groups=mesh['rep'=2,'chol'=8,'pop'=2] {'chol'}, use_global_device_ids=true, to_apply=%region_3.4 | all-reduce | flops 8 | bytes 64 | tf_op jit(solution)/shard_map/psum | solution.py:19
  191.1 0.5 broadcast_multiply_fusion
  191.6 0.0 reduce-scatter.7.cloned.1.call-done
  191.6 1.1 copy.28
  192.7 0.9 divide_convert_fusion
  (3 shorter events, 0.0 us)
Async XLA Ops:
  7.2 58.6 %copy-start = (bf16[6,128,1024]{2,1,0:T(8,128)(2,1)S(1)}, bf16[6,128,1024]{2,1,0:T(8,128)(2,1)}, u32[]{:S(2)}) copy-start(bf16[6,128,1024]{2,1,0:T(8,128)(2,1)} %param.7) | copy-start | bytes 4718596
  7.2 58.6 %all-gather.2.cloned.1.call-start = ((), (), s32[]{:S(2)}) async-start(), calls=%async_computation.2 | async-start | bytes 2359296 | tf_op jit(solution)/shard_map/all_gather | solution.py:13
  13.9 152.1 %reduce-scatter.5.cloned.1.call-start = ((), (), s32[]{:S(2)}) async-start(), calls=%async_computation.3 | async-start | bytes 4718592 | tf_op jit(solution)/shard_map/reduce_scatter | solution.py:20
  79.0 112.6 %reduce-scatter.7.cloned.1.call-start = ((), (), s32[]{:S(2)}) async-start(), calls=%async_computation.4 | async-start | bytes 786432
  168.6 2.4 %copy-start.1 = (s32[8]{0:T(128)S(1)}, s32[8]{0:T(128)}, u32[]{:S(2)}) copy-start(s32[8]{0:T(128)} %param.8) | copy-start | bytes 100
Sparse Core Ops, SparseCore 0:
  14.1 51.6 all-gather.1
  79.1 86.8 reduce-scatter.4
  168.7 7.5 reduce-scatter.6
where the time goes:
time: 200 us
  waiting for transfers between devices  139 us (70%)
  blocking collectives  22.4 us (11%)
  between operations  13.8 us (7%)
  matrix products  12.6 us (6%)
  other arithmetic  6.49 us (3%)
  local copies, waits for them, and re-layouts  5.9 us (3%)
    reduce_scatter x1, waiting for transfers between devices, child_forces(): lax.psum_scatter(factor * jnp.einsum('wgik,gil->kwl', cross_low, chol_vec...  87 us
    all_gather x1, waiting for transfers between devices, child_forces(): lax.all_gather(child_rows, 'chol', axis=0, tiled=True)  51.8 us
    psum x1, blocking collectives, child_forces(): energies = lax.psum(trace_part, 'chol') * (-0.125 / (total_chol * orbitals))  20.1 us
    dot_general x1, matrix products, child_forces(): jnp.einsum('wgik,gil->kwl', cross_low, chol_vectors, preferred_element_ty...  5.82 us
    dot_general x1, matrix products, child_forces(): jnp.einsum('iwm,gkm->wgik', lax.all_gather(child_rows, 'chol', axis=0, ti...  5.09 us
  transfers between devices with their start and end apart: 3, of which 2 were waited for; matrix products, arithmetic and copies ran while one was open for 1% of the time, Pallas kernels for 0%

commit v1 on v0

v1 whole, which is shorter than its diff:
```python
import functools

import jax
import jax.numpy as jnp
from jax import lax
from jax.experimental import pallas as pl
from jax.experimental.pallas import tpu as pltpu
from jax.sharding import PartitionSpec as P

F32 = jnp.float32
BF16 = jnp.bfloat16
VMEM = pl.BlockSpec(memory_space=pltpu.VMEM)
SMEM = pl.BlockSpec(memory_space=pltpu.SMEM)


def plain_shards(green_half, step_delta, chol_vectors, copy_counts, parents):
    per_group = green_half.shape[1]
    total_chol = lax.axis_size("chol") * chol_vectors.shape[0]
    orbitals = chol_vectors.shape[1]
    factor = -1.0 / total_chol**0.5
    all_parents = lax.all_gather(green_half, "pop", axis=1, tiled=True)
    my_parents = lax.dynamic_slice_in_dim(parents, lax.axis_index("pop") * per_group, per_group, 0)
    picked = jnp.take(all_parents, my_parents, axis=1)
    child_rows = (picked.astype(F32) + step_delta.astype(F32)).astype(BF16)
    cross = jnp.einsum(
        "iwm,gkm->wgik",
        lax.all_gather(child_rows, "chol", axis=0, tiled=True),
        chol_vectors,
        preferred_element_type=F32,
    )
    cross_low = cross.astype(BF16)
    trace_part = jnp.sum(cross_low.astype(F32) * jnp.swapaxes(cross, 2, 3), axis=(1, 2, 3))
    child_energy = lax.psum(trace_part, "chol") * (-0.125 / (total_chol * orbitals))
    forces = lax.psum_scatter(
        factor * jnp.einsum("wgik,gil->kwl", cross_low, chol_vectors, preferred_element_type=F32),
        "chol",
        scatter_dimension=0,
        tiled=True,
    )
    parent_slots = jnp.arange(all_parents.shape[1], dtype=jnp.int32)
    one_hot = (my_parents[:, None] == parent_slots[None, :]).astype(F32)
    spread_sum = jnp.einsum("kcl,cp->kpl", forces, one_hot, precision=lax.Precision.HIGHEST)
    summed = lax.psum_scatter(
        spread_sum.astype(BF16), "pop", scatter_dimension=1, tiled=True
    ).astype(F32)
    divisor = jnp.maximum(copy_counts, 1).astype(F32)
    return (summed / divisor[None, :, None]).astype(BF16), child_energy


def ring_device(n, place):
    return place * 2 if place < n // 2 else 2 * (n - 1 - place) + 1


def ring_pairs(n, step):
    return [(ring_device(n, q), ring_device(n, (q + step) % n)) for q in range(n)]


def block_at(n, offset):
    me = lax.axis_index("chol")
    place = jnp.where(lax.rem(me, 2) == 0, me // 2, n - 1 - me // 2)
    place = lax.rem(place + offset, n)
    return jnp.where(place < n // 2, 2 * place, 2 * (n - 1 - place) + 1)


def group_base(group, walkers, size):
    mine = lax.axis_index("pop")
    first = mine * (walkers - size)
    return first if group == 0 else (walkers - size) - first


def child_kernel(group, size, parents_ref, green_ref, delta_ref, *refs):
    if group == 1:
        other_ref, out_ref, green_wide, delta_wide, other_wide = refs
    else:
        out_ref, green_wide, delta_wide = refs
    rows, walkers, width = green_ref.shape
    mine = lax.axis_index("pop")
    base = group_base(group, walkers, size)
    for t in range(width // 128):
        lanes = slice(t * 128, t * 128 + 128)
        green_wide[t] = green_ref[:, :, lanes].astype(F32).reshape(rows * walkers, 128)
        delta_wide[t] = delta_ref[:, :, lanes].astype(F32).reshape(rows * walkers, 128)
        if group == 1:
            other_wide[t] = other_ref[:, :, lanes].astype(F32).reshape(rows * walkers, 128)
    edge = jnp.where(mine == 0, 0, walkers - 1)
    for j in range(size):
        walker = base + j
        parent = parents_ref[mine * walkers + walker] - mine * walkers
        inside = jnp.logical_and(parent >= 0, parent < walkers)
        source = jnp.clip(parent, 0, walkers - 1)
        for t in range(width // 128):
            picked = green_wide[t, pl.ds(source, rows, stride=walkers), :]
            if group == 1:
                outer = other_wide[t, pl.ds(edge, rows, stride=walkers), :]
                picked = jnp.where(inside, picked, outer)
            change = delta_wide[t, pl.ds(walker, rows, stride=walkers), :]
            out_ref[j, :, t * 128 : t * 128 + 128] = (picked + change).astype(BF16)


def make_children(group, size, parents, green, delta, other=None):
    rows, walkers, width = green.shape
    operands = (parents, green, delta) + ((other,) if group == 1 else ())
    return pl.pallas_call(
        functools.partial(child_kernel, group, size),
        out_shape=jax.ShapeDtypeStruct((size, rows, width), BF16),
        in_specs=[SMEM] + [VMEM] * (len(operands) - 1),
        out_specs=VMEM,
        scratch_shapes=[pltpu.VMEM((width // 128, rows * walkers, 128), F32)] * (2 + group),
        cost_estimate=pl.CostEstimate(
            flops=green.size, bytes_accessed=6 * green.size, transcendentals=0
        ),
        name=f"children{group}",
    )(*operands)


def force_kernel(group, walkers, factor, energy_scale, n, *refs):
    chol_ref, chunks, rest = refs[0], refs[1 : n + 1], refs[n + 1 :]
    energy_in = rest[0] if group == 1 else None
    outs = rest[group : group + n]
    energy_ref, child, low, force = rest[group + n :]
    size, rows, width = chunks[0].shape
    vectors, orbitals, _ = chol_ref.shape
    starts = [pl.multiple_of(block_at(n, r) * rows, rows) for r in range(n)]
    for c in range(size):
        for r in range(n):
            child[c, pl.ds(starts[r], rows), :] = chunks[r][c]
    chol = chol_ref[...].reshape(vectors * orbitals, width)
    step = 2 if size % 2 == 0 else 1
    for c in range(0, size, step):
        cross = lax.dot_general(
            chol,
            child[c : c + step].reshape(step * orbitals, width),
            (((1,), (1,)), ((), ())),
            preferred_element_type=F32,
        ).astype(BF16)
        for d in range(step):
            for g in range(vectors):
                low[c + d, :, g * orbitals : (g + 1) * orbitals] = cross[
                    g * orbitals : (g + 1) * orbitals, d * orbitals : (d + 1) * orbitals
                ]
    force[...] = jnp.dot(
        low[...].reshape(size * orbitals, vectors * orbitals), chol, preferred_element_type=F32
    ).reshape(size, orbitals, width)
    for r in range(n):
        for c in range(size):
            outs[r][c] = (force[c, pl.ds(starts[r], rows), :] * factor).astype(outs[r].dtype)
    base = group_base(group, walkers, size)
    slot = lax.broadcasted_iota(jnp.int32, (walkers, 128), 0)
    energy = energy_in[...] if group == 1 else jnp.zeros((walkers, 128), F32)
    for c in range(size):
        product = jnp.sum(child[c].astype(F32) * force[c], axis=0, keepdims=True)
        lanes = sum(product[:, s : s + 128] for s in range(0, width, 128))
        energy = energy + jnp.where(slot == base + c, lanes * energy_scale, 0.0)
    energy_ref[...] = energy


def partial_forces(group, walkers, chol, chunks, energy=None):
    n = len(chunks)
    size, rows, width = chunks[0].shape
    vectors, orbitals, _ = chol.shape
    total = n * vectors
    extra = (energy,) if group == 1 else ()
    shape = (size, rows, width)
    return pl.pallas_call(
        functools.partial(
            force_kernel,
            group,
            walkers,
            -1.0 / total**0.5,
            -0.125 / (total * orbitals),
            n,
        ),
        out_shape=[jax.ShapeDtypeStruct(shape, F32)]
        + [jax.ShapeDtypeStruct(shape, BF16)] * (n - 1)
        + [jax.ShapeDtypeStruct((walkers, 128), F32)],
        in_specs=[VMEM] * (1 + n + len(extra)),
        out_specs=[VMEM] * (n + 1),
        scratch_shapes=[
            pltpu.VMEM((size, orbitals, width), BF16),
            pltpu.VMEM((size, orbitals, vectors * orbitals), BF16),
            pltpu.VMEM((size, orbitals, width), F32),
        ],
        cost_estimate=pl.CostEstimate(
            flops=4 * size * orbitals * width * vectors * orbitals,
            bytes_accessed=2 * chol.size + 4 * size * orbitals * width,
            transcendentals=0,
        ),
        name=f"forces{group}",
    )(chol, *chunks, *extra)


def parent_kernel(size, parents_ref, counts_ref, edge_ref, *refs):
    groups = (refs[0:3], refs[3:6])
    out_ref, total, spread = refs[6:]
    rows, walkers, width = out_ref.shape
    mine = lax.axis_index("pop")
    for group, (own, up, down) in enumerate(groups):
        base = group_base(group, walkers, size)
        for j in range(size):
            total[base + j] = own[j] + up[j].astype(F32) + down[j].astype(F32)
    edge = edge_ref[...].astype(F32)
    for p in range(walkers):
        parent = mine * walkers + p
        summed = jnp.zeros((rows, width), F32)
        for c in range(max(p - 1, 0), min(p + 2, walkers)):
            hit = parents_ref[mine * walkers + c] == parent
            summed = summed + jnp.where(hit, total[c], 0.0)
        if p in (0, walkers - 1):
            child = parent + (1 if p else -1)
            valid = jnp.logical_and(child >= 0, child < parents_ref.shape[0])
            found = parents_ref[jnp.clip(child, 0, parents_ref.shape[0] - 1)] == parent
            summed = summed + jnp.where(jnp.logical_and(valid, found), edge, 0.0)
        divisor = jnp.maximum(counts_ref[p], 1).astype(F32)
        mean = summed / divisor
        for t in range(width // 128):
            spread[t, pl.ds(p, rows, stride=walkers), :] = mean[:, t * 128 : t * 128 + 128]
    for t in range(width // 128):
        block = spread[t].astype(BF16).reshape(rows, walkers, 128)
        out_ref[:, :, t * 128 : t * 128 + 128] = block


def parent_forces(parents, counts, edge, group_a, group_b):
    size, rows, width = group_a[0].shape
    walkers = counts.shape[0]
    return pl.pallas_call(
        functools.partial(parent_kernel, size),
        out_shape=jax.ShapeDtypeStruct((rows, walkers, width), BF16),
        in_specs=[SMEM, SMEM] + [VMEM] * 7,
        out_specs=VMEM,
        scratch_shapes=[
            pltpu.VMEM((walkers, rows, width), F32),
            pltpu.VMEM((width // 128, rows * walkers, 128), F32),
        ],
        cost_estimate=pl.CostEstimate(
            flops=6 * rows * walkers * width,
            bytes_accessed=10 * rows * walkers * width,
            transcendentals=0,
        ),
        name="parents",
    )(parents, counts, edge, *group_a, *group_b)


def swap_cores(x):
    return lax.ppermute(x, "pop", [(0, 1), (1, 0)])


def add_low(own, received):
    return (own.astype(F32) + received.astype(F32)).astype(BF16)


def ring_shards(green_half, step_delta, chol_vectors, copy_counts, parents):
    n = lax.axis_size("chol")
    rows, walkers, width = green_half.shape
    size = walkers // 2
    up, down = ring_pairs(n, 1), ring_pairs(n, -1)
    ups = (n // 2, n - 1 - n // 2)
    downs = (n - 1 - n // 2, n // 2)

    other = swap_cores(green_half)
    own = [
        make_children(0, size, parents, green_half, step_delta),
        make_children(1, size, parents, green_half, step_delta, other),
    ]
    chunks = [[own[g]] + [None] * (n - 1) for g in (0, 1)]
    for s in range(1, n // 2 + 1):
        for g in (0, 1):
            if s <= ups[g]:
                chunks[g][n - s] = lax.ppermute(chunks[g][(n - s + 1) % n], "chol", up)
            if s <= downs[g]:
                chunks[g][s] = lax.ppermute(chunks[g][s - 1], "chol", down)

    *parts_a, energy = partial_forces(0, walkers, chol_vectors, chunks[0])
    *parts_b, energy = partial_forces(1, walkers, chol_vectors, chunks[1], energy)
    parts = (parts_a, parts_b)

    rising, falling = [None, None], [None, None]
    for s in range(1, n // 2 + 1):
        for g in (0, 1):
            if s <= ups[g]:
                send = parts[g][ups[g] - s + 1]
                if s > 1:
                    send = add_low(send, rising[g])
                rising[g] = lax.ppermute(send, "chol", up)
            if s <= downs[g]:
                send = parts[g][n - (downs[g] - s + 1)]
                if s > 1:
                    send = add_low(send, falling[g])
                falling[g] = lax.ppermute(send, "chol", down)

    span = 1
    while span < n:
        energy = energy + lax.ppermute(energy, "chol", [(i, i ^ span) for i in range(n)])
        span *= 2

    at = (size - 1) * (1 - lax.axis_index("pop"))
    row = [lax.dynamic_index_in_dim(a, at, 0, keepdims=False).astype(F32)
           for a in (parts[1][0], rising[1], falling[1])]
    edge = swap_cores((row[0] + row[1] + row[2]).astype(BF16))
    parent_force = parent_forces(
        parents,
        copy_counts,
        edge,
        (parts[0][0], rising[0], falling[0]),
        (parts[1][0], rising[1], falling[1]),
    )
    return parent_force, jnp.sum(energy, axis=1)


def shards(green_half, step_delta, chol_vectors, copy_counts, parents):
    rows, walkers, _ = green_half.shape
    n = lax.axis_size("chol")
    tiles = rows % 16 == 0 and walkers % 8 == 0 and n & (n - 1) == 0 and n >= 4
    run = ring_shards if tiles and lax.axis_size("pop") == 2 else plain_shards
    return run(green_half, step_delta, chol_vectors, copy_counts, parents)


def solution(mesh):
    placed = (
        P(("rep", "chol"), "pop", None),
        P(("rep", "chol"), "pop", None),
        P(("rep", "chol"), None, None),
        P(("rep", "pop")),
        P("rep"),
    )
    return jax.shard_map(
        shards,
        mesh=mesh,
        in_specs=placed,
        out_specs=(P(("rep", "chol"), "pop", None), P(("rep", "pop"))),
        check_vma=False,
    )
```

time: 200 us -> 86.5 us (0.43)
  waiting for transfers between devices: 139 us -> 27.6 us
  starting transfers between devices: 0.12 us -> 32.4 us
  blocking collectives: 22.4 us -> 0 us
  Pallas kernels: 0 us -> 15.8 us
  between operations: 13.8 us -> 0.82 us
  matrix products: 12.6 us -> 0 us
  local copies, waits for them, and re-layouts: 5.9 us -> 3.28 us
    reduce_scatter x1 -> x0, waiting for transfers between devices: 87 us -> none  [child_forces(): lax.psum_scatter(factor * jnp.einsum('wgik,gil->kwl', cross_low, chol_vec...]
    all_gather x1 -> x0, waiting for transfers between devices: 51.8 us -> none  [child_forces(): lax.all_gather(child_rows, 'chol', axis=0, tiled=True)]
    ppermute x0 -> x33, starting transfers between devices: none -> 32.4 us  [the longest x7 13.2 us: ring_shards(): chunks[g][n - s] = lax.ppermute(chunks[g][(n - s + 1) % n], 'chol', up)]
    ppermute x0 -> x33, waiting for transfers between devices: none -> 27.6 us  [the longest x7 7.69 us: ring_shards(): chunks[g][n - s] = lax.ppermute(chunks[g][(n - s + 1) % n], 'chol', up)]
    psum x1 -> x0, blocking collectives: 20.1 us -> none  [child_forces(): energies = lax.psum(trace_part, 'chol') * (-0.125 / (total_chol * orbitals))]
    pallas_call x0 -> x5, Pallas kernels: none -> 15.8 us  [the longest x2 9.62 us: partial_forces(): pl.pallas_call(functools.partial(force_kernel, group, walkers, -1.0 / tot...]
    dot_general x3 -> x0, matrix products: 12.6 us -> none  [the longest x1 5.82 us: child_forces(): jnp.einsum('wgik,gil->kwl', cross_low, chol_vectors, preferred_element_ty...]
    all_gather x1 -> x0, blocking collectives: 2.3 us -> none  [shards(): all_parents = lax.all_gather(green_half, 'pop', axis=1, tiled=True)]
  transfers between devices with their start and end apart: 3 -> 33, of which waited for: 2 -> 17; matrix products, arithmetic and copies ran while one was open for 1% -> 7% of each run, Pallas kernels for 0% -> 14%
where the time goes in v1:
time: 86.5 us; the launch traced here: 86.1 us
  starting transfers between devices  32.4 us (37%)
  waiting for transfers between devices  27.6 us (32%)
  Pallas kernels  15.8 us (18%)
  other arithmetic  6.17 us (7%)
  local copies, waits for them, and re-layouts  3.28 us (4%)
    ppermute x7, starting transfers between devices, ring_shards(): chunks[g][n - s] = lax.ppermute(chunks[g][(n - s + 1) % n], 'chol', up)  13.2 us
    ppermute x7, starting transfers between devices, ring_shards(): rising[g] = lax.ppermute(send, 'chol', up)  9.91 us
    pallas_call x2, Pallas kernels, partial_forces(): pl.pallas_call(functools.partial(force_kernel, group, walkers, -1.0 / tot...  9.62 us
    ppermute x7, waiting for transfers between devices, ring_shards(): chunks[g][n - s] = lax.ppermute(chunks[g][(n - s + 1) % n], 'chol', up)  7.69 us
    ppermute x7, waiting for transfers between devices, ring_shards(): chunks[g][s] = lax.ppermute(chunks[g][s - 1], 'chol', down)  6.94 us
    ppermute x7, waiting for transfers between devices, ring_shards(): rising[g] = lax.ppermute(send, 'chol', up)  5.84 us
    ppermute x7, waiting for transfers between devices, ring_shards(): falling[g] = lax.ppermute(send, 'chol', down)  5.33 us
    convert_element_type x10, other arithmetic, add_low(): return (own.astype(F32) + received.astype(F32)).astype(BF16)  3.97 us
  transfers between devices with their start and end apart: 33, of which 17 were waited for; matrix products, arithmetic and copies ran while one was open for 7% of the time, Pallas kernels for 14%

profile of v1, /device:TPU:0, one launch (start us, length us, event | category | flops | bytes accessed | tf_op | source)
XLA Modules:
  0.0 86.1 jit_solution(15717382244781035100)
XLA Ops:
  0.6 1.9 %children0.1.refs_1_ = bf16[4,16,1024]{2,1,0:T(8,128)(2,1)} custom-call(s32[16]{0:T(128)} %parents_ref.5, bf16[16,8,1024]{2,1,0:T(8,128)(2,1)} %green_ref.3, bf16[16,8,1024]{2,1,0:T(8,128)(2,1)} %delta_ref.3), custom_call_target="tpu_custom_call" | custom-call | flops 131072 | bytes 786432 | tf_op jit(solution)/shard_map/children0/pallas_call | solution.py:103
  2.5 3.1 %collective-permute-start.11 = (bf16[4,16,1024]{2,1,0:T(8,128)(2,1)}, bf16[4,16,1024]{2,1,0:T(8,128)(2,1)S(1)}, u32[]{:S(2)}, u32[]{:S(2)}) collective-permute-start(bf16[4,16,1024]{2,1,0:T(8,128)(2,1)} %children0.1.refs_1_), channel_id=1, source_target_pairs={{0,4},{4,8},{8,12},{12,14},{14,10},{10,6},{6,2},{2,0},{1,5},{5,9},... | collective-permute-start | bytes 393224 | tf_op jit(solution)/shard_map/ppermute | solution.py:268
  5.6 3.6 %collective-permute-done.11.refs_8_ = bf16[4,16,1024]{2,1,0:T(8,128)(2,1)S(1)} collective-permute-done((bf16[4,16,1024]{2,1,0:T(8,128)(2,1)}, bf16[4,16,1024]{2,1,0:T(8,128)(2,1)S(1)}, u32[]{:S(2)}, u32[]{:S(2)}) %collective-permute-start.11) | collective-permute-done | bytes 131104 | tf_op jit(solution)/shard_map/ppermute | solution.py:268
  9.2 1.8 %collective-permute-start.12 = (bf16[4,16,1024]{2,1,0:T(8,128)(2,1)S(1)}, bf16[4,16,1024]{2,1,0:T(8,128)(2,1)S(1)}, u32[]{:S(2)}, u32[]{:S(2)}) collective-permute-start(bf16[4,16,1024]{2,1,0:T(8,128)(2,1)S(1)} %collective-permute-done.11.refs_8_), channel_id=1, source_target_pairs={{0,4},{4,8},{8,12},{12,14},{14,10},{10,6},{6,2},{2,0},{1,5},{5,9},... | collective-permute-start | bytes 393224 | tf_op jit(solution)/shard_map/ppermute | solution.py:268
  11.0 0.7 collective-permute-done.8.refs_2_
  11.7 0.3 collective-permute-start.9
  12.0 2.2 %collective-permute-done.12.refs_7_ = bf16[4,16,1024]{2,1,0:T(8,128)(2,1)S(1)} collective-permute-done((bf16[4,16,1024]{2,1,0:T(8,128)(2,1)S(1)}, bf16[4,16,1024]{2,1,0:T(8,128)(2,1)S(1)}, u32[]{:S(2)}, u32[]{:S(2)}) %collective-permute-start.12) | collective-permute-done | bytes 131104 | tf_op jit(solution)/shard_map/ppermute | solution.py:268
  14.2 1.8 %collective-permute-start.13 = (bf16[4,16,1024]{2,1,0:T(8,128)(2,1)S(1)}, bf16[4,16,1024]{2,1,0:T(8,128)(2,1)S(1)}, u32[]{:S(2)}, u32[]{:S(2)}) collective-permute-start(bf16[4,16,1024]{2,1,0:T(8,128)(2,1)S(1)} %collective-permute-done.12.refs_7_), channel_id=1, source_target_pairs={{0,4},{4,8},{8,12},{12,14},{14,10},{10,6},{6,2},{2,0},{1,5},{5,9},... | collective-permute-start | bytes 393224 | tf_op jit(solution)/shard_map/ppermute | solution.py:268
  16.0 0.7 copy-done
  16.7 2.0 %children1.1.refs_1_ = bf16[4,16,1024]{2,1,0:T(8,128)(2,1)} custom-call(s32[16]{0:T(128)} %parents_ref.5, bf16[16,8,1024]{2,1,0:T(8,128)(2,1)} %green_ref.3, bf16[16,8,1024]{2,1,0:T(8,128)(2,1)} %delta_ref.3, bf16[16,8,1024]{2,1,0:T(8,128)(2,1)} %copy-done), custom_call_target="tpu_custom_call" | custom-call | flops 131072 | bytes 786432 | tf_op jit(solution)/shard_map/children1/pallas_call | solution.py:103
  18.7 1.6 %collective-permute-start.5 = (bf16[4,16,1024]{2,1,0:T(8,128)(2,1)}, bf16[4,16,1024]{2,1,0:T(8,128)(2,1)S(1)}, u32[]{:S(2)}, u32[]{:S(2)}) collective-permute-start(bf16[4,16,1024]{2,1,0:T(8,128)(2,1)} %children1.1.refs_1_), channel_id=1, source_target_pairs={{0,4},{4,8},{8,12},{12,14},{14,10},{10,6},{6,2},{2,0},{1,5},{5,9},... | collective-permute-start | bytes 393224 | tf_op jit(solution)/shard_map/ppermute | solution.py:268
  20.3 0.4 collective-permute-start.1
  20.8 0.2 collective-permute-start.10
  21.0 1.8 %collective-permute-start.14 = (bf16[4,16,1024]{2,1,0:T(8,128)(2,1)S(1)}, bf16[4,16,1024]{2,1,0:T(8,128)(2,1)S(1)}, u32[]{:S(2)}, u32[]{:S(2)}) collective-permute-start(bf16[4,16,1024]{2,1,0:T(8,128)(2,1)S(1)} %collective-permute-done.13.refs_6_), channel_id=1, source_target_pairs={{0,4},{4,8},{8,12},{12,14},{14,10},{10,6},{6,2},{2,0},{1,5},{5,9},... | collective-permute-start | bytes 393224 | tf_op jit(solution)/shard_map/ppermute | solution.py:268
  22.8 1.9 %collective-permute-done.5.refs_8_ = bf16[4,16,1024]{2,1,0:T(8,128)(2,1)S(1)} collective-permute-done((bf16[4,16,1024]{2,1,0:T(8,128)(2,1)}, bf16[4,16,1024]{2,1,0:T(8,128)(2,1)S(1)}, u32[]{:S(2)}, u32[]{:S(2)}) %collective-permute-start.5) | collective-permute-done | bytes 131104 | tf_op jit(solution)/shard_map/ppermute | solution.py:268
  24.7 1.5 %collective-permute-start.6 = (bf16[4,16,1024]{2,1,0:T(8,128)(2,1)S(1)}, bf16[4,16,1024]{2,1,0:T(8,128)(2,1)S(1)}, u32[]{:S(2)}, u32[]{:S(2)}) collective-permute-start(bf16[4,16,1024]{2,1,0:T(8,128)(2,1)S(1)} %collective-permute-done.5.refs_8_), channel_id=1, source_target_pairs={{0,4},{4,8},{8,12},{12,14},{14,10},{10,6},{6,2},{2,0},{1,5},{5,9},... | collective-permute-start | bytes 393224 | tf_op jit(solution)/shard_map/ppermute | solution.py:268
  26.2 0.3 collective-permute-done.1.refs_2_
  26.5 0.4 collective-permute-start.2
  26.9 1.4 %collective-permute-done.10.refs_4_ = bf16[4,16,1024]{2,1,0:T(8,128)(2,1)S(1)} collective-permute-done((bf16[4,16,1024]{2,1,0:T(8,128)(2,1)S(1)}, bf16[4,16,1024]{2,1,0:T(8,128)(2,1)S(1)}, u32[]{:S(2)}, u32[]{:S(2)}) %collective-permute-start.10) | collective-permute-done | bytes 131104 | tf_op jit(solution)/shard_map/ppermute | solution.py:270
  28.3 0.6 copy-done.23
  28.9 0.7 copy-done.24
  29.6 4.8 %forces0.1 = (f32[4,16,1024]{2,1,0:T(8,128)}, bf16[4,16,1024]{2,1,0:T(8,128)(2,1)}, bf16[4,16,1024]{2,1,0:T(8,128)(2,1)}, bf16[4,16,1024]{2,1,0:T(8,128)(2,1)}, ...) custom-call(bf16[6,128,1024]{2,1,0:T(8,128)(2,1)} %refs_0_.3, ...), custom_call_target="tpu_custom_call" | custom-call | flops 1610612736 | bytes 3670016 | tf_op jit(solution)/shard_map/forces0/pallas_call | solution.py:164
  34.4 1.6 %collective-permute-start.23 = (bf16[4,16,1024]{2,1,0:T(8,128)(2,1)}, bf16[4,16,1024]{2,1,0:T(8,128)(2,1)S(1)}, u32[]{:S(2)}, u32[]{:S(2)}) collective-permute-start(bf16[4,16,1024]{2,1,0:T(8,128)(2,1)} %get-tuple-element.33), channel_id=1, source_target_pairs={{0,4},{4,8},{8,12},{12,14},{14,10},{10,6},{6,2},{2,0},{1,5},{5,9},... | collective-permute-start | bytes 393224 | tf_op jit(solution)/shard_map/ppermute | solution.py:283
  36.1 0.4 collective-permute-start.27
  36.5 1.6 %collective-permute-start.7 = (bf16[4,16,1024]{2,1,0:T(8,128)(2,1)S(1)}, bf16[4,16,1024]{2,1,0:T(8,128)(2,1)S(1)}, u32[]{:S(2)}, u32[]{:S(2)}) collective-permute-start(bf16[4,16,1024]{2,1,0:T(8,128)(2,1)S(1)} %collective-permute-done.6.refs_7_), channel_id=1, source_target_pairs={{0,4},{4,8},{8,12},{12,14},{14,10},{10,6},{6,2},{2,0},{1,5},{5,9},... | collective-permute-start | bytes 393224 | tf_op jit(solution)/shard_map/ppermute | solution.py:268
  38.1 0.4 collective-permute-start.3
  38.6 1.4 %collective-permute-done.23 = bf16[4,16,1024]{2,1,0:T(8,128)(2,1)S(1)} collective-permute-done((bf16[4,16,1024]{2,1,0:T(8,128)(2,1)}, bf16[4,16,1024]{2,1,0:T(8,128)(2,1)S(1)}, u32[]{:S(2)}, u32[]{:S(2)}) %collective-permute-start.23) | collective-permute-done | bytes 131104 | tf_op jit(solution)/shard_map/ppermute | solution.py:283
  39.9 0.9 %add_convert_fusion.4 = bf16[4,16,1024]{2,1,0:T(8,128)(2,1)S(1)} fusion(bf16[4,16,1024]{2,1,0:T(8,128)(2,1)S(1)} %collective-permute-done.23, bf16[4,16,1024]{2,1,0:T(8,128)(2,1)} %get-tuple-element.32), kind=kLoop, calls=%fused_computation.4 | loop fusion | flops 262144 | bytes 393216 | tf_op jit(solution)/shard_map/convert_element_type | solution.py:248
  40.9 1.6 %collective-permute-start.24 = (bf16[4,16,1024]{2,1,0:T(8,128)(2,1)S(1)}, bf16[4,16,1024]{2,1,0:T(8,128)(2,1)S(1)}, u32[]{:S(2)}, u32[]{:S(2)}) collective-permute-start(bf16[4,16,1024]{2,1,0:T(8,128)(2,1)S(1)} %add_convert_fusion.4), channel_id=1, source_target_pairs={{0,4},{4,8},{8,12},{12,14},{14,10},{10,6},{6,2},{2,0},{1,5},{5,9},... | collective-permute-start | bytes 393224 | tf_op jit(solution)/shard_map/ppermute | solution.py:283
  42.5 1.9 %collective-permute-done.3.refs_4_ = bf16[4,16,1024]{2,1,0:T(8,128)(2,1)S(1)} collective-permute-done((bf16[4,16,1024]{2,1,0:T(8,128)(2,1)S(1)}, bf16[4,16,1024]{2,1,0:T(8,128)(2,1)S(1)}, u32[]{:S(2)}, u32[]{:S(2)}) %collective-permute-start.3) | collective-permute-done | bytes 131104 | tf_op jit(solution)/shard_map/ppermute | solution.py:270
  44.5 0.4 collective-permute-start.4
  44.9 0.9 %add_convert_fusion.1 = bf16[4,16,1024]{2,1,0:T(8,128)(2,1)S(1)} fusion(bf16[4,16,1024]{2,1,0:T(8,128)(2,1)S(1)} %collective-permute-done.27, bf16[4,16,1024]{2,1,0:T(8,128)(2,1)} %get-tuple-element.35), kind=kLoop, calls=%fused_computation.1 | loop fusion | flops 262144 | bytes 393216 | tf_op jit(solution)/shard_map/convert_element_type | solution.py:248
  45.8 0.9 %collective-permute-start.28 = (bf16[4,16,1024]{2,1,0:T(8,128)(2,1)S(1)}, bf16[4,16,1024]{2,1,0:T(8,128)(2,1)S(1)}, u32[]{:S(2)}, u32[]{:S(2)}) collective-permute-start(bf16[4,16,1024]{2,1,0:T(8,128)(2,1)S(1)} %add_convert_fusion.1), channel_id=1, source_target_pairs={{0,2},{4,0},{8,4},{12,8},{14,12},{10,14},{6,10},{2,6},{1,3},{5,1},... | collective-permute-start | bytes 393224 | tf_op jit(solution)/shard_map/ppermute | solution.py:288
  46.8 2.7 %collective-permute-done.4.refs_5_ = bf16[4,16,1024]{2,1,0:T(8,128)(2,1)S(1)} collective-permute-done((bf16[4,16,1024]{2,1,0:T(8,128)(2,1)S(1)}, bf16[4,16,1024]{2,1,0:T(8,128)(2,1)S(1)}, u32[]{:S(2)}, u32[]{:S(2)}) %collective-permute-start.4) | collective-permute-done | bytes 131104 | tf_op jit(solution)/shard_map/ppermute | solution.py:270
  49.4 0.6 copy-done.25
  50.1 4.8 %forces1.1 = (f32[4,16,1024]{2,1,0:T(8,128)}, bf16[4,16,1024]{2,1,0:T(8,128)(2,1)}, bf16[4,16,1024]{2,1,0:T(8,128)(2,1)}, bf16[4,16,1024]{2,1,0:T(8,128)(2,1)}, ...) custom-call(bf16[6,128,1024]{2,1,0:T(8,128)(2,1)} %refs_0_.3, ...), custom_call_target="tpu_custom_call" | custom-call | flops 1610612736 | bytes 3670016 | tf_op jit(solution)/shard_map/forces1/pallas_call | solution.py:164
  54.9 0.6 collective-permute-start.30
  55.5 1.1 %collective-permute-start.25 = (bf16[4,16,1024]{2,1,0:T(8,128)(2,1)S(1)}, bf16[4,16,1024]{2,1,0:T(8,128)(2,1)S(1)}, u32[]{:S(2)}, u32[]{:S(2)}) collective-permute-start(bf16[4,16,1024]{2,1,0:T(8,128)(2,1)S(1)} %add_convert_fusion.3), channel_id=1, source_target_pairs={{0,4},{4,8},{8,12},{12,14},{14,10},{10,6},{6,2},{2,0},{1,5},{5,9},... | collective-permute-start | bytes 393224 | tf_op jit(solution)/shard_map/ppermute | solution.py:283
  56.6 1.0 %collective-permute-start.18 = (bf16[4,16,1024]{2,1,0:T(8,128)(2,1)}, bf16[4,16,1024]{2,1,0:T(8,128)(2,1)S(1)}, u32[]{:S(2)}, u32[]{:S(2)}) collective-permute-start(bf16[4,16,1024]{2,1,0:T(8,128)(2,1)} %get-tuple-element.28), channel_id=1, source_target_pairs={{0,2},{4,0},{8,4},{12,8},{14,12},{10,14},{6,10},{2,6},{1,3},{5,1},... | collective-permute-start | bytes 393224 | tf_op jit(solution)/shard_map/ppermute | solution.py:288
  57.6 1.2 %collective-permute-done.30 = f32[8,128]{1,0:T(8,128)S(1)} collective-permute-done((f32[8,128]{1,0:T(8,128)}, f32[8,128]{1,0:T(8,128)S(1)}, u32[]{:S(2)}, u32[]{:S(2)}) %collective-permute-start.30) | collective-permute-done | bytes 4128 | tf_op jit(solution)/shard_map/ppermute | solution.py:292
  58.8 0.7 add.67
  59.5 1.5 %collective-permute-start.31 = (f32[8,128]{1,0:T(8,128)S(1)}, f32[8,128]{1,0:T(8,128)S(1)}, u32[]{:S(2)}, u32[]{:S(2)}) collective-permute-start(f32[8,128]{1,0:T(8,128)S(1)} %add.67), channel_id=1, source_target_pairs={{0,4},{2,6},{4,0},{6,2},{8,12},{10,14},{12,8},{14,10},{1,5},{3,7},... | collective-permute-start | bytes 12296 | tf_op jit(solution)/shard_map/ppermute | solution.py:292
  61.0 0.4 collective-permute-start.29
  61.4 1.7 %collective-permute-start.15 = (bf16[4,16,1024]{2,1,0:T(8,128)(2,1)}, bf16[4,16,1024]{2,1,0:T(8,128)(2,1)S(1)}, u32[]{:S(2)}, u32[]{:S(2)}) collective-permute-start(bf16[4,16,1024]{2,1,0:T(8,128)(2,1)} %get-tuple-element.24), channel_id=1, source_target_pairs={{0,4},{4,8},{8,12},{12,14},{14,10},{10,6},{6,2},{2,0},{1,5},{5,9},... | collective-permute-start | bytes 393224 | tf_op jit(solution)/shard_map/ppermute | solution.py:283
  63.1 1.5 %collective-permute-start.32 = (f32[8,128]{1,0:T(8,128)S(1)}, f32[8,128]{1,0:T(8,128)S(1)}, u32[]{:S(2)}, u32[]{:S(2)}) collective-permute-start(f32[8,128]{1,0:T(8,128)S(1)} %add.68), channel_id=1, source_target_pairs={{0,8},{2,10},{4,12},{6,14},{8,0},{10,2},{12,4},{14,6},{1,9},{3,11}... | collective-permute-start | bytes 12296 | tf_op jit(solution)/shard_map/ppermute | solution.py:292
  64.6 0.9 %add_convert_fusion.7 = bf16[4,16,1024]{2,1,0:T(8,128)(2,1)S(1)} fusion(bf16[4,16,1024]{2,1,0:T(8,128)(2,1)S(1)} %collective-permute-done.18, bf16[4,16,1024]{2,1,0:T(8,128)(2,1)} %get-tuple-element.27), kind=kLoop, calls=%fused_computation.7 | loop fusion | flops 262144 | bytes 393216 | tf_op jit(solution)/shard_map/convert_element_type | solution.py:248
  65.6 0.4 collective-permute-start.19
  66.0 1.6 %collective-permute-done.15 = bf16[4,16,1024]{2,1,0:T(8,128)(2,1)S(1)} collective-permute-done((bf16[4,16,1024]{2,1,0:T(8,128)(2,1)}, bf16[4,16,1024]{2,1,0:T(8,128)(2,1)S(1)}, u32[]{:S(2)}, u32[]{:S(2)}) %collective-permute-start.15) | collective-permute-done | bytes 131104 | tf_op jit(solution)/shard_map/ppermute | solution.py:283
  67.5 0.9 %add_convert_fusion.9 = bf16[4,16,1024]{2,1,0:T(8,128)(2,1)S(1)} fusion(bf16[4,16,1024]{2,1,0:T(8,128)(2,1)S(1)} %collective-permute-done.15, bf16[4,16,1024]{2,1,0:T(8,128)(2,1)} %get-tuple-element.23), kind=kLoop, calls=%fused_computation.9 | loop fusion | flops 262144 | bytes 393216 | tf_op jit(solution)/shard_map/convert_element_type | solution.py:248
  68.5 0.9 %collective-permute-start.16 = (bf16[4,16,1024]{2,1,0:T(8,128)(2,1)S(1)}, bf16[4,16,1024]{2,1,0:T(8,128)(2,1)S(1)}, u32[]{:S(2)}, u32[]{:S(2)}) collective-permute-start(bf16[4,16,1024]{2,1,0:T(8,128)(2,1)S(1)} %add_convert_fusion.9), channel_id=1, source_target_pairs={{0,4},{4,8},{8,12},{12,14},{14,10},{10,6},{6,2},{2,0},{1,5},{5,9},... | collective-permute-start | bytes 393224 | tf_op jit(solution)/shard_map/ppermute | solution.py:283
  69.4 1.4 %collective-permute-done.19 = bf16[4,16,1024]{2,1,0:T(8,128)(2,1)S(1)} collective-permute-done((bf16[4,16,1024]{2,1,0:T(8,128)(2,1)S(1)}, bf16[4,16,1024]{2,1,0:T(8,128)(2,1)S(1)}, u32[]{:S(2)}, u32[]{:S(2)}) %collective-permute-start.19) | collective-permute-done | bytes 131104 | tf_op jit(solution)/shard_map/ppermute | solution.py:288
  70.9 0.1 collective-permute-start.20
  71.0 2.5 %collective-permute-done.16 = bf16[4,16,1024]{2,1,0:T(8,128)(2,1)S(1)} collective-permute-done((bf16[4,16,1024]{2,1,0:T(8,128)(2,1)S(1)}, bf16[4,16,1024]{2,1,0:T(8,128)(2,1)S(1)}, u32[]{:S(2)}, u32[]{:S(2)}) %collective-permute-start.16) | collective-permute-done | bytes 131104 | tf_op jit(solution)/shard_map/ppermute | solution.py:283
  73.6 0.9 %collective-permute-start.17 = (bf16[4,16,1024]{2,1,0:T(8,128)(2,1)S(1)}, bf16[4,16,1024]{2,1,0:T(8,128)(2,1)S(1)}, u32[]{:S(2)}, u32[]{:S(2)}) collective-permute-start(bf16[4,16,1024]{2,1,0:T(8,128)(2,1)S(1)} %add_convert_fusion.8), channel_id=1, source_target_pairs={{0,4},{4,8},{8,12},{12,14},{14,10},{10,6},{6,2},{2,0},{1,5},{5,9},... | collective-permute-start | bytes 393224 | tf_op jit(solution)/shard_map/ppermute | solution.py:283
  74.5 1.4 %collective-permute-done.20 = bf16[4,16,1024]{2,1,0:T(8,128)(2,1)S(1)} collective-permute-done((bf16[4,16,1024]{2,1,0:T(8,128)(2,1)S(1)}, bf16[4,16,1024]{2,1,0:T(8,128)(2,1)S(1)}, u32[]{:S(2)}, u32[]{:S(2)}) %collective-permute-start.20) | collective-permute-done | bytes 131104 | tf_op jit(solution)/shard_map/ppermute | solution.py:288
  76.0 0.1 collective-permute-start.21
  76.1 2.0 %collective-permute-start.26 = (bf16[4,16,1024]{2,1,0:T(8,128)(2,1)S(1)}, bf16[4,16,1024]{2,1,0:T(8,128)(2,1)S(1)}, u32[]{:S(2)}, u32[]{:S(2)}) collective-permute-start(bf16[4,16,1024]{2,1,0:T(8,128)(2,1)S(1)} %add_convert_fusion.2), channel_id=1, source_target_pairs={{0,4},{4,8},{8,12},{12,14},{14,10},{10,6},{6,2},{2,0},{1,5},{5,9},... | collective-permute-start | bytes 393224 | tf_op jit(solution)/shard_map/ppermute | solution.py:283
  78.2 0.4 collective-permute-done.17.refs_4_
  78.6 2.4 %collective-permute-done.21.refs_5_ = bf16[4,16,1024]{2,1,0:T(8,128)(2,1)S(1)} collective-permute-done((bf16[4,16,1024]{2,1,0:T(8,128)(2,1)S(1)}, bf16[4,16,1024]{2,1,0:T(8,128)(2,1)S(1)}, u32[]{:S(2)}, u32[]{:S(2)}) %collective-permute-start.21) | collective-permute-done | bytes 131104 | tf_op jit(solution)/shard_map/ppermute | solution.py:288
  81.0 0.9 %fusion = bf16[16,1024]{1,0:T(8,128)(2,1)S(1)} fusion(f32[4,16,1024]{2,1,0:T(8,128)} %get-tuple-element.21.refs_3_, s32[]{:T(128)S(6)} %select_n.7, bf16[4,16,1024]{2,1,0:T(8,128)(2,1)S(1)} %collective-permute-done.21.refs_5_, bf16[4,16,1024]{2,1,0:T(8,128)(2,1)S(1)} %collective-permute-done.17.refs_4_), kind=kLoop, calls=%fused_computation.11 | loop fusion | flops 81920 | bytes 163844 | tf_op jit(solution)/shard_map/convert_element_type | solution.py:298
  82.0 0.6 add_reduce_fusion
  82.6 0.5 collective-permute-done.22.edge_ref
  83.3 0.5 copy-done.11
  83.8 2.3 %parents.1 = bf16[16,8,1024]{2,1,0:T(8,128)(2,1)} custom-call(s32[16]{0:T(128)} %parents_ref.5, s32[8]{0:T(128)} %counts_ref.1, bf16[16,1024]{1,0:T(8,128)(2,1)} %copy-done.11, f32[4,16,1024]{2,1,0:T(8,128)} %get-tuple-element.29.refs_0_, bf16[4,16,1024]{2,1,0:T(8,128)(2,1)} %copy-done.10, bf16[4,16,1024]{2,1,0:T(8,128)(2,1)} %copy-done.6, ...), custom_call_target="tpu_custom_call" | custom-call | flops 786432 | bytes 1310720 | tf_op jit(solution)/shard_map/parents/pallas_call | solution.py:225
  (73 shorter events, 0.6 us)
Async XLA Ops:
  2.5 6.7 %collective-permute-start.11 = (bf16[4,16,1024]{2,1,0:T(8,128)(2,1)}, bf16[4,16,1024]{2,1,0:T(8,128)(2,1)S(1)}, u32[]{:S(2)}, u32[]{:S(2)}) collective-permute-start(bf16[4,16,1024]{2,1,0:T(8,128)(2,1)} %children0.1.refs_1_), channel_id=1, source_target_pairs={{0,4},{4,8},{8,12},{12,14},{14,10},{10,6},{6,2},{2,0},{1,5},{5,9},... | collective-permute-start | bytes 393224 | tf_op jit(solution)/shard_map/ppermute | solution.py:268
  5.6 10.4 %collective-permute-start = (bf16[16,8,1024]{2,1,0:T(8,128)(2,1)}, bf16[16,8,1024]{2,1,0:T(8,128)(2,1)S(1)}, u32[]{:S(2)}, u32[]{:S(2)}) collective-permute-start(bf16[16,8,1024]{2,1,0:T(8,128)(2,1)} %green_ref.3), channel_id=1, source_target_pairs={{0,1},{1,0},{2,3},{3,2},{4,5},{5,4},{6,7},{7,6},{8,9},{9,8},{10,11... | collective-permute-start | bytes 786440 | tf_op jit(solution)/shard_map/ppermute | solution.py:244
  5.6 6.1 %collective-permute-start.8 = (bf16[4,16,1024]{2,1,0:T(8,128)(2,1)}, bf16[4,16,1024]{2,1,0:T(8,128)(2,1)S(1)}, u32[]{:S(2)}, u32[]{:S(2)}) collective-permute-start(bf16[4,16,1024]{2,1,0:T(8,128)(2,1)} %children0.1.refs_1_), channel_id=1, source_target_pairs={{0,2},{4,0},{8,4},{12,8},{14,12},{10,14},{6,10},{2,6},{1,3},{5,1},... | collective-permute-start | bytes 393224 | tf_op jit(solution)/shard_map/ppermute | solution.py:270
  9.2 19.1 %copy-start.16 = (bf16[4,16,1024]{2,1,0:T(8,128)(2,1)}, bf16[4,16,1024]{2,1,0:T(8,128)(2,1)S(1)}, u32[]{:S(2)}) copy-start(bf16[4,16,1024]{2,1,0:T(8,128)(2,1)S(1)} %collective-permute-done.11.refs_8_) | copy-start | bytes 393220
  9.2 5.0 %collective-permute-start.12 = (bf16[4,16,1024]{2,1,0:T(8,128)(2,1)S(1)}, bf16[4,16,1024]{2,1,0:T(8,128)(2,1)S(1)}, u32[]{:S(2)}, u32[]{:S(2)}) collective-permute-start(bf16[4,16,1024]{2,1,0:T(8,128)(2,1)S(1)} %collective-permute-done.11.refs_8_), channel_id=1, source_target_pairs={{0,4},{4,8},{8,12},{12,14},{14,10},{10,6},{6,2},{2,0},{1,5},{5,9},... | collective-permute-start | bytes 393224 | tf_op jit(solution)/shard_map/ppermute | solution.py:268
  11.7 16.6 %copy-start.17 = (bf16[4,16,1024]{2,1,0:T(8,128)(2,1)}, bf16[4,16,1024]{2,1,0:T(8,128)(2,1)S(1)}, u32[]{:S(2)}) copy-start(bf16[4,16,1024]{2,1,0:T(8,128)(2,1)S(1)} %collective-permute-done.8.refs_2_) | copy-start | bytes 393220
  11.7 9.1 %collective-permute-start.9 = (bf16[4,16,1024]{2,1,0:T(8,128)(2,1)S(1)}, bf16[4,16,1024]{2,1,0:T(8,128)(2,1)S(1)}, u32[]{:S(2)}, u32[]{:S(2)}) collective-permute-start(bf16[4,16,1024]{2,1,0:T(8,128)(2,1)S(1)} %collective-permute-done.8.refs_2_), channel_id=1, source_target_pairs={{0,2},{4,0},{8,4},{12,8},{14,12},{10,14},{6,10},{2,6},{1,3},{5,1},... | collective-permute-start | bytes 393224 | tf_op jit(solution)/shard_map/ppermute | solution.py:270
  14.2 14.2 %copy-start.18 = (bf16[4,16,1024]{2,1,0:T(8,128)(2,1)}, bf16[4,16,1024]{2,1,0:T(8,128)(2,1)S(1)}, u32[]{:S(2)}) copy-start(bf16[4,16,1024]{2,1,0:T(8,128)(2,1)S(1)} %collective-permute-done.12.refs_7_) | copy-start | bytes 393220
  14.2 6.8 %collective-permute-start.13 = (bf16[4,16,1024]{2,1,0:T(8,128)(2,1)S(1)}, bf16[4,16,1024]{2,1,0:T(8,128)(2,1)S(1)}, u32[]{:S(2)}, u32[]{:S(2)}) collective-permute-start(bf16[4,16,1024]{2,1,0:T(8,128)(2,1)S(1)} %collective-permute-done.12.refs_7_), channel_id=1, source_target_pairs={{0,4},{4,8},{8,12},{12,14},{14,10},{10,6},{6,2},{2,0},{1,5},{5,9},... | collective-permute-start | bytes 393224 | tf_op jit(solution)/shard_map/ppermute | solution.py:268
  16.0 0.7 copy-start
  18.7 5.9 %collective-permute-start.5 = (bf16[4,16,1024]{2,1,0:T(8,128)(2,1)}, bf16[4,16,1024]{2,1,0:T(8,128)(2,1)S(1)}, u32[]{:S(2)}, u32[]{:S(2)}) collective-permute-start(bf16[4,16,1024]{2,1,0:T(8,128)(2,1)} %children1.1.refs_1_), channel_id=1, source_target_pairs={{0,4},{4,8},{8,12},{12,14},{14,10},{10,6},{6,2},{2,0},{1,5},{5,9},... | collective-permute-start | bytes 393224 | tf_op jit(solution)/shard_map/ppermute | solution.py:268
  20.3 6.2 %collective-permute-start.1 = (bf16[4,16,1024]{2,1,0:T(8,128)(2,1)}, bf16[4,16,1024]{2,1,0:T(8,128)(2,1)S(1)}, u32[]{:S(2)}, u32[]{:S(2)}) collective-permute-start(bf16[4,16,1024]{2,1,0:T(8,128)(2,1)} %children1.1.refs_1_), channel_id=1, source_target_pairs={{0,2},{4,0},{8,4},{12,8},{14,12},{10,14},{6,10},{2,6},{1,3},{5,1},... | collective-permute-start | bytes 393224 | tf_op jit(solution)/shard_map/ppermute | solution.py:270
  20.8 7.6 %copy-start.19 = (bf16[4,16,1024]{2,1,0:T(8,128)(2,1)}, bf16[4,16,1024]{2,1,0:T(8,128)(2,1)S(1)}, u32[]{:S(2)}) copy-start(bf16[4,16,1024]{2,1,0:T(8,128)(2,1)S(1)} %collective-permute-done.9.refs_3_) | copy-start | bytes 393220
  20.8 7.5 %collective-permute-start.10 = (bf16[4,16,1024]{2,1,0:T(8,128)(2,1)S(1)}, bf16[4,16,1024]{2,1,0:T(8,128)(2,1)S(1)}, u32[]{:S(2)}, u32[]{:S(2)}) collective-permute-start(bf16[4,16,1024]{2,1,0:T(8,128)(2,1)S(1)} %collective-permute-done.9.refs_3_), channel_id=1, source_target_pairs={{0,2},{4,0},{8,4},{12,8},{14,12},{10,14},{6,10},{2,6},{1,3},{5,1},... | collective-permute-start | bytes 393224 | tf_op jit(solution)/shard_map/ppermute | solution.py:270
  21.0 7.4 %copy-start.20 = (bf16[4,16,1024]{2,1,0:T(8,128)(2,1)}, bf16[4,16,1024]{2,1,0:T(8,128)(2,1)S(1)}, u32[]{:S(2)}) copy-start(bf16[4,16,1024]{2,1,0:T(8,128)(2,1)S(1)} %collective-permute-done.13.refs_6_) | copy-start | bytes 393220
  21.0 7.3 %collective-permute-start.14 = (bf16[4,16,1024]{2,1,0:T(8,128)(2,1)S(1)}, bf16[4,16,1024]{2,1,0:T(8,128)(2,1)S(1)}, u32[]{:S(2)}, u32[]{:S(2)}) collective-permute-start(bf16[4,16,1024]{2,1,0:T(8,128)(2,1)S(1)} %collective-permute-done.13.refs_6_), channel_id=1, source_target_pairs={{0,4},{4,8},{8,12},{12,14},{14,10},{10,6},{6,2},{2,0},{1,5},{5,9},... | collective-permute-start | bytes 393224 | tf_op jit(solution)/shard_map/ppermute | solution.py:268
  24.7 9.8 %copy-start.12 = (bf16[4,16,1024]{2,1,0:T(8,128)(2,1)}, bf16[4,16,1024]{2,1,0:T(8,128)(2,1)S(1)}, u32[]{:S(2)}) copy-start(bf16[4,16,1024]{2,1,0:T(8,128)(2,1)S(1)} %collective-permute-done.5.refs_8_) | copy-start | bytes 393220
  24.7 11.8 %collective-permute-start.6 = (bf16[4,16,1024]{2,1,0:T(8,128)(2,1)S(1)}, bf16[4,16,1024]{2,1,0:T(8,128)(2,1)S(1)}, u32[]{:S(2)}, u32[]{:S(2)}) collective-permute-start(bf16[4,16,1024]{2,1,0:T(8,128)(2,1)S(1)} %collective-permute-done.5.refs_8_), channel_id=1, source_target_pairs={{0,4},{4,8},{8,12},{12,14},{14,10},{10,6},{6,2},{2,0},{1,5},{5,9},... | collective-permute-start | bytes 393224 | tf_op jit(solution)/shard_map/ppermute | solution.py:268
  26.5 8.0 %copy-start.13 = (bf16[4,16,1024]{2,1,0:T(8,128)(2,1)}, bf16[4,16,1024]{2,1,0:T(8,128)(2,1)S(1)}, u32[]{:S(2)}) copy-start(bf16[4,16,1024]{2,1,0:T(8,128)(2,1)S(1)} %collective-permute-done.1.refs_2_) | copy-start | bytes 393220
  26.5 11.6 %collective-permute-start.2 = (bf16[4,16,1024]{2,1,0:T(8,128)(2,1)S(1)}, bf16[4,16,1024]{2,1,0:T(8,128)(2,1)S(1)}, u32[]{:S(2)}, u32[]{:S(2)}) collective-permute-start(bf16[4,16,1024]{2,1,0:T(8,128)(2,1)S(1)} %collective-permute-done.1.refs_2_), channel_id=1, source_target_pairs={{0,2},{4,0},{8,4},{12,8},{14,12},{10,14},{6,10},{2,6},{1,3},{5,1},... | collective-permute-start | bytes 393224 | tf_op jit(solution)/shard_map/ppermute | solution.py:270
  28.3 0.6 copy-start.23
  28.9 0.7 copy-start.24
  34.4 5.5 %collective-permute-start.23 = (bf16[4,16,1024]{2,1,0:T(8,128)(2,1)}, bf16[4,16,1024]{2,1,0:T(8,128)(2,1)S(1)}, u32[]{:S(2)}, u32[]{:S(2)}) collective-permute-start(bf16[4,16,1024]{2,1,0:T(8,128)(2,1)} %get-tuple-element.33), channel_id=1, source_target_pairs={{0,4},{4,8},{8,12},{12,14},{14,10},{10,6},{6,2},{2,0},{1,5},{5,9},... | collective-permute-start | bytes 393224 | tf_op jit(solution)/shard_map/ppermute | solution.py:283
  36.1 8.8 %collective-permute-start.27 = (bf16[4,16,1024]{2,1,0:T(8,128)(2,1)}, bf16[4,16,1024]{2,1,0:T(8,128)(2,1)S(1)}, u32[]{:S(2)}, u32[]{:S(2)}) collective-permute-start(bf16[4,16,1024]{2,1,0:T(8,128)(2,1)} %get-tuple-element.36), channel_id=1, source_target_pairs={{0,2},{4,0},{8,4},{12,8},{14,12},{10,14},{6,10},{2,6},{1,3},{5,1},... | collective-permute-start | bytes 393224 | tf_op jit(solution)/shard_map/ppermute | solution.py:288
  36.5 12.9 %copy-start.14 = (bf16[4,16,1024]{2,1,0:T(8,128)(2,1)}, bf16[4,16,1024]{2,1,0:T(8,128)(2,1)S(1)}, u32[]{:S(2)}) copy-start(bf16[4,16,1024]{2,1,0:T(8,128)(2,1)S(1)} %collective-permute-done.6.refs_7_) | copy-start | bytes 393220
  36.5 10.2 %collective-permute-start.7 = (bf16[4,16,1024]{2,1,0:T(8,128)(2,1)S(1)}, bf16[4,16,1024]{2,1,0:T(8,128)(2,1)S(1)}, u32[]{:S(2)}, u32[]{:S(2)}) collective-permute-start(bf16[4,16,1024]{2,1,0:T(8,128)(2,1)S(1)} %collective-permute-done.6.refs_7_), channel_id=1, source_target_pairs={{0,4},{4,8},{8,12},{12,14},{14,10},{10,6},{6,2},{2,0},{1,5},{5,9},... | collective-permute-start | bytes 393224 | tf_op jit(solution)/shard_map/ppermute | solution.py:268
  38.1 11.3 %copy-start.15 = (bf16[4,16,1024]{2,1,0:T(8,128)(2,1)}, bf16[4,16,1024]{2,1,0:T(8,128)(2,1)S(1)}, u32[]{:S(2)}) copy-start(bf16[4,16,1024]{2,1,0:T(8,128)(2,1)S(1)} %collective-permute-done.2.refs_3_) | copy-start | bytes 393220
  38.1 6.3 %collective-permute-start.3 = (bf16[4,16,1024]{2,1,0:T(8,128)(2,1)S(1)}, bf16[4,16,1024]{2,1,0:T(8,128)(2,1)S(1)}, u32[]{:S(2)}, u32[]{:S(2)}) collective-permute-start(bf16[4,16,1024]{2,1,0:T(8,128)(2,1)S(1)} %collective-permute-done.2.refs_3_), channel_id=1, source_target_pairs={{0,2},{4,0},{8,4},{12,8},{14,12},{10,14},{6,10},{2,6},{1,3},{5,1},... | collective-permute-start | bytes 393224 | tf_op jit(solution)/shard_map/ppermute | solution.py:270
  40.9 14.6 %collective-permute-start.24 = (bf16[4,16,1024]{2,1,0:T(8,128)(2,1)S(1)}, bf16[4,16,1024]{2,1,0:T(8,128)(2,1)S(1)}, u32[]{:S(2)}, u32[]{:S(2)}) collective-permute-start(bf16[4,16,1024]{2,1,0:T(8,128)(2,1)S(1)} %add_convert_fusion.4), channel_id=1, source_target_pairs={{0,4},{4,8},{8,12},{12,14},{14,10},{10,6},{6,2},{2,0},{1,5},{5,9},... | collective-permute-start | bytes 393224 | tf_op jit(solution)/shard_map/ppermute | solution.py:283
  44.4 5.0 %copy-start.22 = (bf16[4,16,1024]{2,1,0:T(8,128)(2,1)}, bf16[4,16,1024]{2,1,0:T(8,128)(2,1)S(1)}, u32[]{:S(2)}) copy-start(bf16[4,16,1024]{2,1,0:T(8,128)(2,1)S(1)} %collective-permute-done.3.refs_4_) | copy-start | bytes 393220
  44.5 5.0 %collective-permute-start.4 = (bf16[4,16,1024]{2,1,0:T(8,128)(2,1)S(1)}, bf16[4,16,1024]{2,1,0:T(8,128)(2,1)S(1)}, u32[]{:S(2)}, u32[]{:S(2)}) collective-permute-start(bf16[4,16,1024]{2,1,0:T(8,128)(2,1)S(1)} %collective-permute-done.3.refs_4_), channel_id=1, source_target_pairs={{0,2},{4,0},{8,4},{12,8},{14,12},{10,14},{6,10},{2,6},{1,3},{5,1},... | collective-permute-start | bytes 393224 | tf_op jit(solution)/shard_map/ppermute | solution.py:270
  45.8 15.1 %collective-permute-start.28 = (bf16[4,16,1024]{2,1,0:T(8,128)(2,1)S(1)}, bf16[4,16,1024]{2,1,0:T(8,128)(2,1)S(1)}, u32[]{:S(2)}, u32[]{:S(2)}) collective-permute-start(bf16[4,16,1024]{2,1,0:T(8,128)(2,1)S(1)} %add_convert_fusion.1), channel_id=1, source_target_pairs={{0,2},{4,0},{8,4},{12,8},{14,12},{10,14},{6,10},{2,6},{1,3},{5,1},... | collective-permute-start | bytes 393224 | tf_op jit(solution)/shard_map/ppermute | solution.py:288
  46.8 2.7 %copy-start.21 = (bf16[4,16,1024]{2,1,0:T(8,128)(2,1)}, bf16[4,16,1024]{2,1,0:T(8,128)(2,1)S(1)}, u32[]{:S(2)}) copy-start(bf16[4,16,1024]{2,1,0:T(8,128)(2,1)S(1)} %collective-permute-done.7.refs_6_) | copy-start | bytes 393220
  49.4 0.7 copy-start.25
  50.1 5.4 %copy-start.5 = (bf16[4,16,1024]{2,1,0:T(8,128)(2,1)S(1)}, bf16[4,16,1024]{2,1,0:T(8,128)(2,1)}, u32[]{:S(2)}) copy-start(bf16[4,16,1024]{2,1,0:T(8,128)(2,1)} %get-tuple-element.31) | copy-start | bytes 393220
  50.1 10.9 %copy-start.4 = (bf16[4,16,1024]{2,1,0:T(8,128)(2,1)S(1)}, bf16[4,16,1024]{2,1,0:T(8,128)(2,1)}, u32[]{:S(2)}) copy-start(bf16[4,16,1024]{2,1,0:T(8,128)(2,1)} %get-tuple-element.34) | copy-start | bytes 393220
  54.9 16.0 %copy-start.9 = (bf16[4,16,1024]{2,1,0:T(8,128)(2,1)S(1)}, bf16[4,16,1024]{2,1,0:T(8,128)(2,1)}, u32[]{:S(2)}) copy-start(bf16[4,16,1024]{2,1,0:T(8,128)(2,1)} %get-tuple-element.26) | copy-start | bytes 393220
  54.9 18.6 %copy-start.8 = (bf16[4,16,1024]{2,1,0:T(8,128)(2,1)S(1)}, bf16[4,16,1024]{2,1,0:T(8,128)(2,1)}, u32[]{:S(2)}) copy-start(bf16[4,16,1024]{2,1,0:T(8,128)(2,1)} %get-tuple-element.22) | copy-start | bytes 393220
  54.9 21.0 %copy-start.7 = (bf16[4,16,1024]{2,1,0:T(8,128)(2,1)S(1)}, bf16[4,16,1024]{2,1,0:T(8,128)(2,1)}, u32[]{:S(2)}) copy-start(bf16[4,16,1024]{2,1,0:T(8,128)(2,1)} %get-tuple-element.25) | copy-start | bytes 393220
  54.9 21.2 %copy-start.3 = (bf16[4,16,1024]{2,1,0:T(8,128)(2,1)S(1)}, bf16[4,16,1024]{2,1,0:T(8,128)(2,1)}, u32[]{:S(2)}) copy-start(bf16[4,16,1024]{2,1,0:T(8,128)(2,1)} %get-tuple-element.30) | copy-start | bytes 393220
  54.9 3.9 %collective-permute-start.30 = (f32[8,128]{1,0:T(8,128)}, f32[8,128]{1,0:T(8,128)S(1)}, u32[]{:S(2)}, u32[]{:S(2)}) collective-permute-start(f32[8,128]{1,0:T(8,128)} %get-tuple-element.37), channel_id=1, source_target_pairs={{0,2},{2,0},{4,6},{6,4},{8,10},{10,8},{12,14},{14,12},{1,3},{3,1},... | collective-permute-start | bytes 12296 | tf_op jit(solution)/shard_map/ppermute | solution.py:292
  55.5 20.6 %collective-permute-start.25 = (bf16[4,16,1024]{2,1,0:T(8,128)(2,1)S(1)}, bf16[4,16,1024]{2,1,0:T(8,128)(2,1)S(1)}, u32[]{:S(2)}, u32[]{:S(2)}) collective-permute-start(bf16[4,16,1024]{2,1,0:T(8,128)(2,1)S(1)} %add_convert_fusion.3), channel_id=1, source_target_pairs={{0,4},{4,8},{8,12},{12,14},{14,10},{10,6},{6,2},{2,0},{1,5},{5,9},... | collective-permute-start | bytes 393224 | tf_op jit(solution)/shard_map/ppermute | solution.py:283
  56.6 8.0 %collective-permute-start.18 = (bf16[4,16,1024]{2,1,0:T(8,128)(2,1)}, bf16[4,16,1024]{2,1,0:T(8,128)(2,1)S(1)}, u32[]{:S(2)}, u32[]{:S(2)}) collective-permute-start(bf16[4,16,1024]{2,1,0:T(8,128)(2,1)} %get-tuple-element.28), channel_id=1, source_target_pairs={{0,2},{4,0},{8,4},{12,8},{14,12},{10,14},{6,10},{2,6},{1,3},{5,1},... | collective-permute-start | bytes 393224 | tf_op jit(solution)/shard_map/ppermute | solution.py:288
  59.5 3.6 %collective-permute-start.31 = (f32[8,128]{1,0:T(8,128)S(1)}, f32[8,128]{1,0:T(8,128)S(1)}, u32[]{:S(2)}, u32[]{:S(2)}) collective-permute-start(f32[8,128]{1,0:T(8,128)S(1)} %add.67), channel_id=1, source_target_pairs={{0,4},{2,6},{4,0},{6,2},{8,12},{10,14},{12,8},{14,10},{1,5},{3,7},... | collective-permute-start | bytes 12296 | tf_op jit(solution)/shard_map/ppermute | solution.py:292
  61.0 21.6 %collective-permute-start.29 = (bf16[4,16,1024]{2,1,0:T(8,128)(2,1)S(1)}, bf16[4,16,1024]{2,1,0:T(8,128)(2,1)S(1)}, u32[]{:S(2)}, u32[]{:S(2)}) collective-permute-start(bf16[4,16,1024]{2,1,0:T(8,128)(2,1)S(1)} %add_convert_fusion), channel_id=1, source_target_pairs={{0,2},{4,0},{8,4},{12,8},{14,12},{10,14},{6,10},{2,6},{1,3},{5,1},... | collective-permute-start | bytes 393224 | tf_op jit(solution)/shard_map/ppermute | solution.py:288
  61.4 6.2 %collective-permute-start.15 = (bf16[4,16,1024]{2,1,0:T(8,128)(2,1)}, bf16[4,16,1024]{2,1,0:T(8,128)(2,1)S(1)}, u32[]{:S(2)}, u32[]{:S(2)}) collective-permute-start(bf16[4,16,1024]{2,1,0:T(8,128)(2,1)} %get-tuple-element.24), channel_id=1, source_target_pairs={{0,4},{4,8},{8,12},{12,14},{14,10},{10,6},{6,2},{2,0},{1,5},{5,9},... | collective-permute-start | bytes 393224 | tf_op jit(solution)/shard_map/ppermute | solution.py:283
  63.1 18.9 %collective-permute-start.32 = (f32[8,128]{1,0:T(8,128)S(1)}, f32[8,128]{1,0:T(8,128)S(1)}, u32[]{:S(2)}, u32[]{:S(2)}) collective-permute-start(f32[8,128]{1,0:T(8,128)S(1)} %add.68), channel_id=1, source_target_pairs={{0,8},{2,10},{4,12},{6,14},{8,0},{10,2},{12,4},{14,6},{1,9},{3,11}... | collective-permute-start | bytes 12296 | tf_op jit(solution)/shard_map/ppermute | solution.py:292
  65.6 5.3 %collective-permute-start.19 = (bf16[4,16,1024]{2,1,0:T(8,128)(2,1)S(1)}, bf16[4,16,1024]{2,1,0:T(8,128)(2,1)S(1)}, u32[]{:S(2)}, u32[]{:S(2)}) collective-permute-start(bf16[4,16,1024]{2,1,0:T(8,128)(2,1)S(1)} %add_convert_fusion.7), channel_id=1, source_target_pairs={{0,2},{4,0},{8,4},{12,8},{14,12},{10,14},{6,10},{2,6},{1,3},{5,1},... | collective-permute-start | bytes 393224 | tf_op jit(solution)/shard_map/ppermute | solution.py:288
  68.5 5.0 %collective-permute-start.16 = (bf16[4,16,1024]{2,1,0:T(8,128)(2,1)S(1)}, bf16[4,16,1024]{2,1,0:T(8,128)(2,1)S(1)}, u32[]{:S(2)}, u32[]{:S(2)}) collective-permute-start(bf16[4,16,1024]{2,1,0:T(8,128)(2,1)S(1)} %add_convert_fusion.9), channel_id=1, source_target_pairs={{0,4},{4,8},{8,12},{12,14},{14,10},{10,6},{6,2},{2,0},{1,5},{5,9},... | collective-permute-start | bytes 393224 | tf_op jit(solution)/shard_map/ppermute | solution.py:283
  70.9 5.0 %collective-permute-start.20 = (bf16[4,16,1024]{2,1,0:T(8,128)(2,1)S(1)}, bf16[4,16,1024]{2,1,0:T(8,128)(2,1)S(1)}, u32[]{:S(2)}, u32[]{:S(2)}) collective-permute-start(bf16[4,16,1024]{2,1,0:T(8,128)(2,1)S(1)} %add_convert_fusion.6), channel_id=1, source_target_pairs={{0,2},{4,0},{8,4},{12,8},{14,12},{10,14},{6,10},{2,6},{1,3},{5,1},... | collective-permute-start | bytes 393224 | tf_op jit(solution)/shard_map/ppermute | solution.py:288
  73.6 5.0 %collective-permute-start.17 = (bf16[4,16,1024]{2,1,0:T(8,128)(2,1)S(1)}, bf16[4,16,1024]{2,1,0:T(8,128)(2,1)S(1)}, u32[]{:S(2)}, u32[]{:S(2)}) collective-permute-start(bf16[4,16,1024]{2,1,0:T(8,128)(2,1)S(1)} %add_convert_fusion.8), channel_id=1, source_target_pairs={{0,4},{4,8},{8,12},{12,14},{14,10},{10,6},{6,2},{2,0},{1,5},{5,9},... | collective-permute-start | bytes 393224 | tf_op jit(solution)/shard_map/ppermute | solution.py:283
  76.0 5.0 %collective-permute-start.21 = (bf16[4,16,1024]{2,1,0:T(8,128)(2,1)S(1)}, bf16[4,16,1024]{2,1,0:T(8,128)(2,1)S(1)}, u32[]{:S(2)}, u32[]{:S(2)}) collective-permute-start(bf16[4,16,1024]{2,1,0:T(8,128)(2,1)S(1)} %add_convert_fusion.5), channel_id=1, source_target_pairs={{0,2},{4,0},{8,4},{12,8},{14,12},{10,14},{6,10},{2,6},{1,3},{5,1},... | collective-permute-start | bytes 393224 | tf_op jit(solution)/shard_map/ppermute | solution.py:288
  76.1 6.5 %collective-permute-start.26 = (bf16[4,16,1024]{2,1,0:T(8,128)(2,1)S(1)}, bf16[4,16,1024]{2,1,0:T(8,128)(2,1)S(1)}, u32[]{:S(2)}, u32[]{:S(2)}) collective-permute-start(bf16[4,16,1024]{2,1,0:T(8,128)(2,1)S(1)} %add_convert_fusion.2), channel_id=1, source_target_pairs={{0,4},{4,8},{8,12},{12,14},{14,10},{10,6},{6,2},{2,0},{1,5},{5,9},... | collective-permute-start | bytes 393224 | tf_op jit(solution)/shard_map/ppermute | solution.py:283
  78.6 4.6 %copy-start.1 = (bf16[4,16,1024]{2,1,0:T(8,128)(2,1)}, bf16[4,16,1024]{2,1,0:T(8,128)(2,1)S(1)}, u32[]{:S(2)}) copy-start(bf16[4,16,1024]{2,1,0:T(8,128)(2,1)S(1)} %collective-permute-done.17.refs_4_) | copy-start | bytes 393220
  81.0 2.2 %copy-start.2 = (bf16[4,16,1024]{2,1,0:T(8,128)(2,1)}, bf16[4,16,1024]{2,1,0:T(8,128)(2,1)S(1)}, u32[]{:S(2)}) copy-start(bf16[4,16,1024]{2,1,0:T(8,128)(2,1)S(1)} %collective-permute-done.21.refs_5_) | copy-start | bytes 393220
  81.9 1.3 %collective-permute-start.22 = (bf16[16,1024]{1,0:T(8,128)(2,1)S(1)}, bf16[16,1024]{1,0:T(8,128)(2,1)S(1)}, u32[]{:S(2)}, u32[]{:S(2)}) collective-permute-start(bf16[16,1024]{1,0:T(8,128)(2,1)S(1)} %fusion), channel_id=1, source_target_pairs={{0,1},{1,0},{2,3},{3,2},{4,5},{5,4},{6,7},{7,6},{8,9},{9,8},{10,11... | collective-permute-start | bytes 98312 | tf_op jit(solution)/shard_map/ppermute | solution.py:244
  82.6 0.7 copy-start.6
  82.6 0.7 copy-start.10
  83.2 0.6 copy-start.11

commit v2 on v1

--- a/solution.py
+++ b/solution.py
@@ -6,6 +6,7 @@
 from jax.experimental import pallas as pl
 from jax.experimental.pallas import tpu as pltpu
 from jax.sharding import PartitionSpec as P
+
 
 F32 = jnp.float32
 BF16 = jnp.bfloat16
@@ -109,7 +110,7 @@
         cost_estimate=pl.CostEstimate(
             flops=green.size, bytes_accessed=6 * green.size, transcendentals=0
         ),
-        name=f"children{group}",
+        compiler_params=pltpu.CompilerParams(vmem_limit_bytes=6 << 20),
     )(*operands)
 
 
@@ -185,7 +186,7 @@
             bytes_accessed=2 * chol.size + 4 * size * orbitals * width,
             transcendentals=0,
         ),
-        name=f"forces{group}",
+        compiler_params=pltpu.CompilerParams(vmem_limit_bytes=16 << 20),
     )(chol, *chunks, *extra)
 
 
@@ -236,6 +237,7 @@
             bytes_accessed=10 * rows * walkers * width,
             transcendentals=0,
         ),
+        compiler_params=pltpu.CompilerParams(vmem_limit_bytes=6 << 20),
         name="parents",
     )(parents, counts, edge, *group_a, *group_b)
 
@@ -248,13 +250,27 @@
     return (own.astype(F32) + received.astype(F32)).astype(BF16)
 
 
+def hop_order(n):
+    longer = (("up", "down"), ("down", "up"))
+    order = []
+    for phase in ("gather", "sum"):
+        for s in range(1, n // 2 + 1):
+            for g in (0, 1):
+                for way in ("up", "down"):
+                    if s < n // 2 or way == longer[g][0]:
+                        order.append((phase, s, g, way))
+    return order
+
+
 def ring_shards(green_half, step_delta, chol_vectors, copy_counts, parents):
     n = lax.axis_size("chol")
-    rows, walkers, width = green_half.shape
+    _, walkers, _ = green_half.shape
     size = walkers // 2
-    up, down = ring_pairs(n, 1), ring_pairs(n, -1)
-    ups = (n // 2, n - 1 - n // 2)
-    downs = (n - 1 - n // 2, n // 2)
+    pairs = {"up": ring_pairs(n, 1), "down": ring_pairs(n, -1)}
+    hops = ({"up": n // 2, "down": n // 2 - 1}, {"up": n // 2 - 1, "down": n // 2})
+
+    def hop(x, key):
+        return lax.ppermute(x, "chol", pairs[key[3]])
 
     other = swap_cores(green_half)
     own = [
@@ -262,30 +278,22 @@
         make_children(1, size, parents, green_half, step_delta, other),
     ]
     chunks = [[own[g]] + [None] * (n - 1) for g in (0, 1)]
-    for s in range(1, n // 2 + 1):
-        for g in (0, 1):
-            if s <= ups[g]:
-                chunks[g][n - s] = lax.ppermute(chunks[g][(n - s + 1) % n], "chol", up)
-            if s <= downs[g]:
-                chunks[g][s] = lax.ppermute(chunks[g][s - 1], "chol", down)
-
-    *parts_a, energy = partial_forces(0, walkers, chol_vectors, chunks[0])
-    *parts_b, energy = partial_forces(1, walkers, chol_vectors, chunks[1], energy)
-    parts = (parts_a, parts_b)
-
-    rising, falling = [None, None], [None, None]
-    for s in range(1, n // 2 + 1):
-        for g in (0, 1):
-            if s <= ups[g]:
-                send = parts[g][ups[g] - s + 1]
-                if s > 1:
-                    send = add_low(send, rising[g])
-                rising[g] = lax.ppermute(send, "chol", up)
-            if s <= downs[g]:
-                send = parts[g][n - (downs[g] - s + 1)]
-                if s > 1:
-                    send = add_low(send, falling[g])
-                falling[g] = lax.ppermute(send, "chol", down)
+    parts = [None, None]
+    arrived = [{}, {}]
+    for key in hop_order(n):
+        phase, s, g, way = key
+        if phase == "gather":
+            here, there = (n - s, (n - s + 1) % n) if way == "up" else (s, s - 1)
+            chunks[g][here] = hop(chunks[g][there], key)
+            continue
+        if parts[g] is None:
+            extra = () if g == 0 else (energy,)
+            *parts[g], energy = partial_forces(g, walkers, chol_vectors, chunks[g], *extra)
+        left = hops[g][way] - s + 1
+        send = parts[g][left if way == "up" else n - left]
+        if s > 1:
+            send = add_low(send, arrived[g][way])
+        arrived[g][way] = hop(send, key)
 
     span = 1
     while span < n:
@@ -293,25 +301,23 @@
         span *= 2
 
     at = (size - 1) * (1 - lax.axis_index("pop"))
-    row = [lax.dynamic_index_in_dim(a, at, 0, keepdims=False).astype(F32)
-           for a in (parts[1][0], rising[1], falling[1])]
+    last = (parts[1][0], arrived[1]["up"], arrived[1]["down"])
+    row = [lax.dynamic_index_in_dim(a, at, 0, keepdims=False).astype(F32) for a in last]
     edge = swap_cores((row[0] + row[1] + row[2]).astype(BF16))
-    parent_force = parent_forces(
-        parents,
-        copy_counts,
-        edge,
-        (parts[0][0], rising[0], falling[0]),
-        (parts[1][0], rising[1], falling[1]),
-    )
+    first = (parts[0][0], arrived[0]["up"], arrived[0]["down"])
+    parent_force = parent_forces(parents, copy_counts, edge, first, last)
     return parent_force, jnp.sum(energy, axis=1)
+
+
+def on_ring(n, pops, rows, walkers):
+    return rows % 16 == 0 and walkers % 8 == 0 and n & (n - 1) == 0 and n >= 4 and pops == 2
 
 
 def shards(green_half, step_delta, chol_vectors, copy_counts, parents):
     rows, walkers, _ = green_half.shape
-    n = lax.axis_size("chol")
-    tiles = rows % 16 == 0 and walkers % 8 == 0 and n & (n - 1) == 0 and n >= 4
-    run = ring_shards if tiles and lax.axis_size("pop") == 2 else plain_shards
-    return run(green_half, step_delta, chol_vectors, copy_counts, parents)
+    if on_ring(lax.axis_size("chol"), lax.axis_size("pop"), rows, walkers):
+        return ring_shards(green_half, step_delta, chol_vectors, copy_counts, parents)
+    return plain_shards(green_half, step_delta, chol_vectors, copy_counts, parents)
 
 
 def solution(mesh):
@@ -322,10 +328,16 @@
         P(("rep", "pop")),
         P("rep"),
     )
-    return jax.shard_map(
+    step = jax.shard_map(
         shards,
         mesh=mesh,
         in_specs=placed,
         out_specs=(P(("rep", "chol"), "pop", None), P(("rep", "pop"))),
         check_vma=False,
     )
+
+    def run(green_half, step_delta, chol_vectors, copy_counts, parents):
+        given = (green_half, step_delta, chol_vectors, copy_counts, parents)
+        return step(*given)
+
+    return run

time: 86.5 us -> 74.1 us (0.86)
  Pallas kernels: 15.8 us -> 7.35 us
  other arithmetic: 6.17 us -> 1 us
  starting transfers between devices: 32.4 us -> 33.8 us
    pallas_call x2, Pallas kernels: 9.62 us -> 4.23 us  [partial_forces(): pl.pallas_call(functools.partial(force_kernel, group, walkers, -1.0 / tot...]
    convert_element_type x10, other arithmetic: 3.97 us -> 0.35 us  [add_low(): return (own.astype(F32) + received.astype(F32)).astype(BF16)]
    pallas_call x2, Pallas kernels: 3.92 us -> 1.53 us  [make_children(): pl.pallas_call(functools.partial(child_kernel, group, size), out_shape=ja...]
    ppermute x28, starting transfers between devices: 28.8 us -> 30.2 us  [hop(): return lax.ppermute(x, 'chol', pairs[key[3]])]
    convert_element_type x1, other arithmetic: 0.9 us -> 0.01 us  [ring_shards(): edge = swap_cores((row[0] + row[1] + row[2]).astype(BF16))]
    unnamed x52 -> x12, local copies, waits for them, and re-layouts: 3.28 us -> 2.56 us
  transfers between devices with their start and end apart: 33 -> 33, of which waited for: 17 -> 18; matrix products, arithmetic and copies ran while one was open for 7% -> 1% of each run, Pallas kernels for 14% -> 7%
where the time goes in v2:
time: 74.1 us; the launch traced here: 73.9 us
  starting transfers between devices  33.8 us (46%)
  waiting for transfers between devices  28.4 us (38%)
  Pallas kernels  7.35 us (10%)
  local copies, waits for them, and re-layouts  2.56 us (3%)
  other arithmetic  1 us (1%)
  between operations  0.77 us (1%)
    ppermute x28, starting transfers between devices, hop(): return lax.ppermute(x, 'chol', pairs[key[3]])  30.2 us
    ppermute x28, waiting for transfers between devices, hop(): return lax.ppermute(x, 'chol', pairs[key[3]])  26.5 us
    pallas_call x2, Pallas kernels, partial_forces(): pl.pallas_call(functools.partial(force_kernel, group, walkers, -1.0 / tot...  4.23 us
    ppermute x3, starting transfers between devices, ring_shards(): lax.ppermute(energy, 'chol', [(i, i ^ span) for i in range(n)])  3.51 us
    unnamed x12, local copies, waits for them, and re-layouts  2.56 us
    pallas_call x1, Pallas kernels, parent_forces(): pl.pallas_call(functools.partial(parent_kernel, size), out_shape=jax.Shap...  1.6 us
    pallas_call x2, Pallas kernels, make_children(): pl.pallas_call(functools.partial(child_kernel, group, size), out_shape=ja...  1.53 us
  transfers between devices with their start and end apart: 33, of which 18 were waited for; matrix products, arithmetic and copies ran while one was open for 1% of the time, Pallas kernels for 7%

profile of v2, /device:TPU:0, one launch (start us, length us, event | category | flops | bytes accessed | tf_op | source)
XLA Modules:
  0.0 73.9 jit_solution(3620209922857429927)
XLA Ops:
  0.6 0.9 %copy-done = bf16[16,8,1024]{2,1,0:T(8,128)(2,1)S(1)} copy-done((bf16[16,8,1024]{2,1,0:T(8,128)(2,1)S(1)}, bf16[16,8,1024]{2,1,0:T(8,128)(2,1)}, u32[]{:S(2)}) %copy-start) | copy-done | bytes 262168
  1.6 0.9 %copy-done.1 = bf16[16,8,1024]{2,1,0:T(8,128)(2,1)S(1)} copy-done((bf16[16,8,1024]{2,1,0:T(8,128)(2,1)S(1)}, bf16[16,8,1024]{2,1,0:T(8,128)(2,1)}, u32[]{:S(2)}) %copy-start.1) | copy-done | bytes 262168
  2.5 0.7 copy-done.2
  3.2 0.7 shard_map.69.refs_1_
  3.9 3.1 %collective-permute-start.11 = (bf16[4,16,1024]{2,1,0:T(8,128)(2,1)S(1)}, bf16[4,16,1024]{2,1,0:T(8,128)(2,1)S(1)}, u32[]{:S(2)}, u32[]{:S(2)}) collective-permute-start(bf16[4,16,1024]{2,1,0:T(8,128)(2,1)S(1)} %shard_map.69.refs_1_), channel_id=1, source_target_pairs={{0,4},{4,8},{8,12},{12,14},{14,10},{10,6},{6,2},{2,0},{1,5},{5,9},... | collective-permute-start | bytes 393224 | tf_op jit(solution)/shard_map/ppermute | solution.py:273
  7.0 0.1 collective-permute-start.8
  7.1 3.3 %collective-permute-done.11.refs_8_ = bf16[4,16,1024]{2,1,0:T(8,128)(2,1)S(1)} collective-permute-done((bf16[4,16,1024]{2,1,0:T(8,128)(2,1)S(1)}, bf16[4,16,1024]{2,1,0:T(8,128)(2,1)S(1)}, u32[]{:S(2)}, u32[]{:S(2)}) %collective-permute-start.11) | collective-permute-done | bytes 131104 | tf_op jit(solution)/shard_map/ppermute | solution.py:273
  10.4 1.8 %collective-permute-start.12 = (bf16[4,16,1024]{2,1,0:T(8,128)(2,1)S(1)}, bf16[4,16,1024]{2,1,0:T(8,128)(2,1)S(1)}, u32[]{:S(2)}, u32[]{:S(2)}) collective-permute-start(bf16[4,16,1024]{2,1,0:T(8,128)(2,1)S(1)} %collective-permute-done.11.refs_8_), channel_id=1, source_target_pairs={{0,4},{4,8},{8,12},{12,14},{14,10},{10,6},{6,2},{2,0},{1,5},{5,9},... | collective-permute-start | bytes 393224 | tf_op jit(solution)/shard_map/ppermute | solution.py:273
  12.3 0.7 collective-permute-done.8.refs_2_
  12.9 0.3 collective-permute-start.9
  13.2 2.2 %collective-permute-done.12.refs_7_ = bf16[4,16,1024]{2,1,0:T(8,128)(2,1)S(1)} collective-permute-done((bf16[4,16,1024]{2,1,0:T(8,128)(2,1)S(1)}, bf16[4,16,1024]{2,1,0:T(8,128)(2,1)S(1)}, u32[]{:S(2)}, u32[]{:S(2)}) %collective-permute-start.12) | collective-permute-done | bytes 131104 | tf_op jit(solution)/shard_map/ppermute | solution.py:273
  15.4 1.8 %collective-permute-start.13 = (bf16[4,16,1024]{2,1,0:T(8,128)(2,1)S(1)}, bf16[4,16,1024]{2,1,0:T(8,128)(2,1)S(1)}, u32[]{:S(2)}, u32[]{:S(2)}) collective-permute-start(bf16[4,16,1024]{2,1,0:T(8,128)(2,1)S(1)} %collective-permute-done.12.refs_7_), channel_id=1, source_target_pairs={{0,4},{4,8},{8,12},{12,14},{14,10},{10,6},{6,2},{2,0},{1,5},{5,9},... | collective-permute-start | bytes 393224 | tf_op jit(solution)/shard_map/ppermute | solution.py:273
  17.2 0.0 collective-permute-done.refs_0_
  17.2 0.8 %shard_map.68.refs_1_ = bf16[4,16,1024]{2,1,0:T(8,128)(2,1)S(1)} custom-call(s32[16]{0:T(128)S(1)} %copy-done.2, bf16[16,8,1024]{2,1,0:T(8,128)(2,1)S(1)} %copy-done, bf16[16,8,1024]{2,1,0:T(8,128)(2,1)S(1)} %copy-done.1, bf16[16,8,1024]{2,1,0:T(8,128)(2,1)S(1)} %collective-permute-done.refs_0_), custom_call_target="tpu_custom_call" | custom-call | flops 131072 | bytes 786432 | tf_op jit(solution)/shard_map/pallas_call | solution.py:104
  18.0 1.6 %collective-permute-start.5 = (bf16[4,16,1024]{2,1,0:T(8,128)(2,1)S(1)}, bf16[4,16,1024]{2,1,0:T(8,128)(2,1)S(1)}, u32[]{:S(2)}, u32[]{:S(2)}) collective-permute-start(bf16[4,16,1024]{2,1,0:T(8,128)(2,1)S(1)} %shard_map.68.refs_1_), channel_id=1, source_target_pairs={{0,4},{4,8},{8,12},{12,14},{14,10},{10,6},{6,2},{2,0},{1,5},{5,9},... | collective-permute-start | bytes 393224 | tf_op jit(solution)/shard_map/ppermute | solution.py:273
  19.7 0.4 collective-permute-start.1
  20.1 0.0 collective-permute-done.9.refs_3_
  20.1 0.2 collective-permute-start.10
  20.3 1.4 %collective-permute-done.13.refs_6_ = bf16[4,16,1024]{2,1,0:T(8,128)(2,1)S(1)} collective-permute-done((bf16[4,16,1024]{2,1,0:T(8,128)(2,1)S(1)}, bf16[4,16,1024]{2,1,0:T(8,128)(2,1)S(1)}, u32[]{:S(2)}, u32[]{:S(2)}) %collective-permute-start.13) | collective-permute-done | bytes 131104 | tf_op jit(solution)/shard_map/ppermute | solution.py:273
  21.8 1.7 %collective-permute-start.14 = (bf16[4,16,1024]{2,1,0:T(8,128)(2,1)S(1)}, bf16[4,16,1024]{2,1,0:T(8,128)(2,1)S(1)}, u32[]{:S(2)}, u32[]{:S(2)}) collective-permute-start(bf16[4,16,1024]{2,1,0:T(8,128)(2,1)S(1)} %collective-permute-done.13.refs_6_), channel_id=1, source_target_pairs={{0,4},{4,8},{8,12},{12,14},{14,10},{10,6},{6,2},{2,0},{1,5},{5,9},... | collective-permute-start | bytes 393224 | tf_op jit(solution)/shard_map/ppermute | solution.py:273
  23.5 1.1 %collective-permute-done.5.refs_8_ = bf16[4,16,1024]{2,1,0:T(8,128)(2,1)S(1)} collective-permute-done((bf16[4,16,1024]{2,1,0:T(8,128)(2,1)S(1)}, bf16[4,16,1024]{2,1,0:T(8,128)(2,1)S(1)}, u32[]{:S(2)}, u32[]{:S(2)}) %collective-permute-start.5) | collective-permute-done | bytes 131104 | tf_op jit(solution)/shard_map/ppermute | solution.py:273
  24.6 1.7 %collective-permute-start.6 = (bf16[4,16,1024]{2,1,0:T(8,128)(2,1)S(1)}, bf16[4,16,1024]{2,1,0:T(8,128)(2,1)S(1)}, u32[]{:S(2)}, u32[]{:S(2)}) collective-permute-start(bf16[4,16,1024]{2,1,0:T(8,128)(2,1)S(1)} %collective-permute-done.5.refs_8_), channel_id=1, source_target_pairs={{0,4},{4,8},{8,12},{12,14},{14,10},{10,6},{6,2},{2,0},{1,5},{5,9},... | collective-permute-start | bytes 393224 | tf_op jit(solution)/shard_map/ppermute | solution.py:273
  26.3 0.0 collective-permute-done.1.refs_2_
  26.3 0.3 collective-permute-start.2
  26.6 0.8 %collective-permute-done.10.refs_4_ = bf16[4,16,1024]{2,1,0:T(8,128)(2,1)S(1)} collective-permute-done((bf16[4,16,1024]{2,1,0:T(8,128)(2,1)S(1)}, bf16[4,16,1024]{2,1,0:T(8,128)(2,1)S(1)}, u32[]{:S(2)}, u32[]{:S(2)}) %collective-permute-start.10) | collective-permute-done | bytes 131104 | tf_op jit(solution)/shard_map/ppermute | solution.py:273
  27.4 2.1 %shard_map.70 = (f32[4,16,1024]{2,1,0:T(8,128)S(1)}, bf16[4,16,1024]{2,1,0:T(8,128)(2,1)S(1)}, bf16[4,16,1024]{2,1,0:T(8,128)(2,1)S(1)}, bf16[4,16,1024]{2,1,0:T...) custom-call(bf16[6,128,1024]{2,1,0:T(8,128)(2,1)S(1)} %copy-done.5, ...), custom_call_target="tpu_custom_call" | custom-call | flops 1610612736 | bytes 3670016 | tf_op jit(solution)/shard_map/pallas_call | solution.py:165
  29.6 1.6 %collective-permute-start.23 = (bf16[4,16,1024]{2,1,0:T(8,128)(2,1)S(1)}, bf16[4,16,1024]{2,1,0:T(8,128)(2,1)S(1)}, u32[]{:S(2)}, u32[]{:S(2)}) collective-permute-start(bf16[4,16,1024]{2,1,0:T(8,128)(2,1)S(1)} %get-tuple-element.33), channel_id=1, source_target_pairs={{0,4},{4,8},{8,12},{12,14},{14,10},{10,6},{6,2},{2,0},{1,5},{5,9},... | collective-permute-start | bytes 393224 | tf_op jit(solution)/shard_map/ppermute | solution.py:273
  31.2 0.4 collective-permute-start.27
  31.6 1.6 %collective-permute-start.7 = (bf16[4,16,1024]{2,1,0:T(8,128)(2,1)S(1)}, bf16[4,16,1024]{2,1,0:T(8,128)(2,1)S(1)}, u32[]{:S(2)}, u32[]{:S(2)}) collective-permute-start(bf16[4,16,1024]{2,1,0:T(8,128)(2,1)S(1)} %collective-permute-done.6.refs_7_), channel_id=1, source_target_pairs={{0,4},{4,8},{8,12},{12,14},{14,10},{10,6},{6,2},{2,0},{1,5},{5,9},... | collective-permute-start | bytes 393224 | tf_op jit(solution)/shard_map/ppermute | solution.py:273
  33.2 0.5 collective-permute-start.3
  33.7 2.0 %collective-permute-done.23 = bf16[4,16,1024]{2,1,0:T(8,128)(2,1)S(1)} collective-permute-done((bf16[4,16,1024]{2,1,0:T(8,128)(2,1)S(1)}, bf16[4,16,1024]{2,1,0:T(8,128)(2,1)S(1)}, u32[]{:S(2)}, u32[]{:S(2)}) %collective-permute-start.23) | collective-permute-done | bytes 131104 | tf_op jit(solution)/shard_map/ppermute | solution.py:273
  35.8 1.8 %collective-permute-start.24 = (bf16[4,16,1024]{2,1,0:T(8,128)(2,1)S(1)}, bf16[4,16,1024]{2,1,0:T(8,128)(2,1)S(1)}, u32[]{:S(2)}, u32[]{:S(2)}) collective-permute-start(bf16[4,16,1024]{2,1,0:T(8,128)(2,1)S(1)} %add_convert_fusion.4), channel_id=1, source_target_pairs={{0,4},{4,8},{8,12},{12,14},{14,10},{10,6},{6,2},{2,0},{1,5},{5,9},... | collective-permute-start | bytes 393224 | tf_op jit(solution)/shard_map/ppermute | solution.py:273
  37.5 2.1 %collective-permute-done.3.refs_4_ = bf16[4,16,1024]{2,1,0:T(8,128)(2,1)S(1)} collective-permute-done((bf16[4,16,1024]{2,1,0:T(8,128)(2,1)S(1)}, bf16[4,16,1024]{2,1,0:T(8,128)(2,1)S(1)}, u32[]{:S(2)}, u32[]{:S(2)}) %collective-permute-start.3) | collective-permute-done | bytes 131104 | tf_op jit(solution)/shard_map/ppermute | solution.py:273
  39.6 0.5 collective-permute-start.4
  40.1 0.5 collective-permute-start.28
  40.6 4.0 %collective-permute-done.4.refs_5_ = bf16[4,16,1024]{2,1,0:T(8,128)(2,1)S(1)} collective-permute-done((bf16[4,16,1024]{2,1,0:T(8,128)(2,1)S(1)}, bf16[4,16,1024]{2,1,0:T(8,128)(2,1)S(1)}, u32[]{:S(2)}, u32[]{:S(2)}) %collective-permute-start.4) | collective-permute-done | bytes 131104 | tf_op jit(solution)/shard_map/ppermute | solution.py:273
  44.6 2.1 %shard_map.71 = (f32[4,16,1024]{2,1,0:T(8,128)S(1)}, bf16[4,16,1024]{2,1,0:T(8,128)(2,1)S(1)}, bf16[4,16,1024]{2,1,0:T(8,128)(2,1)S(1)}, bf16[4,16,1024]{2,1,0:T...) custom-call(bf16[6,128,1024]{2,1,0:T(8,128)(2,1)S(1)} %copy-done.5, ...), custom_call_target="tpu_custom_call" | custom-call | flops 1610612736 | bytes 3670016 | tf_op jit(solution)/shard_map/pallas_call | solution.py:165
  46.7 0.6 collective-permute-start.30
  47.3 0.0 copy-start.3
  47.3 0.0 copy-start.4
  47.3 1.1 %collective-permute-start.25 = (bf16[4,16,1024]{2,1,0:T(8,128)(2,1)S(1)}, bf16[4,16,1024]{2,1,0:T(8,128)(2,1)S(1)}, u32[]{:S(2)}, u32[]{:S(2)}) collective-permute-start(bf16[4,16,1024]{2,1,0:T(8,128)(2,1)S(1)} %add_convert_fusion.3), channel_id=1, source_target_pairs={{0,4},{4,8},{8,12},{12,14},{14,10},{10,6},{6,2},{2,0},{1,5},{5,9},... | collective-permute-start | bytes 393224 | tf_op jit(solution)/shard_map/ppermute | solution.py:273
  48.4 1.0 %collective-permute-start.18 = (bf16[4,16,1024]{2,1,0:T(8,128)(2,1)S(1)}, bf16[4,16,1024]{2,1,0:T(8,128)(2,1)S(1)}, u32[]{:S(2)}, u32[]{:S(2)}) collective-permute-start(bf16[4,16,1024]{2,1,0:T(8,128)(2,1)S(1)} %get-tuple-element.28), channel_id=1, source_target_pairs={{0,2},{4,0},{8,4},{12,8},{14,12},{10,14},{6,10},{2,6},{1,3},{5,1},... | collective-permute-start | bytes 393224 | tf_op jit(solution)/shard_map/ppermute | solution.py:273
  49.4 1.0 %collective-permute-done.30 = f32[8,128]{1,0:T(8,128)S(1)} collective-permute-done((f32[8,128]{1,0:T(8,128)S(1)}, f32[8,128]{1,0:T(8,128)S(1)}, u32[]{:S(2)}, u32[]{:S(2)}) %collective-permute-start.30) | collective-permute-done | bytes 4128 | tf_op jit(solution)/shard_map/ppermute | solution.py:300
  50.4 1.5 %collective-permute-start.31 = (f32[8,128]{1,0:T(8,128)S(1)}, f32[8,128]{1,0:T(8,128)S(1)}, u32[]{:S(2)}, u32[]{:S(2)}) collective-permute-start(f32[8,128]{1,0:T(8,128)S(1)} %add.67), channel_id=1, source_target_pairs={{0,4},{2,6},{4,0},{6,2},{8,12},{10,14},{12,8},{14,10},{1,5},{3,7},... | collective-permute-start | bytes 12296 | tf_op jit(solution)/shard_map/ppermute | solution.py:300
  51.9 0.6 collective-permute-start.29
  52.5 1.5 %collective-permute-start.15 = (bf16[4,16,1024]{2,1,0:T(8,128)(2,1)S(1)}, bf16[4,16,1024]{2,1,0:T(8,128)(2,1)S(1)}, u32[]{:S(2)}, u32[]{:S(2)}) collective-permute-start(bf16[4,16,1024]{2,1,0:T(8,128)(2,1)S(1)} %get-tuple-element.24), channel_id=1, source_target_pairs={{0,4},{4,8},{8,12},{12,14},{14,10},{10,6},{6,2},{2,0},{1,5},{5,9},... | collective-permute-start | bytes 393224 | tf_op jit(solution)/shard_map/ppermute | solution.py:273
  54.0 0.4 collective-permute-done.31
  54.3 1.5 %collective-permute-start.32 = (f32[8,128]{1,0:T(8,128)S(1)}, f32[8,128]{1,0:T(8,128)S(1)}, u32[]{:S(2)}, u32[]{:S(2)}) collective-permute-start(f32[8,128]{1,0:T(8,128)S(1)} %add.68), channel_id=1, source_target_pairs={{0,8},{2,10},{4,12},{6,14},{8,0},{10,2},{12,4},{14,6},{1,9},{3,11}... | collective-permute-start | bytes 12296 | tf_op jit(solution)/shard_map/ppermute | solution.py:300
  55.8 0.7 collective-permute-start.19
  56.5 1.7 %collective-permute-done.15 = bf16[4,16,1024]{2,1,0:T(8,128)(2,1)S(1)} collective-permute-done((bf16[4,16,1024]{2,1,0:T(8,128)(2,1)S(1)}, bf16[4,16,1024]{2,1,0:T(8,128)(2,1)S(1)}, u32[]{:S(2)}, u32[]{:S(2)}) %collective-permute-start.15) | collective-permute-done | bytes 131104 | tf_op jit(solution)/shard_map/ppermute | solution.py:273
  58.3 1.2 %collective-permute-start.16 = (bf16[4,16,1024]{2,1,0:T(8,128)(2,1)S(1)}, bf16[4,16,1024]{2,1,0:T(8,128)(2,1)S(1)}, u32[]{:S(2)}, u32[]{:S(2)}) collective-permute-start(bf16[4,16,1024]{2,1,0:T(8,128)(2,1)S(1)} %add_convert_fusion.9), channel_id=1, source_target_pairs={{0,4},{4,8},{8,12},{12,14},{14,10},{10,6},{6,2},{2,0},{1,5},{5,9},... | collective-permute-start | bytes 393224 | tf_op jit(solution)/shard_map/ppermute | solution.py:273
  59.5 1.3 %collective-permute-done.19 = bf16[4,16,1024]{2,1,0:T(8,128)(2,1)S(1)} collective-permute-done((bf16[4,16,1024]{2,1,0:T(8,128)(2,1)S(1)}, bf16[4,16,1024]{2,1,0:T(8,128)(2,1)S(1)}, u32[]{:S(2)}, u32[]{:S(2)}) %collective-permute-start.19) | collective-permute-done | bytes 131104 | tf_op jit(solution)/shard_map/ppermute | solution.py:273
  60.9 0.7 collective-permute-start.20
  61.6 2.8 %collective-permute-done.16 = bf16[4,16,1024]{2,1,0:T(8,128)(2,1)S(1)} collective-permute-done((bf16[4,16,1024]{2,1,0:T(8,128)(2,1)S(1)}, bf16[4,16,1024]{2,1,0:T(8,128)(2,1)S(1)}, u32[]{:S(2)}, u32[]{:S(2)}) %collective-permute-start.16) | collective-permute-done | bytes 131104 | tf_op jit(solution)/shard_map/ppermute | solution.py:273
  64.3 1.4 %collective-permute-start.17 = (bf16[4,16,1024]{2,1,0:T(8,128)(2,1)S(1)}, bf16[4,16,1024]{2,1,0:T(8,128)(2,1)S(1)}, u32[]{:S(2)}, u32[]{:S(2)}) collective-permute-start(bf16[4,16,1024]{2,1,0:T(8,128)(2,1)S(1)} %add_convert_fusion.8), channel_id=1, source_target_pairs={{0,4},{4,8},{8,12},{12,14},{14,10},{10,6},{6,2},{2,0},{1,5},{5,9},... | collective-permute-start | bytes 393224 | tf_op jit(solution)/shard_map/ppermute | solution.py:273
  65.8 0.1 collective-permute-done.20
  66.0 0.7 collective-permute-start.21
  66.7 1.5 %collective-permute-start.26 = (bf16[4,16,1024]{2,1,0:T(8,128)(2,1)S(1)}, bf16[4,16,1024]{2,1,0:T(8,128)(2,1)S(1)}, u32[]{:S(2)}, u32[]{:S(2)}) collective-permute-start(bf16[4,16,1024]{2,1,0:T(8,128)(2,1)S(1)} %add_convert_fusion.2), channel_id=1, source_target_pairs={{0,4},{4,8},{8,12},{12,14},{14,10},{10,6},{6,2},{2,0},{1,5},{5,9},... | collective-permute-start | bytes 393224 | tf_op jit(solution)/shard_map/ppermute | solution.py:273
  68.1 1.2 %collective-permute-done.17.refs_4_ = bf16[4,16,1024]{2,1,0:T(8,128)(2,1)S(1)} collective-permute-done((bf16[4,16,1024]{2,1,0:T(8,128)(2,1)S(1)}, bf16[4,16,1024]{2,1,0:T(8,128)(2,1)S(1)}, u32[]{:S(2)}, u32[]{:S(2)}) %collective-permute-start.17) | collective-permute-done | bytes 131104 | tf_op jit(solution)/shard_map/ppermute | solution.py:273
  69.4 1.6 %collective-permute-done.21.refs_5_ = bf16[4,16,1024]{2,1,0:T(8,128)(2,1)S(1)} collective-permute-done((bf16[4,16,1024]{2,1,0:T(8,128)(2,1)S(1)}, bf16[4,16,1024]{2,1,0:T(8,128)(2,1)S(1)}, u32[]{:S(2)}, u32[]{:S(2)}) %collective-permute-start.21) | collective-permute-done | bytes 131104 | tf_op jit(solution)/shard_map/ppermute | solution.py:273
  71.0 0.1 collective-permute-start.22
  71.1 0.6 add_reduce_fusion
  71.7 0.6 collective-permute-done.22.edge_ref
  72.3 1.6 %parents.1 = bf16[16,8,1024]{2,1,0:T(8,128)(2,1)} custom-call(s32[16]{0:T(128)S(1)} %copy-done.3, s32[8]{0:T(128)S(1)} %copy-done.4, bf16[16,1024]{1,0:T(8,128)(2,1)S(1)} %collective-permute-done.22.edge_ref, f32[4,16,1024]{2,1,0:T(8,128)S(1)} %get-tuple-element.29.refs_0_, bf16[4,16,1024]{2,1,0:T(8,128)(2,1)S(1)} %collective-permute-done.26.refs_1_, ...), custom_call_target="tpu_custom_call" | custom-call | flops 786432 | bytes 1310720 | tf_op jit(solution)/shard_map/parents/pallas_call | solution.py:226
  (33 shorter events, 0.4 us)
Async XLA Ops:
  0.6 1.0 %copy-start = (bf16[16,8,1024]{2,1,0:T(8,128)(2,1)S(1)}, bf16[16,8,1024]{2,1,0:T(8,128)(2,1)}, u32[]{:S(2)}) copy-start(bf16[16,8,1024]{2,1,0:T(8,128)(2,1)} %green_ref.3) | copy-start | bytes 786436
  1.6 0.9 %copy-start.1 = (bf16[16,8,1024]{2,1,0:T(8,128)(2,1)S(1)}, bf16[16,8,1024]{2,1,0:T(8,128)(2,1)}, u32[]{:S(2)}) copy-start(bf16[16,8,1024]{2,1,0:T(8,128)(2,1)} %delta_ref.3) | copy-start | bytes 786436
  2.5 0.7 copy-start.2
  3.2 24.3 %copy-start.5 = (bf16[6,128,1024]{2,1,0:T(8,128)(2,1)S(1)}, bf16[6,128,1024]{2,1,0:T(8,128)(2,1)}, u32[]{:S(2)}) copy-start(bf16[6,128,1024]{2,1,0:T(8,128)(2,1)} %refs_0_.3) | copy-start | bytes 4718596
  3.9 6.5 %collective-permute-start.11 = (bf16[4,16,1024]{2,1,0:T(8,128)(2,1)S(1)}, bf16[4,16,1024]{2,1,0:T(8,128)(2,1)S(1)}, u32[]{:S(2)}, u32[]{:S(2)}) collective-permute-start(bf16[4,16,1024]{2,1,0:T(8,128)(2,1)S(1)} %shard_map.69.refs_1_), channel_id=1, source_target_pairs={{0,4},{4,8},{8,12},{12,14},{14,10},{10,6},{6,2},{2,0},{1,5},{5,9},... | collective-permute-start | bytes 393224 | tf_op jit(solution)/shard_map/ppermute | solution.py:273
  7.0 10.2 %collective-permute-start = (bf16[16,8,1024]{2,1,0:T(8,128)(2,1)S(1)}, bf16[16,8,1024]{2,1,0:T(8,128)(2,1)S(1)}, u32[]{:S(2)}, u32[]{:S(2)}) collective-permute-start(bf16[16,8,1024]{2,1,0:T(8,128)(2,1)S(1)} %copy-done), channel_id=1, source_target_pairs={{0,1},{1,0},{2,3},{3,2},{4,5},{5,4},{6,7},{7,6},{8,9},{9,8},{10,11... | collective-permute-start | bytes 786440 | tf_op jit(solution)/shard_map/ppermute | solution.py:246
  7.0 5.9 %collective-permute-start.8 = (bf16[4,16,1024]{2,1,0:T(8,128)(2,1)S(1)}, bf16[4,16,1024]{2,1,0:T(8,128)(2,1)S(1)}, u32[]{:S(2)}, u32[]{:S(2)}) collective-permute-start(bf16[4,16,1024]{2,1,0:T(8,128)(2,1)S(1)} %shard_map.69.refs_1_), channel_id=1, source_target_pairs={{0,2},{4,0},{8,4},{12,8},{14,12},{10,14},{6,10},{2,6},{1,3},{5,1},... | collective-permute-start | bytes 393224 | tf_op jit(solution)/shard_map/ppermute | solution.py:273
  10.4 5.0 %collective-permute-start.12 = (bf16[4,16,1024]{2,1,0:T(8,128)(2,1)S(1)}, bf16[4,16,1024]{2,1,0:T(8,128)(2,1)S(1)}, u32[]{:S(2)}, u32[]{:S(2)}) collective-permute-start(bf16[4,16,1024]{2,1,0:T(8,128)(2,1)S(1)} %collective-permute-done.11.refs_8_), channel_id=1, source_target_pairs={{0,4},{4,8},{8,12},{12,14},{14,10},{10,6},{6,2},{2,0},{1,5},{5,9},... | collective-permute-start | bytes 393224 | tf_op jit(solution)/shard_map/ppermute | solution.py:273
  12.9 7.2 %collective-permute-start.9 = (bf16[4,16,1024]{2,1,0:T(8,128)(2,1)S(1)}, bf16[4,16,1024]{2,1,0:T(8,128)(2,1)S(1)}, u32[]{:S(2)}, u32[]{:S(2)}) collective-permute-start(bf16[4,16,1024]{2,1,0:T(8,128)(2,1)S(1)} %collective-permute-done.8.refs_2_), channel_id=1, source_target_pairs={{0,2},{4,0},{8,4},{12,8},{14,12},{10,14},{6,10},{2,6},{1,3},{5,1},... | collective-permute-start | bytes 393224 | tf_op jit(solution)/shard_map/ppermute | solution.py:273
  15.4 6.4 %collective-permute-start.13 = (bf16[4,16,1024]{2,1,0:T(8,128)(2,1)S(1)}, bf16[4,16,1024]{2,1,0:T(8,128)(2,1)S(1)}, u32[]{:S(2)}, u32[]{:S(2)}) collective-permute-start(bf16[4,16,1024]{2,1,0:T(8,128)(2,1)S(1)} %collective-permute-done.12.refs_7_), channel_id=1, source_target_pairs={{0,4},{4,8},{8,12},{12,14},{14,10},{10,6},{6,2},{2,0},{1,5},{5,9},... | collective-permute-start | bytes 393224 | tf_op jit(solution)/shard_map/ppermute | solution.py:273
  18.0 6.5 %collective-permute-start.5 = (bf16[4,16,1024]{2,1,0:T(8,128)(2,1)S(1)}, bf16[4,16,1024]{2,1,0:T(8,128)(2,1)S(1)}, u32[]{:S(2)}, u32[]{:S(2)}) collective-permute-start(bf16[4,16,1024]{2,1,0:T(8,128)(2,1)S(1)} %shard_map.68.refs_1_), channel_id=1, source_target_pairs={{0,4},{4,8},{8,12},{12,14},{14,10},{10,6},{6,2},{2,0},{1,5},{5,9},... | collective-permute-start | bytes 393224 | tf_op jit(solution)/shard_map/ppermute | solution.py:273
  19.7 6.6 %collective-permute-start.1 = (bf16[4,16,1024]{2,1,0:T(8,128)(2,1)S(1)}, bf16[4,16,1024]{2,1,0:T(8,128)(2,1)S(1)}, u32[]{:S(2)}, u32[]{:S(2)}) collective-permute-start(bf16[4,16,1024]{2,1,0:T(8,128)(2,1)S(1)} %shard_map.68.refs_1_), channel_id=1, source_target_pairs={{0,2},{4,0},{8,4},{12,8},{14,12},{10,14},{6,10},{2,6},{1,3},{5,1},... | collective-permute-start | bytes 393224 | tf_op jit(solution)/shard_map/ppermute | solution.py:273
  20.1 7.3 %collective-permute-start.10 = (bf16[4,16,1024]{2,1,0:T(8,128)(2,1)S(1)}, bf16[4,16,1024]{2,1,0:T(8,128)(2,1)S(1)}, u32[]{:S(2)}, u32[]{:S(2)}) collective-permute-start(bf16[4,16,1024]{2,1,0:T(8,128)(2,1)S(1)} %collective-permute-done.9.refs_3_), channel_id=1, source_target_pairs={{0,2},{4,0},{8,4},{12,8},{14,12},{10,14},{6,10},{2,6},{1,3},{5,1},... | collective-permute-start | bytes 393224 | tf_op jit(solution)/shard_map/ppermute | solution.py:273
  21.8 5.7 %collective-permute-start.14 = (bf16[4,16,1024]{2,1,0:T(8,128)(2,1)S(1)}, bf16[4,16,1024]{2,1,0:T(8,128)(2,1)S(1)}, u32[]{:S(2)}, u32[]{:S(2)}) collective-permute-start(bf16[4,16,1024]{2,1,0:T(8,128)(2,1)S(1)} %collective-permute-done.13.refs_6_), channel_id=1, source_target_pairs={{0,4},{4,8},{8,12},{12,14},{14,10},{10,6},{6,2},{2,0},{1,5},{5,9},... | collective-permute-start | bytes 393224 | tf_op jit(solution)/shard_map/ppermute | solution.py:273
  24.6 7.1 %collective-permute-start.6 = (bf16[4,16,1024]{2,1,0:T(8,128)(2,1)S(1)}, bf16[4,16,1024]{2,1,0:T(8,128)(2,1)S(1)}, u32[]{:S(2)}, u32[]{:S(2)}) collective-permute-start(bf16[4,16,1024]{2,1,0:T(8,128)(2,1)S(1)} %collective-permute-done.5.refs_8_), channel_id=1, source_target_pairs={{0,4},{4,8},{8,12},{12,14},{14,10},{10,6},{6,2},{2,0},{1,5},{5,9},... | collective-permute-start | bytes 393224 | tf_op jit(solution)/shard_map/ppermute | solution.py:273
  26.3 6.9 %collective-permute-start.2 = (bf16[4,16,1024]{2,1,0:T(8,128)(2,1)S(1)}, bf16[4,16,1024]{2,1,0:T(8,128)(2,1)S(1)}, u32[]{:S(2)}, u32[]{:S(2)}) collective-permute-start(bf16[4,16,1024]{2,1,0:T(8,128)(2,1)S(1)} %collective-permute-done.1.refs_2_), channel_id=1, source_target_pairs={{0,2},{4,0},{8,4},{12,8},{14,12},{10,14},{6,10},{2,6},{1,3},{5,1},... | collective-permute-start | bytes 393224 | tf_op jit(solution)/shard_map/ppermute | solution.py:273
  29.6 6.2 %collective-permute-start.23 = (bf16[4,16,1024]{2,1,0:T(8,128)(2,1)S(1)}, bf16[4,16,1024]{2,1,0:T(8,128)(2,1)S(1)}, u32[]{:S(2)}, u32[]{:S(2)}) collective-permute-start(bf16[4,16,1024]{2,1,0:T(8,128)(2,1)S(1)} %get-tuple-element.33), channel_id=1, source_target_pairs={{0,4},{4,8},{8,12},{12,14},{14,10},{10,6},{6,2},{2,0},{1,5},{5,9},... | collective-permute-start | bytes 393224 | tf_op jit(solution)/shard_map/ppermute | solution.py:273
  31.2 8.9 %collective-permute-start.27 = (bf16[4,16,1024]{2,1,0:T(8,128)(2,1)S(1)}, bf16[4,16,1024]{2,1,0:T(8,128)(2,1)S(1)}, u32[]{:S(2)}, u32[]{:S(2)}) collective-permute-start(bf16[4,16,1024]{2,1,0:T(8,128)(2,1)S(1)} %get-tuple-element.36), channel_id=1, source_target_pairs={{0,2},{4,0},{8,4},{12,8},{14,12},{10,14},{6,10},{2,6},{1,3},{5,1},... | collective-permute-start | bytes 393224 | tf_op jit(solution)/shard_map/ppermute | solution.py:273
  31.6 8.9 %collective-permute-start.7 = (bf16[4,16,1024]{2,1,0:T(8,128)(2,1)S(1)}, bf16[4,16,1024]{2,1,0:T(8,128)(2,1)S(1)}, u32[]{:S(2)}, u32[]{:S(2)}) collective-permute-start(bf16[4,16,1024]{2,1,0:T(8,128)(2,1)S(1)} %collective-permute-done.6.refs_7_), channel_id=1, source_target_pairs={{0,4},{4,8},{8,12},{12,14},{14,10},{10,6},{6,2},{2,0},{1,5},{5,9},... | collective-permute-start | bytes 393224 | tf_op jit(solution)/shard_map/ppermute | solution.py:273
  33.2 6.4 %collective-permute-start.3 = (bf16[4,16,1024]{2,1,0:T(8,128)(2,1)S(1)}, bf16[4,16,1024]{2,1,0:T(8,128)(2,1)S(1)}, u32[]{:S(2)}, u32[]{:S(2)}) collective-permute-start(bf16[4,16,1024]{2,1,0:T(8,128)(2,1)S(1)} %collective-permute-done.2.refs_3_), channel_id=1, source_target_pairs={{0,2},{4,0},{8,4},{12,8},{14,12},{10,14},{6,10},{2,6},{1,3},{5,1},... | collective-permute-start | bytes 393224 | tf_op jit(solution)/shard_map/ppermute | solution.py:273
  35.8 11.5 %collective-permute-start.24 = (bf16[4,16,1024]{2,1,0:T(8,128)(2,1)S(1)}, bf16[4,16,1024]{2,1,0:T(8,128)(2,1)S(1)}, u32[]{:S(2)}, u32[]{:S(2)}) collective-permute-start(bf16[4,16,1024]{2,1,0:T(8,128)(2,1)S(1)} %add_convert_fusion.4), channel_id=1, source_target_pairs={{0,4},{4,8},{8,12},{12,14},{14,10},{10,6},{6,2},{2,0},{1,5},{5,9},... | collective-permute-start | bytes 393224 | tf_op jit(solution)/shard_map/ppermute | solution.py:273
  39.6 5.0 %collective-permute-start.4 = (bf16[4,16,1024]{2,1,0:T(8,128)(2,1)S(1)}, bf16[4,16,1024]{2,1,0:T(8,128)(2,1)S(1)}, u32[]{:S(2)}, u32[]{:S(2)}) collective-permute-start(bf16[4,16,1024]{2,1,0:T(8,128)(2,1)S(1)} %collective-permute-done.3.refs_4_), channel_id=1, source_target_pairs={{0,2},{4,0},{8,4},{12,8},{14,12},{10,14},{6,10},{2,6},{1,3},{5,1},... | collective-permute-start | bytes 393224 | tf_op jit(solution)/shard_map/ppermute | solution.py:273
  40.1 11.8 %collective-permute-start.28 = (bf16[4,16,1024]{2,1,0:T(8,128)(2,1)S(1)}, bf16[4,16,1024]{2,1,0:T(8,128)(2,1)S(1)}, u32[]{:S(2)}, u32[]{:S(2)}) collective-permute-start(bf16[4,16,1024]{2,1,0:T(8,128)(2,1)S(1)} %add_convert_fusion.1), channel_id=1, source_target_pairs={{0,2},{4,0},{8,4},{12,8},{14,12},{10,14},{6,10},{2,6},{1,3},{5,1},... | collective-permute-start | bytes 393224 | tf_op jit(solution)/shard_map/ppermute | solution.py:273
  46.7 3.7 %collective-permute-start.30 = (f32[8,128]{1,0:T(8,128)S(1)}, f32[8,128]{1,0:T(8,128)S(1)}, u32[]{:S(2)}, u32[]{:S(2)}) collective-permute-start(f32[8,128]{1,0:T(8,128)S(1)} %get-tuple-element.37), channel_id=1, source_target_pairs={{0,2},{2,0},{4,6},{6,4},{8,10},{10,8},{12,14},{14,12},{1,3},{3,1},... | collective-permute-start | bytes 12296 | tf_op jit(solution)/shard_map/ppermute | solution.py:300
  47.3 25.0 %copy-start.3 = (s32[16]{0:T(128)S(1)}, s32[16]{0:T(128)}, u32[]{:S(2)}) copy-start(s32[16]{0:T(128)} %parents_ref.5) | copy-start | bytes 196
  47.3 25.0 %copy-start.4 = (s32[8]{0:T(128)S(1)}, s32[8]{0:T(128)}, u32[]{:S(2)}) copy-start(s32[8]{0:T(128)} %counts_ref.1) | copy-start | bytes 100
  47.3 19.3 %collective-permute-start.25 = (bf16[4,16,1024]{2,1,0:T(8,128)(2,1)S(1)}, bf16[4,16,1024]{2,1,0:T(8,128)(2,1)S(1)}, u32[]{:S(2)}, u32[]{:S(2)}) collective-permute-start(bf16[4,16,1024]{2,1,0:T(8,128)(2,1)S(1)} %add_convert_fusion.3), channel_id=1, source_target_pairs={{0,4},{4,8},{8,12},{12,14},{14,10},{10,6},{6,2},{2,0},{1,5},{5,9},... | collective-permute-start | bytes 393224 | tf_op jit(solution)/shard_map/ppermute | solution.py:273
  48.4 7.4 %collective-permute-start.18 = (bf16[4,16,1024]{2,1,0:T(8,128)(2,1)S(1)}, bf16[4,16,1024]{2,1,0:T(8,128)(2,1)S(1)}, u32[]{:S(2)}, u32[]{:S(2)}) collective-permute-start(bf16[4,16,1024]{2,1,0:T(8,128)(2,1)S(1)} %get-tuple-element.28), channel_id=1, source_target_pairs={{0,2},{4,0},{8,4},{12,8},{14,12},{10,14},{6,10},{2,6},{1,3},{5,1},... | collective-permute-start | bytes 393224 | tf_op jit(solution)/shard_map/ppermute | solution.py:273
  50.4 4.0 %collective-permute-start.31 = (f32[8,128]{1,0:T(8,128)S(1)}, f32[8,128]{1,0:T(8,128)S(1)}, u32[]{:S(2)}, u32[]{:S(2)}) collective-permute-start(f32[8,128]{1,0:T(8,128)S(1)} %add.67), channel_id=1, source_target_pairs={{0,4},{2,6},{4,0},{6,2},{8,12},{10,14},{12,8},{14,10},{1,5},{3,7},... | collective-permute-start | bytes 12296 | tf_op jit(solution)/shard_map/ppermute | solution.py:300
  51.9 19.8 %collective-permute-start.29 = (bf16[4,16,1024]{2,1,0:T(8,128)(2,1)S(1)}, bf16[4,16,1024]{2,1,0:T(8,128)(2,1)S(1)}, u32[]{:S(2)}, u32[]{:S(2)}) collective-permute-start(bf16[4,16,1024]{2,1,0:T(8,128)(2,1)S(1)} %add_convert_fusion), channel_id=1, source_target_pairs={{0,2},{4,0},{8,4},{12,8},{14,12},{10,14},{6,10},{2,6},{1,3},{5,1},... | collective-permute-start | bytes 393224 | tf_op jit(solution)/shard_map/ppermute | solution.py:273
  52.5 5.7 %collective-permute-start.15 = (bf16[4,16,1024]{2,1,0:T(8,128)(2,1)S(1)}, bf16[4,16,1024]{2,1,0:T(8,128)(2,1)S(1)}, u32[]{:S(2)}, u32[]{:S(2)}) collective-permute-start(bf16[4,16,1024]{2,1,0:T(8,128)(2,1)S(1)} %get-tuple-element.24), channel_id=1, source_target_pairs={{0,4},{4,8},{8,12},{12,14},{14,10},{10,6},{6,2},{2,0},{1,5},{5,9},... | collective-permute-start | bytes 393224 | tf_op jit(solution)/shard_map/ppermute | solution.py:273
  54.3 16.7 %collective-permute-start.32 = (f32[8,128]{1,0:T(8,128)S(1)}, f32[8,128]{1,0:T(8,128)S(1)}, u32[]{:S(2)}, u32[]{:S(2)}) collective-permute-start(f32[8,128]{1,0:T(8,128)S(1)} %add.68), channel_id=1, source_target_pairs={{0,8},{2,10},{4,12},{6,14},{8,0},{10,2},{12,4},{14,6},{1,9},{3,11}... | collective-permute-start | bytes 12296 | tf_op jit(solution)/shard_map/ppermute | solution.py:300
  55.8 5.0 %collective-permute-start.19 = (bf16[4,16,1024]{2,1,0:T(8,128)(2,1)S(1)}, bf16[4,16,1024]{2,1,0:T(8,128)(2,1)S(1)}, u32[]{:S(2)}, u32[]{:S(2)}) collective-permute-start(bf16[4,16,1024]{2,1,0:T(8,128)(2,1)S(1)} %add_convert_fusion.7), channel_id=1, source_target_pairs={{0,2},{4,0},{8,4},{12,8},{14,12},{10,14},{6,10},{2,6},{1,3},{5,1},... | collective-permute-start | bytes 393224 | tf_op jit(solution)/shard_map/ppermute | solution.py:273
  58.3 6.0 %collective-permute-start.16 = (bf16[4,16,1024]{2,1,0:T(8,128)(2,1)S(1)}, bf16[4,16,1024]{2,1,0:T(8,128)(2,1)S(1)}, u32[]{:S(2)}, u32[]{:S(2)}) collective-permute-start(bf16[4,16,1024]{2,1,0:T(8,128)(2,1)S(1)} %add_convert_fusion.9), channel_id=1, source_target_pairs={{0,4},{4,8},{8,12},{12,14},{14,10},{10,6},{6,2},{2,0},{1,5},{5,9},... | collective-permute-start | bytes 393224 | tf_op jit(solution)/shard_map/ppermute | solution.py:273
  60.9 5.0 %collective-permute-start.20 = (bf16[4,16,1024]{2,1,0:T(8,128)(2,1)S(1)}, bf16[4,16,1024]{2,1,0:T(8,128)(2,1)S(1)}, u32[]{:S(2)}, u32[]{:S(2)}) collective-permute-start(bf16[4,16,1024]{2,1,0:T(8,128)(2,1)S(1)} %add_convert_fusion.6), channel_id=1, source_target_pairs={{0,2},{4,0},{8,4},{12,8},{14,12},{10,14},{6,10},{2,6},{1,3},{5,1},... | collective-permute-start | bytes 393224 | tf_op jit(solution)/shard_map/ppermute | solution.py:273
  64.3 5.0 %collective-permute-start.17 = (bf16[4,16,1024]{2,1,0:T(8,128)(2,1)S(1)}, bf16[4,16,1024]{2,1,0:T(8,128)(2,1)S(1)}, u32[]{:S(2)}, u32[]{:S(2)}) collective-permute-start(bf16[4,16,1024]{2,1,0:T(8,128)(2,1)S(1)} %add_convert_fusion.8), channel_id=1, source_target_pairs={{0,4},{4,8},{8,12},{12,14},{14,10},{10,6},{6,2},{2,0},{1,5},{5,9},... | collective-permute-start | bytes 393224 | tf_op jit(solution)/shard_map/ppermute | solution.py:273
  66.0 5.0 %collective-permute-start.21 = (bf16[4,16,1024]{2,1,0:T(8,128)(2,1)S(1)}, bf16[4,16,1024]{2,1,0:T(8,128)(2,1)S(1)}, u32[]{:S(2)}, u32[]{:S(2)}) collective-permute-start(bf16[4,16,1024]{2,1,0:T(8,128)(2,1)S(1)} %add_convert_fusion.5), channel_id=1, source_target_pairs={{0,2},{4,0},{8,4},{12,8},{14,12},{10,14},{6,10},{2,6},{1,3},{5,1},... | collective-permute-start | bytes 393224 | tf_op jit(solution)/shard_map/ppermute | solution.py:273
  66.7 5.1 %collective-permute-start.26 = (bf16[4,16,1024]{2,1,0:T(8,128)(2,1)S(1)}, bf16[4,16,1024]{2,1,0:T(8,128)(2,1)S(1)}, u32[]{:S(2)}, u32[]{:S(2)}) collective-permute-start(bf16[4,16,1024]{2,1,0:T(8,128)(2,1)S(1)} %add_convert_fusion.2), channel_id=1, source_target_pairs={{0,4},{4,8},{8,12},{12,14},{14,10},{10,6},{6,2},{2,0},{1,5},{5,9},... | collective-permute-start | bytes 393224 | tf_op jit(solution)/shard_map/ppermute | solution.py:273
  71.0 1.3 %collective-permute-start.22 = (bf16[16,1024]{1,0:T(8,128)(2,1)S(1)}, bf16[16,1024]{1,0:T(8,128)(2,1)S(1)}, u32[]{:S(2)}, u32[]{:S(2)}) collective-permute-start(bf16[16,1024]{1,0:T(8,128)(2,1)S(1)} %fusion), channel_id=1, source_target_pairs={{0,1},{1,0},{2,3},{3,2},{4,5},{5,4},{6,7},{7,6},{8,9},{9,8},{10,11... | collective-permute-start | bytes 98312 | tf_op jit(solution)/shard_map/ppermute | solution.py:246

commit v3 on v2

v3 whole, which is shorter than its diff:
```python
import functools

import jax
import jax.numpy as jnp
from jax import lax
from jax.experimental import pallas as pl
from jax.experimental.pallas import tpu as pltpu
from jax.sharding import PartitionSpec as P


F32 = jnp.float32
BF16 = jnp.bfloat16
VMEM = pl.BlockSpec(memory_space=pltpu.VMEM)
SMEM = pl.BlockSpec(memory_space=pltpu.SMEM)


def plain_shards(green_half, step_delta, chol_vectors, copy_counts, parents):
    per_group = green_half.shape[1]
    total_chol = lax.axis_size("chol") * chol_vectors.shape[0]
    orbitals = chol_vectors.shape[1]
    factor = -1.0 / total_chol**0.5
    all_parents = lax.all_gather(green_half, "pop", axis=1, tiled=True)
    my_parents = lax.dynamic_slice_in_dim(parents, lax.axis_index("pop") * per_group, per_group, 0)
    picked = jnp.take(all_parents, my_parents, axis=1)
    child_rows = (picked.astype(F32) + step_delta.astype(F32)).astype(BF16)
    cross = jnp.einsum(
        "iwm,gkm->wgik",
        lax.all_gather(child_rows, "chol", axis=0, tiled=True),
        chol_vectors,
        preferred_element_type=F32,
    )
    cross_low = cross.astype(BF16)
    trace_part = jnp.sum(cross_low.astype(F32) * jnp.swapaxes(cross, 2, 3), axis=(1, 2, 3))
    child_energy = lax.psum(trace_part, "chol") * (-0.125 / (total_chol * orbitals))
    forces = lax.psum_scatter(
        factor * jnp.einsum("wgik,gil->kwl", cross_low, chol_vectors, preferred_element_type=F32),
        "chol",
        scatter_dimension=0,
        tiled=True,
    )
    parent_slots = jnp.arange(all_parents.shape[1], dtype=jnp.int32)
    one_hot = (my_parents[:, None] == parent_slots[None, :]).astype(F32)
    spread_sum = jnp.einsum("kcl,cp->kpl", forces, one_hot, precision=lax.Precision.HIGHEST)
    summed = lax.psum_scatter(
        spread_sum.astype(BF16), "pop", scatter_dimension=1, tiled=True
    ).astype(F32)
    divisor = jnp.maximum(copy_counts, 1).astype(F32)
    return (summed / divisor[None, :, None]).astype(BF16), child_energy


def ring_device(n, place):
    return place * 2 if place < n // 2 else 2 * (n - 1 - place) + 1


def ring_pairs(n, step):
    return [(ring_device(n, q), ring_device(n, (q + step) % n)) for q in range(n)]


def block_at(n, offset):
    me = lax.axis_index("chol")
    place = jnp.where(lax.rem(me, 2) == 0, me // 2, n - 1 - me // 2)
    place = lax.rem(place + offset, n)
    return jnp.where(place < n // 2, 2 * place, 2 * (n - 1 - place) + 1)


def group_base(group, walkers, size):
    first = lax.axis_index("pop") * (walkers - size)
    return (walkers - size) - first if group == 0 else first


def message_rows(size, rows, width):
    return size * rows * (width // 128) + 8


def message_block(c, t, rows, width):
    first = (c * (width // 128) + t) * rows
    return slice(first, first + rows)


def children_kernel(parents_any, green_any, delta_any, other_ref, out0_ref, out1_ref, *scratch):
    parents_ref, green_ref, delta_ref, green_wide, delta_wide, other_wide, sems = scratch
    rows, walkers, width = green_ref.shape
    copies = [
        pltpu.make_async_copy(source, target, sems.at[k])
        for k, (source, target) in enumerate(
            ((parents_any, parents_ref), (green_any, green_ref), (delta_any, delta_ref))
        )
    ]
    for copy in copies:
        copy.start()
    mine = lax.axis_index("pop")
    blocks = [slice(t * 128, t * 128 + 128) for t in range(width // 128)]
    for t, lanes in enumerate(blocks):
        other_wide[t] = other_ref[:, :, lanes].astype(F32).reshape(rows * walkers, 128)
    for copy in copies:
        copy.wait()
    for t, lanes in enumerate(blocks):
        green_wide[t] = green_ref[:, :, lanes].astype(F32).reshape(rows * walkers, 128)
        delta_wide[t] = delta_ref[:, :, lanes].astype(F32).reshape(rows * walkers, 128)
    edge = jnp.where(mine == 0, 0, walkers - 1)
    for group, out_ref in enumerate((out0_ref, out1_ref)):
        size = out_ref.shape[0]
        base = group_base(group, walkers, size)
        for j in range(size):
            walker = base + j
            parent = parents_ref[mine * walkers + walker] - mine * walkers
            inside = jnp.logical_and(parent >= 0, parent < walkers)
            source = jnp.clip(parent, 0, walkers - 1)
            for t, lanes in enumerate(blocks):
                picked = green_wide[t, pl.ds(source, rows, stride=walkers), :]
                if group == 0:
                    outer = other_wide[t, pl.ds(edge, rows, stride=walkers), :]
                    picked = jnp.where(inside, picked, outer)
                change = delta_wide[t, pl.ds(walker, rows, stride=walkers), :]
                out_ref[j, :, lanes] = (picked + change).astype(BF16)


def make_children(size, parents, green, delta, other):
    rows, walkers, width = green.shape
    wide = pltpu.VMEM((width // 128, rows * walkers, 128), F32)
    return pl.pallas_call(
        children_kernel,
        out_shape=[
            jax.ShapeDtypeStruct((size, rows, width), BF16),
            jax.ShapeDtypeStruct((walkers - size, rows, width), BF16),
        ],
        in_specs=[pl.BlockSpec(memory_space=pltpu.HBM)] * 3 + [VMEM],
        out_specs=[VMEM, VMEM],
        scratch_shapes=[
            pltpu.SMEM(parents.shape, jnp.int32),
            pltpu.VMEM(green.shape, BF16),
            pltpu.VMEM(delta.shape, BF16),
            wide,
            wide,
            wide,
            pltpu.SemaphoreType.DMA((3,)),
        ],
        cost_estimate=pl.CostEstimate(
            flops=green.size, bytes_accessed=6 * green.size, transcendentals=0
        ),
        compiler_params=pltpu.CompilerParams(vmem_limit_bytes=8 << 20),
        name="children",
    )(parents, green, delta, other)


def force_kernel(factor, energy_scale, n, *refs):
    chol_ref, chunks, outs = refs[0], refs[1 : n + 1], refs[n + 1 : 2 * n + 1]
    child, low, force = refs[2 * n + 1 :]
    size, rows, width = chunks[0].shape
    vectors, orbitals, _ = chol_ref.shape
    starts = [pl.multiple_of(block_at(n, r) * rows, rows) for r in range(n)]
    for c in range(size):
        for r in range(n):
            child[c, pl.ds(starts[r], rows), :] = chunks[r][c]
    chol = chol_ref[...].reshape(vectors * orbitals, width)
    step = 2 if size % 2 == 0 else 1
    for c in range(0, size, step):
        cross = lax.dot_general(
            chol,
            child[c : c + step].reshape(step * orbitals, width),
            (((1,), (1,)), ((), ())),
            preferred_element_type=F32,
        ).astype(BF16)
        for d in range(step):
            for g in range(vectors):
                low[c + d, :, g * orbitals : (g + 1) * orbitals] = cross[
                    g * orbitals : (g + 1) * orbitals, d * orbitals : (d + 1) * orbitals
                ]
    force[...] = jnp.dot(
        low[...].reshape(size * orbitals, vectors * orbitals), chol, preferred_element_type=F32
    ).reshape(size, orbitals, width)
    sums = []
    for c in range(size):
        product = jnp.sum(child[c].astype(F32) * force[c], axis=0, keepdims=True)
        sums.append(sum(product[:, s : s + 128] for s in range(0, width, 128)))
    sums = jnp.concatenate(sums + [jnp.zeros((8 - size, 128), F32)], axis=0)
    energy = jnp.sum(sums, axis=1, keepdims=True) * energy_scale
    high = energy.astype(BF16).astype(F32)
    lane = lax.broadcasted_iota(jnp.int32, (8, 128), 1) - 2 * lax.axis_index("chol")
    tile = jnp.where(lane == 0, high, 0.0) + jnp.where(lane == 1, energy - high, 0.0)
    for r in range(n):
        for c in range(size):
            for t in range(width // 128):
                block = force[c, pl.ds(starts[r], rows), t * 128 : t * 128 + 128]
                outs[r][message_block(c, t, rows, width), :] = (block * factor).astype(
                    outs[r].dtype
                )
        outs[r][message_rows(size, rows, width) - 8 :, :] = tile.astype(outs[r].dtype)


def partial_forces(chol, chunks):
    n = len(chunks)
    size, rows, width = chunks[0].shape
    vectors, orbitals, _ = chol.shape
    total = n * vectors
    shape = (message_rows(size, rows, width), 128)
    return pl.pallas_call(
        functools.partial(
            force_kernel, -1.0 / total**0.5, -0.125 / (total * orbitals), n
        ),
        out_shape=[jax.ShapeDtypeStruct(shape, F32)]
        + [jax.ShapeDtypeStruct(shape, BF16)] * (n - 1),
        in_specs=[VMEM] * (1 + n),
        out_specs=[VMEM] * n,
        scratch_shapes=[
            pltpu.VMEM((size, orbitals, width), BF16),
            pltpu.VMEM((size, orbitals, vectors * orbitals), BF16),
            pltpu.VMEM((size, orbitals, width), F32),
        ],
        cost_estimate=pl.CostEstimate(
            flops=4 * size * orbitals * width * vectors * orbitals,
            bytes_accessed=2 * chol.size + 4 * size * orbitals * width,
            transcendentals=0,
        ),
        compiler_params=pltpu.CompilerParams(vmem_limit_bytes=16 << 20),
    )(chol, *chunks)


def parents_kernel(size, parents_ref, counts_ref, edge_ref, *refs):
    groups = (refs[0:3], refs[3:6])
    out_ref, energy_ref, total, spread = refs[6:]
    rows, walkers, width = out_ref.shape
    blocks = width // 128
    mine = lax.axis_index("pop")
    row = lax.broadcasted_iota(jnp.int32, (8, 128), 0)
    lane = lax.broadcasted_iota(jnp.int32, (8, 128), 1)
    energies = jnp.zeros((1, 128), F32)
    for group, (own, up, down) in enumerate(groups):
        base = group_base(group, walkers, size)
        for j in range(size):
            span = slice(j * blocks * rows, (j + 1) * blocks * rows)
            total[base + j] = own[span, :] + up[span, :].astype(F32) + down[span, :].astype(F32)
        tail = slice(size * blocks * rows, size * blocks * rows + 8)
        halves = own[tail, :] + up[tail, :].astype(F32) + down[tail, :].astype(F32)
        column = jnp.sum(halves, axis=1, keepdims=True)
        here = jnp.logical_and(lane == row + base, row < size)
        energies = energies + jnp.sum(jnp.where(here, column, 0.0), axis=0, keepdims=True)
    energy_ref[...] = energies[:, :walkers]
    edge = edge_ref[...].astype(F32)
    last = parents_ref.shape[0] - 1
    for p in range(walkers):
        parent = mine * walkers + p
        summed = jnp.zeros((blocks * rows, 128), F32)
        for c in range(max(p - 1, 0), min(p + 2, walkers)):
            hit = parents_ref[mine * walkers + c] == parent
            summed = summed + jnp.where(hit, total[c], 0.0)
        if p in (0, walkers - 1):
            child = parent + (1 if p else -1)
            valid = jnp.logical_and(child >= 0, child <= last)
            found = parents_ref[jnp.clip(child, 0, last)] == parent
            summed = summed + jnp.where(jnp.logical_and(valid, found), edge, 0.0)
        mean = summed * (1.0 / jnp.maximum(counts_ref[p], 1).astype(F32))
        for t in range(blocks):
            spread[t, pl.ds(p, rows, stride=walkers), :] = mean[t * rows : (t + 1) * rows, :]
    for t in range(blocks):
        block = spread[t].astype(BF16).reshape(rows, walkers, 128)
        out_ref[:, :, t * 128 : t * 128 + 128] = block


def parent_forces(shape, size, parents, counts, edge, group0, group1):
    rows, walkers, width = shape
    return pl.pallas_call(
        functools.partial(parents_kernel, size),
        out_shape=[
            jax.ShapeDtypeStruct(shape, BF16),
            jax.ShapeDtypeStruct((1, walkers), F32),
        ],
        in_specs=[SMEM, SMEM] + [VMEM] * 7,
        out_specs=[VMEM, VMEM],
        scratch_shapes=[
            pltpu.VMEM((walkers, rows * width // 128, 128), F32),
            pltpu.VMEM((width // 128, rows * walkers, 128), F32),
        ],
        cost_estimate=pl.CostEstimate(
            flops=6 * rows * walkers * width,
            bytes_accessed=10 * rows * walkers * width,
            transcendentals=0,
        ),
        compiler_params=pltpu.CompilerParams(vmem_limit_bytes=6 << 20),
        name="parents",
    )(parents, counts, edge, *group0, *group1)


def swap_cores(x):
    return lax.ppermute(x, "pop", [(0, 1), (1, 0)])


def add_low(own, received):
    return (own.astype(F32) + received.astype(F32)).astype(BF16)


def hop_order(n):
    half = n // 2
    order = [("gather", 1, 0, "up"), ("gather", 1, 1, "down")]
    for s in range(1, half):
        order += [("gather", s, 0, "down"), ("gather", s + 1, 0, "up")]
        order += [("gather", s, 1, "up"), ("gather", s + 1, 1, "down")]
    for s in range(1, half):
        order += [("sum", s, g, way) for g in (0, 1) for way in ("up", "down")]
    return order + [("sum", half, 0, "up"), ("sum", half, 1, "down")]


def ring_shards(green_half, step_delta, chol_vectors, copy_counts, parents):
    n = lax.axis_size("chol")
    rows, walkers, width = green_half.shape
    size = walkers // 2
    pairs = {"up": ring_pairs(n, 1), "down": ring_pairs(n, -1)}
    hops = ({"up": n // 2, "down": n // 2 - 1}, {"up": n // 2 - 1, "down": n // 2})

    def hop(x, key):
        return lax.ppermute(x, "chol", pairs[key[3]])

    other = swap_cores(green_half)
    own = make_children(size, parents, green_half, step_delta, other)
    chunks = [[own[g]] + [None] * (n - 1) for g in (0, 1)]
    parts = [None, None]
    arrived = [{}, {}]
    for key in hop_order(n):
        phase, s, g, way = key
        if phase == "gather":
            here, there = (n - s, (n - s + 1) % n) if way == "up" else (s, s - 1)
            chunks[g][here] = hop(chunks[g][there], key)
            continue
        if parts[g] is None:
            parts[g] = partial_forces(chol_vectors, chunks[g])
        left = hops[g][way] - s + 1
        send = parts[g][left if way == "up" else n - left]
        if s > 1:
            send = add_low(send, arrived[g][way])
        arrived[g][way] = hop(send, key)

    group0, group1 = [(parts[g][0], arrived[g]["up"], arrived[g]["down"]) for g in (0, 1)]
    per_walker = rows * width // 128
    at = (size - 1) * (1 - lax.axis_index("pop")) * per_walker
    own, up, down = [
        lax.dynamic_slice_in_dim(a, at, per_walker, 0).astype(F32) for a in group0
    ]
    edge = swap_cores((own + up + down).astype(BF16))
    parent_force, energy = parent_forces(
        green_half.shape, size, parents, copy_counts, edge, group0, group1
    )
    return parent_force, energy.reshape(walkers)


def on_ring(n, pops, rows, walkers):
    whole_tiles = rows % 16 == 0 and walkers % 8 == 0 and walkers <= 16
    return whole_tiles and n & (n - 1) == 0 and 4 <= n <= 64 and pops == 2


def shards(green_half, step_delta, chol_vectors, copy_counts, parents):
    rows, walkers, _ = green_half.shape
    if on_ring(lax.axis_size("chol"), lax.axis_size("pop"), rows, walkers):
        return ring_shards(green_half, step_delta, chol_vectors, copy_counts, parents)
    return plain_shards(green_half, step_delta, chol_vectors, copy_counts, parents)


def solution(mesh):
    placed = (
        P(("rep", "chol"), "pop", None),
        P(("rep", "chol"), "pop", None),
        P(("rep", "chol"), None, None),
        P(("rep", "pop")),
        P("rep"),
    )
    step = jax.shard_map(
        shards,
        mesh=mesh,
        in_specs=placed,
        out_specs=(P(("rep", "chol"), "pop", None), P(("rep", "pop"))),
        check_vma=False,
    )

    def run(green_half, step_delta, chol_vectors, copy_counts, parents):
        given = (green_half, step_delta, chol_vectors, copy_counts, parents)
        return step(*given)

    return run
```

time: 74.1 us -> 66.3 us (0.89)
  waiting for transfers between devices: 28.4 us -> 21.9 us
  starting transfers between devices: 33.8 us -> 32 us
  local copies, waits for them, and re-layouts: 2.56 us -> 3.98 us
    ppermute x28, waiting for transfers between devices: 26.5 us -> 20.6 us  [hop(): return lax.ppermute(x, 'chol', pairs[key[3]])]
    ppermute x3 -> x0, starting transfers between devices: 3.51 us -> none  [ring_shards(): lax.ppermute(energy, 'chol', [(i, i ^ span) for i in range(n)])]
    unnamed x12, local copies, waits for them, and re-layouts: 2.56 us -> 3.98 us
    ppermute x3 -> x0, waiting for transfers between devices: 1.32 us -> none  [ring_shards(): lax.ppermute(energy, 'chol', [(i, i ^ span) for i in range(n)])]
    ppermute x28, starting transfers between devices: 30.2 us -> 31.4 us  [hop(): return lax.ppermute(x, 'chol', pairs[key[3]])]
    ppermute x2, waiting for transfers between devices: 0.55 us -> 1.38 us  [swap_cores(): return lax.ppermute(x, 'pop', [(0, 1), (1, 0)])]
    pallas_call x5 -> x4, Pallas kernels: 7.35 us -> 7 us  [the longest x2 4.46 us: partial_forces(): pl.pallas_call(functools.partial(force_kernel, -1.0 / total ** 0.5, -0.12...]
  transfers between devices with their start and end apart: 33 -> 30, of which waited for: 18 -> 14; matrix products, arithmetic and copies ran while one was open for 1% -> 1% of each run, Pallas kernels for 7% -> 7%
where the time goes in v3:
time: 66.3 us; the launch traced here: 66.1 us
  starting transfers between devices  32 us (48%)
  waiting for transfers between devices  21.9 us (33%)
  Pallas kernels  7 us (11%)
  local copies, waits for them, and re-layouts  3.98 us (6%)
  between operations  0.75 us (1%)
    ppermute x28, starting transfers between devices, hop(): return lax.ppermute(x, 'chol', pairs[key[3]])  31.4 us
    ppermute x28, waiting for transfers between devices, hop(): return lax.ppermute(x, 'chol', pairs[key[3]])  20.6 us
    pallas_call x2, Pallas kernels, partial_forces(): pl.pallas_call(functools.partial(force_kernel, -1.0 / total ** 0.5, -0.12...  4.46 us
    unnamed x12, local copies, waits for them, and re-layouts  3.98 us
    pallas_call x1, Pallas kernels, parent_forces(): pl.pallas_call(functools.partial(parents_kernel, size), out_shape=[jax.Sh...  1.64 us
    ppermute x2, waiting for transfers between devices, swap_cores(): return lax.ppermute(x, 'pop', [(0, 1), (1, 0)])  1.38 us
  transfers between devices with their start and end apart: 30, of which 14 were waited for; matrix products, arithmetic and copies ran while one was open for 1% of the time, Pallas kernels for 7%

profile of v3, /device:TPU:0, one launch (start us, length us, event | category | flops | bytes accessed | tf_op | source)
XLA Modules:
  0.0 66.1 jit_solution(4496887100425423658)
XLA Ops:
  0.6 0.6 collective-permute-start
  1.2 1.4 %collective-permute-done.other_ref = bf16[16,8,1024]{2,1,0:T(8,128)(2,1)S(1)} collective-permute-done((bf16[16,8,1024]{2,1,0:T(8,128)(2,1)}, bf16[16,8,1024]{2,1,0:T(8,128)(2,1)S(1)}, u32[]{:S(2)}, u32[]{:S(2)}) %collective-permute-start) | collective-permute-done | bytes 262176 | tf_op jit(solution)/shard_map/ppermute | solution.py:285
  2.6 0.9 %copy-done = bf16[16,8,1024]{2,1,0:T(8,128)(2,1)S(1)} copy-done((bf16[16,8,1024]{2,1,0:T(8,128)(2,1)S(1)}, bf16[16,8,1024]{2,1,0:T(8,128)(2,1)}, u32[]{:S(2)}) %copy-start) | copy-done | bytes 262168
  3.5 0.9 %copy-done.1 = bf16[16,8,1024]{2,1,0:T(8,128)(2,1)S(1)} copy-done((bf16[16,8,1024]{2,1,0:T(8,128)(2,1)S(1)}, bf16[16,8,1024]{2,1,0:T(8,128)(2,1)}, u32[]{:S(2)}) %copy-start.1) | copy-done | bytes 262168
  4.5 0.7 copy-done.2
  5.1 0.9 %children.1 = (bf16[4,16,1024]{2,1,0:T(8,128)(2,1)S(1)}, bf16[4,16,1024]{2,1,0:T(8,128)(2,1)S(1)}) custom-call(s32[16]{0:T(128)S(1)} %copy-done.2, bf16[16,8,1024]{2,1,0:T(8,128)(2,1)S(1)} %copy-done, bf16[16,8,1024]{2,1,0:T(8,128)(2,1)S(1)} %copy-done.1, bf16[16,8,1024]{2,1,0:T(8,128)(2,1)S(1)} %collective-permute-done.other_ref), custom_call_target="tpu_custom_call" | custom-call | flops 131072 | bytes 786432 | tf_op jit(solution)/shard_map/children/pallas_call | solution.py:121
  6.0 2.9 %collective-permute-start.16 = (bf16[4,16,1024]{2,1,0:T(8,128)(2,1)S(1)}, bf16[4,16,1024]{2,1,0:T(8,128)(2,1)S(1)}, u32[]{:S(2)}, u32[]{:S(2)}) collective-permute-start(bf16[4,16,1024]{2,1,0:T(8,128)(2,1)S(1)} %get-tuple-element.31.refs_1_), channel_id=1, source_target_pairs={{0,2},{4,0},{8,4},{12,8},{14,12},{10,14},{6,10},{2,6},{1,3},{5,1},... | collective-permute-start | bytes 393224 | tf_op jit(solution)/shard_map/ppermute | solution.py:311
  8.9 0.2 collective-permute-start.4
  9.1 2.0 %collective-permute-start.20 = (bf16[4,16,1024]{2,1,0:T(8,128)(2,1)S(1)}, bf16[4,16,1024]{2,1,0:T(8,128)(2,1)S(1)}, u32[]{:S(2)}, u32[]{:S(2)}) collective-permute-start(bf16[4,16,1024]{2,1,0:T(8,128)(2,1)S(1)} %get-tuple-element.31.refs_1_), channel_id=1, source_target_pairs={{0,4},{4,8},{8,12},{12,14},{14,10},{10,6},{6,2},{2,0},{1,5},{5,9},... | collective-permute-start | bytes 393224 | tf_op jit(solution)/shard_map/ppermute | solution.py:311
  11.0 1.8 %collective-permute-done.16.refs_2_ = bf16[4,16,1024]{2,1,0:T(8,128)(2,1)S(1)} collective-permute-done((bf16[4,16,1024]{2,1,0:T(8,128)(2,1)S(1)}, bf16[4,16,1024]{2,1,0:T(8,128)(2,1)S(1)}, u32[]{:S(2)}, u32[]{:S(2)}) %collective-permute-start.16) | collective-permute-done | bytes 131104 | tf_op jit(solution)/shard_map/ppermute | solution.py:311
  12.8 1.7 %collective-permute-start.17 = (bf16[4,16,1024]{2,1,0:T(8,128)(2,1)S(1)}, bf16[4,16,1024]{2,1,0:T(8,128)(2,1)S(1)}, u32[]{:S(2)}, u32[]{:S(2)}) collective-permute-start(bf16[4,16,1024]{2,1,0:T(8,128)(2,1)S(1)} %collective-permute-done.16.refs_2_), channel_id=1, source_target_pairs={{0,2},{4,0},{8,4},{12,8},{14,12},{10,14},{6,10},{2,6},{1,3},{5,1},... | collective-permute-start | bytes 393224 | tf_op jit(solution)/shard_map/ppermute | solution.py:311
  14.5 1.6 %collective-permute-start.1 = (bf16[4,16,1024]{2,1,0:T(8,128)(2,1)S(1)}, bf16[4,16,1024]{2,1,0:T(8,128)(2,1)S(1)}, u32[]{:S(2)}, u32[]{:S(2)}) collective-permute-start(bf16[4,16,1024]{2,1,0:T(8,128)(2,1)S(1)} %get-tuple-element.22.refs_1_), channel_id=1, source_target_pairs={{0,2},{4,0},{8,4},{12,8},{14,12},{10,14},{6,10},{2,6},{1,3},{5,1},... | collective-permute-start | bytes 393224 | tf_op jit(solution)/shard_map/ppermute | solution.py:311
  16.0 0.0 collective-permute-done.4.refs_8_
  16.0 0.5 collective-permute-start.5
  16.5 0.5 collective-permute-done.20.refs_8_
  17.0 0.4 collective-permute-start.21
  17.4 1.8 %collective-permute-done.17.refs_3_ = bf16[4,16,1024]{2,1,0:T(8,128)(2,1)S(1)} collective-permute-done((bf16[4,16,1024]{2,1,0:T(8,128)(2,1)S(1)}, bf16[4,16,1024]{2,1,0:T(8,128)(2,1)S(1)}, u32[]{:S(2)}, u32[]{:S(2)}) %collective-permute-start.17) | collective-permute-done | bytes 131104 | tf_op jit(solution)/shard_map/ppermute | solution.py:311
  19.2 1.5 %collective-permute-start.18 = (bf16[4,16,1024]{2,1,0:T(8,128)(2,1)S(1)}, bf16[4,16,1024]{2,1,0:T(8,128)(2,1)S(1)}, u32[]{:S(2)}, u32[]{:S(2)}) collective-permute-start(bf16[4,16,1024]{2,1,0:T(8,128)(2,1)S(1)} %collective-permute-done.17.refs_3_), channel_id=1, source_target_pairs={{0,2},{4,0},{8,4},{12,8},{14,12},{10,14},{6,10},{2,6},{1,3},{5,1},... | collective-permute-start | bytes 393224 | tf_op jit(solution)/shard_map/ppermute | solution.py:311
  20.6 1.3 %collective-permute-done.1.refs_2_ = bf16[4,16,1024]{2,1,0:T(8,128)(2,1)S(1)} collective-permute-done((bf16[4,16,1024]{2,1,0:T(8,128)(2,1)S(1)}, bf16[4,16,1024]{2,1,0:T(8,128)(2,1)S(1)}, u32[]{:S(2)}, u32[]{:S(2)}) %collective-permute-start.1) | collective-permute-done | bytes 131104 | tf_op jit(solution)/shard_map/ppermute | solution.py:311
  22.0 1.5 %collective-permute-start.2 = (bf16[4,16,1024]{2,1,0:T(8,128)(2,1)S(1)}, bf16[4,16,1024]{2,1,0:T(8,128)(2,1)S(1)}, u32[]{:S(2)}, u32[]{:S(2)}) collective-permute-start(bf16[4,16,1024]{2,1,0:T(8,128)(2,1)S(1)} %collective-permute-done.1.refs_2_), channel_id=1, source_target_pairs={{0,2},{4,0},{8,4},{12,8},{14,12},{10,14},{6,10},{2,6},{1,3},{5,1},... | collective-permute-start | bytes 393224 | tf_op jit(solution)/shard_map/ppermute | solution.py:311
  23.5 0.0 collective-permute-done.5.refs_7_
  23.5 0.6 collective-permute-start.6
  24.0 0.0 collective-permute-done.21.refs_7_
  24.0 1.7 %collective-permute-start.22 = (bf16[4,16,1024]{2,1,0:T(8,128)(2,1)S(1)}, bf16[4,16,1024]{2,1,0:T(8,128)(2,1)S(1)}, u32[]{:S(2)}, u32[]{:S(2)}) collective-permute-start(bf16[4,16,1024]{2,1,0:T(8,128)(2,1)S(1)} %collective-permute-done.21.refs_7_), channel_id=1, source_target_pairs={{0,4},{4,8},{8,12},{12,14},{14,10},{10,6},{6,2},{2,0},{1,5},{5,9},... | collective-permute-start | bytes 393224 | tf_op jit(solution)/shard_map/ppermute | solution.py:311
  25.7 0.0 collective-permute-done.18.refs_4_
  25.7 0.7 %collective-permute-start.19 = (bf16[4,16,1024]{2,1,0:T(8,128)(2,1)S(1)}, bf16[4,16,1024]{2,1,0:T(8,128)(2,1)S(1)}, u32[]{:S(2)}, u32[]{:S(2)}) collective-permute-start(bf16[4,16,1024]{2,1,0:T(8,128)(2,1)S(1)} %collective-permute-done.18.refs_4_), channel_id=1, source_target_pairs={{0,2},{4,0},{8,4},{12,8},{14,12},{10,14},{6,10},{2,6},{1,3},{5,1},... | collective-permute-start | bytes 393224 | tf_op jit(solution)/shard_map/ppermute | solution.py:311
  26.4 2.0 %collective-permute-done.2.refs_3_ = bf16[4,16,1024]{2,1,0:T(8,128)(2,1)S(1)} collective-permute-done((bf16[4,16,1024]{2,1,0:T(8,128)(2,1)S(1)}, bf16[4,16,1024]{2,1,0:T(8,128)(2,1)S(1)}, u32[]{:S(2)}, u32[]{:S(2)}) %collective-permute-start.2) | collective-permute-done | bytes 131104 | tf_op jit(solution)/shard_map/ppermute | solution.py:311
  28.4 1.5 %collective-permute-start.3 = (bf16[4,16,1024]{2,1,0:T(8,128)(2,1)S(1)}, bf16[4,16,1024]{2,1,0:T(8,128)(2,1)S(1)}, u32[]{:S(2)}, u32[]{:S(2)}) collective-permute-start(bf16[4,16,1024]{2,1,0:T(8,128)(2,1)S(1)} %collective-permute-done.2.refs_3_), channel_id=1, source_target_pairs={{0,2},{4,0},{8,4},{12,8},{14,12},{10,14},{6,10},{2,6},{1,3},{5,1},... | collective-permute-start | bytes 393224 | tf_op jit(solution)/shard_map/ppermute | solution.py:311
  29.8 0.6 collective-permute-start.7
  30.4 0.8 %collective-permute-done.22.refs_6_ = bf16[4,16,1024]{2,1,0:T(8,128)(2,1)S(1)} collective-permute-done((bf16[4,16,1024]{2,1,0:T(8,128)(2,1)S(1)}, bf16[4,16,1024]{2,1,0:T(8,128)(2,1)S(1)}, u32[]{:S(2)}, u32[]{:S(2)}) %collective-permute-start.22) | collective-permute-done | bytes 131104 | tf_op jit(solution)/shard_map/ppermute | solution.py:311
  31.2 1.4 %copy-done.5 = bf16[6,128,1024]{2,1,0:T(8,128)(2,1)S(1)} copy-done((bf16[6,128,1024]{2,1,0:T(8,128)(2,1)S(1)}, bf16[6,128,1024]{2,1,0:T(8,128)(2,1)}, u32[]{:S(2)}) %copy-start.5) | copy-done | bytes 1572888
  32.7 2.2 %shard_map.69 = (f32[520,128]{1,0:T(8,128)S(1)}, bf16[520,128]{1,0:T(8,128)(2,1)S(1)}, bf16[520,128]{1,0:T(8,128)(2,1)S(1)}, bf16[520,128]{1,0:T(8,128)(2,1)S(1)...) custom-call(bf16[6,128,1024]{2,1,0:T(8,128)(2,1)S(1)} %copy-done.5, ...), custom_call_target="tpu_custom_call" | custom-call | flops 1610612736 | bytes 3670016 | tf_op jit(solution)/shard_map/pallas_call | solution.py:197
  34.9 1.6 %collective-permute-start.26 = (bf16[520,128]{1,0:T(8,128)(2,1)S(1)}, bf16[520,128]{1,0:T(8,128)(2,1)S(1)}, u32[]{:S(2)}, u32[]{:S(2)}) collective-permute-start(bf16[520,128]{1,0:T(8,128)(2,1)S(1)} %get-tuple-element.39), channel_id=1, source_target_pairs={{0,2},{4,0},{8,4},{12,8},{14,12},{10,14},{6,10},{2,6},{1,3},{5,1},... | collective-permute-start | bytes 399368 | tf_op jit(solution)/shard_map/ppermute | solution.py:311
  36.5 0.5 collective-permute-start.23
  36.9 0.0 collective-permute-done.3.refs_4_
  36.9 0.0 collective-permute-done.7.refs_5_
  36.9 2.2 %shard_map.68 = (f32[520,128]{1,0:T(8,128)S(1)}, bf16[520,128]{1,0:T(8,128)(2,1)S(1)}, bf16[520,128]{1,0:T(8,128)(2,1)S(1)}, bf16[520,128]{1,0:T(8,128)(2,1)S(1)...) custom-call(bf16[6,128,1024]{2,1,0:T(8,128)(2,1)S(1)} %copy-done.5, ...), custom_call_target="tpu_custom_call" | custom-call | flops 1610612736 | bytes 3670016 | tf_op jit(solution)/shard_map/pallas_call | solution.py:197
  39.1 0.9 %collective-permute-start.8 = (bf16[520,128]{1,0:T(8,128)(2,1)S(1)}, bf16[520,128]{1,0:T(8,128)(2,1)S(1)}, u32[]{:S(2)}, u32[]{:S(2)}) collective-permute-start(bf16[520,128]{1,0:T(8,128)(2,1)S(1)} %get-tuple-element.27), channel_id=1, source_target_pairs={{0,4},{4,8},{8,12},{12,14},{14,10},{10,6},{6,2},{2,0},{1,5},{5,9},... | collective-permute-start | bytes 399368 | tf_op jit(solution)/shard_map/ppermute | solution.py:311
  40.0 1.1 %collective-permute-start.12 = (bf16[520,128]{1,0:T(8,128)(2,1)S(1)}, bf16[520,128]{1,0:T(8,128)(2,1)S(1)}, u32[]{:S(2)}, u32[]{:S(2)}) collective-permute-start(bf16[520,128]{1,0:T(8,128)(2,1)S(1)} %get-tuple-element.30), channel_id=1, source_target_pairs={{0,2},{4,0},{8,4},{12,8},{14,12},{10,14},{6,10},{2,6},{1,3},{5,1},... | collective-permute-start | bytes 399368 | tf_op jit(solution)/shard_map/ppermute | solution.py:311
  41.2 0.1 collective-permute-done.26
  41.3 1.6 %collective-permute-start.27 = (bf16[520,128]{1,0:T(8,128)(2,1)S(1)}, bf16[520,128]{1,0:T(8,128)(2,1)S(1)}, u32[]{:S(2)}, u32[]{:S(2)}) collective-permute-start(bf16[520,128]{1,0:T(8,128)(2,1)S(1)} %add_convert_fusion.2), channel_id=1, source_target_pairs={{0,2},{4,0},{8,4},{12,8},{14,12},{10,14},{6,10},{2,6},{1,3},{5,1},... | collective-permute-start | bytes 399368 | tf_op jit(solution)/shard_map/ppermute | solution.py:311
  43.0 0.5 collective-permute-start.24
  43.5 1.8 %collective-permute-done.8 = bf16[520,128]{1,0:T(8,128)(2,1)S(1)} collective-permute-done((bf16[520,128]{1,0:T(8,128)(2,1)S(1)}, bf16[520,128]{1,0:T(8,128)(2,1)S(1)}, u32[]{:S(2)}, u32[]{:S(2)}) %collective-permute-start.8) | collective-permute-done | bytes 133152 | tf_op jit(solution)/shard_map/ppermute | solution.py:311
  45.3 0.0 copy-start.3
  45.3 0.0 copy-start.4
  45.3 0.8 %collective-permute-start.9 = (bf16[520,128]{1,0:T(8,128)(2,1)S(1)}, bf16[520,128]{1,0:T(8,128)(2,1)S(1)}, u32[]{:S(2)}, u32[]{:S(2)}) collective-permute-start(bf16[520,128]{1,0:T(8,128)(2,1)S(1)} %add_convert_fusion.9), channel_id=1, source_target_pairs={{0,4},{4,8},{8,12},{12,14},{14,10},{10,6},{6,2},{2,0},{1,5},{5,9},... | collective-permute-start | bytes 399368 | tf_op jit(solution)/shard_map/ppermute | solution.py:311
  46.1 0.3 collective-permute-done.12
  46.5 1.0 %collective-permute-start.13 = (bf16[520,128]{1,0:T(8,128)(2,1)S(1)}, bf16[520,128]{1,0:T(8,128)(2,1)S(1)}, u32[]{:S(2)}, u32[]{:S(2)}) collective-permute-start(bf16[520,128]{1,0:T(8,128)(2,1)S(1)} %add_convert_fusion.6), channel_id=1, source_target_pairs={{0,2},{4,0},{8,4},{12,8},{14,12},{10,14},{6,10},{2,6},{1,3},{5,1},... | collective-permute-start | bytes 399368 | tf_op jit(solution)/shard_map/ppermute | solution.py:311
  47.5 1.7 %collective-permute-done.27 = bf16[520,128]{1,0:T(8,128)(2,1)S(1)} collective-permute-done((bf16[520,128]{1,0:T(8,128)(2,1)S(1)}, bf16[520,128]{1,0:T(8,128)(2,1)S(1)}, u32[]{:S(2)}, u32[]{:S(2)}) %collective-permute-start.27) | collective-permute-done | bytes 133152 | tf_op jit(solution)/shard_map/ppermute | solution.py:311
  49.2 0.2 collective-permute-start.28
  49.5 1.9 %collective-permute-start.25 = (bf16[520,128]{1,0:T(8,128)(2,1)S(1)}, bf16[520,128]{1,0:T(8,128)(2,1)S(1)}, u32[]{:S(2)}, u32[]{:S(2)}) collective-permute-start(bf16[520,128]{1,0:T(8,128)(2,1)S(1)} %add_convert_fusion.3), channel_id=1, source_target_pairs={{0,4},{4,8},{8,12},{12,14},{14,10},{10,6},{6,2},{2,0},{1,5},{5,9},... | collective-permute-start | bytes 399368 | tf_op jit(solution)/shard_map/ppermute | solution.py:311
  51.4 0.0 collective-permute-done.9
  51.5 1.7 %collective-permute-start.10 = (bf16[520,128]{1,0:T(8,128)(2,1)S(1)}, bf16[520,128]{1,0:T(8,128)(2,1)S(1)}, u32[]{:S(2)}, u32[]{:S(2)}) collective-permute-start(bf16[520,128]{1,0:T(8,128)(2,1)S(1)} %add_convert_fusion.8), channel_id=1, source_target_pairs={{0,4},{4,8},{8,12},{12,14},{14,10},{10,6},{6,2},{2,0},{1,5},{5,9},... | collective-permute-start | bytes 399368 | tf_op jit(solution)/shard_map/ppermute | solution.py:311
  53.2 0.0 collective-permute-done.13
  53.2 0.4 collective-permute-start.14
  53.6 3.7 %collective-permute-done.10 = bf16[520,128]{1,0:T(8,128)(2,1)S(1)} collective-permute-done((bf16[520,128]{1,0:T(8,128)(2,1)S(1)}, bf16[520,128]{1,0:T(8,128)(2,1)S(1)}, u32[]{:S(2)}, u32[]{:S(2)}) %collective-permute-start.10) | collective-permute-done | bytes 133152 | tf_op jit(solution)/shard_map/ppermute | solution.py:311
  57.4 1.9 %collective-permute-start.11 = (bf16[520,128]{1,0:T(8,128)(2,1)S(1)}, bf16[520,128]{1,0:T(8,128)(2,1)S(1)}, u32[]{:S(2)}, u32[]{:S(2)}) collective-permute-start(bf16[520,128]{1,0:T(8,128)(2,1)S(1)} %add_convert_fusion.7), channel_id=1, source_target_pairs={{0,4},{4,8},{8,12},{12,14},{14,10},{10,6},{6,2},{2,0},{1,5},{5,9},... | collective-permute-start | bytes 399368 | tf_op jit(solution)/shard_map/ppermute | solution.py:311
  59.4 0.2 collective-permute-start.29
  59.6 2.9 %collective-permute-done.11.refs_1_ = bf16[520,128]{1,0:T(8,128)(2,1)S(1)} collective-permute-done((bf16[520,128]{1,0:T(8,128)(2,1)S(1)}, bf16[520,128]{1,0:T(8,128)(2,1)S(1)}, u32[]{:S(2)}, u32[]{:S(2)}) %collective-permute-start.11) | collective-permute-done | bytes 133152 | tf_op jit(solution)/shard_map/ppermute | solution.py:311
  62.5 0.1 collective-permute-start.15
  62.6 0.0 collective-permute-done.25.refs_4_
  62.6 1.9 %collective-permute-done.29.refs_5_ = bf16[520,128]{1,0:T(8,128)(2,1)S(1)} collective-permute-done((bf16[520,128]{1,0:T(8,128)(2,1)S(1)}, bf16[520,128]{1,0:T(8,128)(2,1)S(1)}, u32[]{:S(2)}, u32[]{:S(2)}) %collective-permute-start.29) | collective-permute-done | bytes 133152 | tf_op jit(solution)/shard_map/ppermute | solution.py:311
  64.4 0.0 collective-permute-done.15.edge_ref
  64.4 1.6 %parents.1 = (bf16[16,8,1024]{2,1,0:T(8,128)(2,1)}, f32[1,8]{1,0:T(1,128)}) custom-call(s32[16]{0:T(128)S(1)} %copy-done.3, s32[8]{0:T(128)S(1)} %copy-done.4, bf16[128,128]{1,0:T(8,128)(2,1)S(1)} %collective-permute-done.15.edge_ref, f32[520,128]{1,0:T(8,128)S(1)} %get-tuple-element.23.refs_0_, bf16[520,128]{1,0:T(8,128)(2,1)S(1)} %collective-permute-done.11.refs_1_, ...), custom_call_target="tpu_custom_call" | custom-call | flops 786432 | bytes 1310720 | tf_op jit(solution)/shard_map/parents/pallas_call | solution.py:262
  (23 shorter events, 0.4 us)
Async XLA Ops:
  0.6 1.9 %collective-permute-start = (bf16[16,8,1024]{2,1,0:T(8,128)(2,1)}, bf16[16,8,1024]{2,1,0:T(8,128)(2,1)S(1)}, u32[]{:S(2)}, u32[]{:S(2)}) collective-permute-start(bf16[16,8,1024]{2,1,0:T(8,128)(2,1)} %green_any.1), channel_id=1, source_target_pairs={{0,1},{1,0},{2,3},{3,2},{4,5},{5,4},{6,7},{7,6},{8,9},{9,8},{10,11... | collective-permute-start | bytes 786440 | tf_op jit(solution)/shard_map/ppermute | solution.py:285
  2.6 0.9 %copy-start = (bf16[16,8,1024]{2,1,0:T(8,128)(2,1)S(1)}, bf16[16,8,1024]{2,1,0:T(8,128)(2,1)}, u32[]{:S(2)}) copy-start(bf16[16,8,1024]{2,1,0:T(8,128)(2,1)} %green_any.1) | copy-start | bytes 786436
  3.5 0.9 %copy-start.1 = (bf16[16,8,1024]{2,1,0:T(8,128)(2,1)S(1)}, bf16[16,8,1024]{2,1,0:T(8,128)(2,1)}, u32[]{:S(2)}) copy-start(bf16[16,8,1024]{2,1,0:T(8,128)(2,1)} %delta_any.1) | copy-start | bytes 786436
  4.5 0.7 copy-start.2
  6.0 6.8 %collective-permute-start.16 = (bf16[4,16,1024]{2,1,0:T(8,128)(2,1)S(1)}, bf16[4,16,1024]{2,1,0:T(8,128)(2,1)S(1)}, u32[]{:S(2)}, u32[]{:S(2)}) collective-permute-start(bf16[4,16,1024]{2,1,0:T(8,128)(2,1)S(1)} %get-tuple-element.31.refs_1_), channel_id=1, source_target_pairs={{0,2},{4,0},{8,4},{12,8},{14,12},{10,14},{6,10},{2,6},{1,3},{5,1},... | collective-permute-start | bytes 393224 | tf_op jit(solution)/shard_map/ppermute | solution.py:311
  8.9 7.1 %collective-permute-start.4 = (bf16[4,16,1024]{2,1,0:T(8,128)(2,1)S(1)}, bf16[4,16,1024]{2,1,0:T(8,128)(2,1)S(1)}, u32[]{:S(2)}, u32[]{:S(2)}) collective-permute-start(bf16[4,16,1024]{2,1,0:T(8,128)(2,1)S(1)} %get-tuple-element.22.refs_1_), channel_id=1, source_target_pairs={{0,4},{4,8},{8,12},{12,14},{14,10},{10,6},{6,2},{2,0},{1,5},{5,9},... | collective-permute-start | bytes 393224 | tf_op jit(solution)/shard_map/ppermute | solution.py:311
  9.1 7.9 %collective-permute-start.20 = (bf16[4,16,1024]{2,1,0:T(8,128)(2,1)S(1)}, bf16[4,16,1024]{2,1,0:T(8,128)(2,1)S(1)}, u32[]{:S(2)}, u32[]{:S(2)}) collective-permute-start(bf16[4,16,1024]{2,1,0:T(8,128)(2,1)S(1)} %get-tuple-element.31.refs_1_), channel_id=1, source_target_pairs={{0,4},{4,8},{8,12},{12,14},{14,10},{10,6},{6,2},{2,0},{1,5},{5,9},... | collective-permute-start | bytes 393224 | tf_op jit(solution)/shard_map/ppermute | solution.py:311
  12.8 6.4 %collective-permute-start.17 = (bf16[4,16,1024]{2,1,0:T(8,128)(2,1)S(1)}, bf16[4,16,1024]{2,1,0:T(8,128)(2,1)S(1)}, u32[]{:S(2)}, u32[]{:S(2)}) collective-permute-start(bf16[4,16,1024]{2,1,0:T(8,128)(2,1)S(1)} %collective-permute-done.16.refs_2_), channel_id=1, source_target_pairs={{0,2},{4,0},{8,4},{12,8},{14,12},{10,14},{6,10},{2,6},{1,3},{5,1},... | collective-permute-start | bytes 393224 | tf_op jit(solution)/shard_map/ppermute | solution.py:311
  14.5 7.5 %collective-permute-start.1 = (bf16[4,16,1024]{2,1,0:T(8,128)(2,1)S(1)}, bf16[4,16,1024]{2,1,0:T(8,128)(2,1)S(1)}, u32[]{:S(2)}, u32[]{:S(2)}) collective-permute-start(bf16[4,16,1024]{2,1,0:T(8,128)(2,1)S(1)} %get-tuple-element.22.refs_1_), channel_id=1, source_target_pairs={{0,2},{4,0},{8,4},{12,8},{14,12},{10,14},{6,10},{2,6},{1,3},{5,1},... | collective-permute-start | bytes 393224 | tf_op jit(solution)/shard_map/ppermute | solution.py:311
  16.0 7.4 %collective-permute-start.5 = (bf16[4,16,1024]{2,1,0:T(8,128)(2,1)S(1)}, bf16[4,16,1024]{2,1,0:T(8,128)(2,1)S(1)}, u32[]{:S(2)}, u32[]{:S(2)}) collective-permute-start(bf16[4,16,1024]{2,1,0:T(8,128)(2,1)S(1)} %collective-permute-done.4.refs_8_), channel_id=1, source_target_pairs={{0,4},{4,8},{8,12},{12,14},{14,10},{10,6},{6,2},{2,0},{1,5},{5,9},... | collective-permute-start | bytes 393224 | tf_op jit(solution)/shard_map/ppermute | solution.py:311
  17.0 7.0 %collective-permute-start.21 = (bf16[4,16,1024]{2,1,0:T(8,128)(2,1)S(1)}, bf16[4,16,1024]{2,1,0:T(8,128)(2,1)S(1)}, u32[]{:S(2)}, u32[]{:S(2)}) collective-permute-start(bf16[4,16,1024]{2,1,0:T(8,128)(2,1)S(1)} %collective-permute-done.20.refs_8_), channel_id=1, source_target_pairs={{0,4},{4,8},{8,12},{12,14},{14,10},{10,6},{6,2},{2,0},{1,5},{5,9},... | collective-permute-start | bytes 393224 | tf_op jit(solution)/shard_map/ppermute | solution.py:311
  19.2 6.5 %collective-permute-start.18 = (bf16[4,16,1024]{2,1,0:T(8,128)(2,1)S(1)}, bf16[4,16,1024]{2,1,0:T(8,128)(2,1)S(1)}, u32[]{:S(2)}, u32[]{:S(2)}) collective-permute-start(bf16[4,16,1024]{2,1,0:T(8,128)(2,1)S(1)} %collective-permute-done.17.refs_3_), channel_id=1, source_target_pairs={{0,2},{4,0},{8,4},{12,8},{14,12},{10,14},{6,10},{2,6},{1,3},{5,1},... | collective-permute-start | bytes 393224 | tf_op jit(solution)/shard_map/ppermute | solution.py:311
  22.0 6.4 %collective-permute-start.2 = (bf16[4,16,1024]{2,1,0:T(8,128)(2,1)S(1)}, bf16[4,16,1024]{2,1,0:T(8,128)(2,1)S(1)}, u32[]{:S(2)}, u32[]{:S(2)}) collective-permute-start(bf16[4,16,1024]{2,1,0:T(8,128)(2,1)S(1)} %collective-permute-done.1.refs_2_), channel_id=1, source_target_pairs={{0,2},{4,0},{8,4},{12,8},{14,12},{10,14},{6,10},{2,6},{1,3},{5,1},... | collective-permute-start | bytes 393224 | tf_op jit(solution)/shard_map/ppermute | solution.py:311
  23.5 6.4 %collective-permute-start.6 = (bf16[4,16,1024]{2,1,0:T(8,128)(2,1)S(1)}, bf16[4,16,1024]{2,1,0:T(8,128)(2,1)S(1)}, u32[]{:S(2)}, u32[]{:S(2)}) collective-permute-start(bf16[4,16,1024]{2,1,0:T(8,128)(2,1)S(1)} %collective-permute-done.5.refs_7_), channel_id=1, source_target_pairs={{0,4},{4,8},{8,12},{12,14},{14,10},{10,6},{6,2},{2,0},{1,5},{5,9},... | collective-permute-start | bytes 393224 | tf_op jit(solution)/shard_map/ppermute | solution.py:311
  24.0 7.2 %collective-permute-start.22 = (bf16[4,16,1024]{2,1,0:T(8,128)(2,1)S(1)}, bf16[4,16,1024]{2,1,0:T(8,128)(2,1)S(1)}, u32[]{:S(2)}, u32[]{:S(2)}) collective-permute-start(bf16[4,16,1024]{2,1,0:T(8,128)(2,1)S(1)} %collective-permute-done.21.refs_7_), channel_id=1, source_target_pairs={{0,4},{4,8},{8,12},{12,14},{14,10},{10,6},{6,2},{2,0},{1,5},{5,9},... | collective-permute-start | bytes 393224 | tf_op jit(solution)/shard_map/ppermute | solution.py:311
  25.7 5.6 %collective-permute-start.19 = (bf16[4,16,1024]{2,1,0:T(8,128)(2,1)S(1)}, bf16[4,16,1024]{2,1,0:T(8,128)(2,1)S(1)}, u32[]{:S(2)}, u32[]{:S(2)}) collective-permute-start(bf16[4,16,1024]{2,1,0:T(8,128)(2,1)S(1)} %collective-permute-done.18.refs_4_), channel_id=1, source_target_pairs={{0,2},{4,0},{8,4},{12,8},{14,12},{10,14},{6,10},{2,6},{1,3},{5,1},... | collective-permute-start | bytes 393224 | tf_op jit(solution)/shard_map/ppermute | solution.py:311
  28.4 8.6 %collective-permute-start.3 = (bf16[4,16,1024]{2,1,0:T(8,128)(2,1)S(1)}, bf16[4,16,1024]{2,1,0:T(8,128)(2,1)S(1)}, u32[]{:S(2)}, u32[]{:S(2)}) collective-permute-start(bf16[4,16,1024]{2,1,0:T(8,128)(2,1)S(1)} %collective-permute-done.2.refs_3_), channel_id=1, source_target_pairs={{0,2},{4,0},{8,4},{12,8},{14,12},{10,14},{6,10},{2,6},{1,3},{5,1},... | collective-permute-start | bytes 393224 | tf_op jit(solution)/shard_map/ppermute | solution.py:311
  29.8 7.1 %collective-permute-start.7 = (bf16[4,16,1024]{2,1,0:T(8,128)(2,1)S(1)}, bf16[4,16,1024]{2,1,0:T(8,128)(2,1)S(1)}, u32[]{:S(2)}, u32[]{:S(2)}) collective-permute-start(bf16[4,16,1024]{2,1,0:T(8,128)(2,1)S(1)} %collective-permute-done.6.refs_6_), channel_id=1, source_target_pairs={{0,4},{4,8},{8,12},{12,14},{14,10},{10,6},{6,2},{2,0},{1,5},{5,9},... | collective-permute-start | bytes 393224 | tf_op jit(solution)/shard_map/ppermute | solution.py:311
  31.2 1.4 %copy-start.5 = (bf16[6,128,1024]{2,1,0:T(8,128)(2,1)S(1)}, bf16[6,128,1024]{2,1,0:T(8,128)(2,1)}, u32[]{:S(2)}) copy-start(bf16[6,128,1024]{2,1,0:T(8,128)(2,1)} %refs_0_.3) | copy-start | bytes 4718596
  34.9 6.4 %collective-permute-start.26 = (bf16[520,128]{1,0:T(8,128)(2,1)S(1)}, bf16[520,128]{1,0:T(8,128)(2,1)S(1)}, u32[]{:S(2)}, u32[]{:S(2)}) collective-permute-start(bf16[520,128]{1,0:T(8,128)(2,1)S(1)} %get-tuple-element.39), channel_id=1, source_target_pairs={{0,2},{4,0},{8,4},{12,8},{14,12},{10,14},{6,10},{2,6},{1,3},{5,1},... | collective-permute-start | bytes 399368 | tf_op jit(solution)/shard_map/ppermute | solution.py:311
  36.5 6.5 %collective-permute-start.23 = (bf16[520,128]{1,0:T(8,128)(2,1)S(1)}, bf16[520,128]{1,0:T(8,128)(2,1)S(1)}, u32[]{:S(2)}, u32[]{:S(2)}) collective-permute-start(bf16[520,128]{1,0:T(8,128)(2,1)S(1)} %get-tuple-element.35), channel_id=1, source_target_pairs={{0,4},{4,8},{8,12},{12,14},{14,10},{10,6},{6,2},{2,0},{1,5},{5,9},... | collective-permute-start | bytes 399368 | tf_op jit(solution)/shard_map/ppermute | solution.py:311
  39.1 6.1 %collective-permute-start.8 = (bf16[520,128]{1,0:T(8,128)(2,1)S(1)}, bf16[520,128]{1,0:T(8,128)(2,1)S(1)}, u32[]{:S(2)}, u32[]{:S(2)}) collective-permute-start(bf16[520,128]{1,0:T(8,128)(2,1)S(1)} %get-tuple-element.27), channel_id=1, source_target_pairs={{0,4},{4,8},{8,12},{12,14},{14,10},{10,6},{6,2},{2,0},{1,5},{5,9},... | collective-permute-start | bytes 399368 | tf_op jit(solution)/shard_map/ppermute | solution.py:311
  40.0 6.4 %collective-permute-start.12 = (bf16[520,128]{1,0:T(8,128)(2,1)S(1)}, bf16[520,128]{1,0:T(8,128)(2,1)S(1)}, u32[]{:S(2)}, u32[]{:S(2)}) collective-permute-start(bf16[520,128]{1,0:T(8,128)(2,1)S(1)} %get-tuple-element.30), channel_id=1, source_target_pairs={{0,2},{4,0},{8,4},{12,8},{14,12},{10,14},{6,10},{2,6},{1,3},{5,1},... | collective-permute-start | bytes 399368 | tf_op jit(solution)/shard_map/ppermute | solution.py:311
  41.3 7.9 %collective-permute-start.27 = (bf16[520,128]{1,0:T(8,128)(2,1)S(1)}, bf16[520,128]{1,0:T(8,128)(2,1)S(1)}, u32[]{:S(2)}, u32[]{:S(2)}) collective-permute-start(bf16[520,128]{1,0:T(8,128)(2,1)S(1)} %add_convert_fusion.2), channel_id=1, source_target_pairs={{0,2},{4,0},{8,4},{12,8},{14,12},{10,14},{6,10},{2,6},{1,3},{5,1},... | collective-permute-start | bytes 399368 | tf_op jit(solution)/shard_map/ppermute | solution.py:311
  43.0 6.4 %collective-permute-start.24 = (bf16[520,128]{1,0:T(8,128)(2,1)S(1)}, bf16[520,128]{1,0:T(8,128)(2,1)S(1)}, u32[]{:S(2)}, u32[]{:S(2)}) collective-permute-start(bf16[520,128]{1,0:T(8,128)(2,1)S(1)} %add_convert_fusion.4), channel_id=1, source_target_pairs={{0,4},{4,8},{8,12},{12,14},{14,10},{10,6},{6,2},{2,0},{1,5},{5,9},... | collective-permute-start | bytes 399368 | tf_op jit(solution)/shard_map/ppermute | solution.py:311
  45.3 19.1 %copy-start.3 = (s32[16]{0:T(128)S(1)}, s32[16]{0:T(128)}, u32[]{:S(2)}) copy-start(s32[16]{0:T(128)} %parents_ref.1) | copy-start | bytes 196
  45.3 19.1 %copy-start.4 = (s32[8]{0:T(128)S(1)}, s32[8]{0:T(128)}, u32[]{:S(2)}) copy-start(s32[8]{0:T(128)} %counts_ref.1) | copy-start | bytes 100
  45.3 6.1 %collective-permute-start.9 = (bf16[520,128]{1,0:T(8,128)(2,1)S(1)}, bf16[520,128]{1,0:T(8,128)(2,1)S(1)}, u32[]{:S(2)}, u32[]{:S(2)}) collective-permute-start(bf16[520,128]{1,0:T(8,128)(2,1)S(1)} %add_convert_fusion.9), channel_id=1, source_target_pairs={{0,4},{4,8},{8,12},{12,14},{14,10},{10,6},{6,2},{2,0},{1,5},{5,9},... | collective-permute-start | bytes 399368 | tf_op jit(solution)/shard_map/ppermute | solution.py:311
  46.5 6.7 %collective-permute-start.13 = (bf16[520,128]{1,0:T(8,128)(2,1)S(1)}, bf16[520,128]{1,0:T(8,128)(2,1)S(1)}, u32[]{:S(2)}, u32[]{:S(2)}) collective-permute-start(bf16[520,128]{1,0:T(8,128)(2,1)S(1)} %add_convert_fusion.6), channel_id=1, source_target_pairs={{0,2},{4,0},{8,4},{12,8},{14,12},{10,14},{6,10},{2,6},{1,3},{5,1},... | collective-permute-start | bytes 399368 | tf_op jit(solution)/shard_map/ppermute | solution.py:311
  49.2 10.1 %collective-permute-start.28 = (bf16[520,128]{1,0:T(8,128)(2,1)S(1)}, bf16[520,128]{1,0:T(8,128)(2,1)S(1)}, u32[]{:S(2)}, u32[]{:S(2)}) collective-permute-start(bf16[520,128]{1,0:T(8,128)(2,1)S(1)} %add_convert_fusion.1), channel_id=1, source_target_pairs={{0,2},{4,0},{8,4},{12,8},{14,12},{10,14},{6,10},{2,6},{1,3},{5,1},... | collective-permute-start | bytes 399368 | tf_op jit(solution)/shard_map/ppermute | solution.py:311
  49.5 13.1 %collective-permute-start.25 = (bf16[520,128]{1,0:T(8,128)(2,1)S(1)}, bf16[520,128]{1,0:T(8,128)(2,1)S(1)}, u32[]{:S(2)}, u32[]{:S(2)}) collective-permute-start(bf16[520,128]{1,0:T(8,128)(2,1)S(1)} %add_convert_fusion.3), channel_id=1, source_target_pairs={{0,4},{4,8},{8,12},{12,14},{14,10},{10,6},{6,2},{2,0},{1,5},{5,9},... | collective-permute-start | bytes 399368 | tf_op jit(solution)/shard_map/ppermute | solution.py:311
  51.5 5.9 %collective-permute-start.10 = (bf16[520,128]{1,0:T(8,128)(2,1)S(1)}, bf16[520,128]{1,0:T(8,128)(2,1)S(1)}, u32[]{:S(2)}, u32[]{:S(2)}) collective-permute-start(bf16[520,128]{1,0:T(8,128)(2,1)S(1)} %add_convert_fusion.8), channel_id=1, source_target_pairs={{0,4},{4,8},{8,12},{12,14},{14,10},{10,6},{6,2},{2,0},{1,5},{5,9},... | collective-permute-start | bytes 399368 | tf_op jit(solution)/shard_map/ppermute | solution.py:311
  53.2 6.4 %collective-permute-start.14 = (bf16[520,128]{1,0:T(8,128)(2,1)S(1)}, bf16[520,128]{1,0:T(8,128)(2,1)S(1)}, u32[]{:S(2)}, u32[]{:S(2)}) collective-permute-start(bf16[520,128]{1,0:T(8,128)(2,1)S(1)} %add_convert_fusion.5), channel_id=1, source_target_pairs={{0,2},{4,0},{8,4},{12,8},{14,12},{10,14},{6,10},{2,6},{1,3},{5,1},... | collective-permute-start | bytes 399368 | tf_op jit(solution)/shard_map/ppermute | solution.py:311
  57.4 5.0 %collective-permute-start.11 = (bf16[520,128]{1,0:T(8,128)(2,1)S(1)}, bf16[520,128]{1,0:T(8,128)(2,1)S(1)}, u32[]{:S(2)}, u32[]{:S(2)}) collective-permute-start(bf16[520,128]{1,0:T(8,128)(2,1)S(1)} %add_convert_fusion.7), channel_id=1, source_target_pairs={{0,4},{4,8},{8,12},{12,14},{14,10},{10,6},{6,2},{2,0},{1,5},{5,9},... | collective-permute-start | bytes 399368 | tf_op jit(solution)/shard_map/ppermute | solution.py:311
  59.4 5.0 %collective-permute-start.29 = (bf16[520,128]{1,0:T(8,128)(2,1)S(1)}, bf16[520,128]{1,0:T(8,128)(2,1)S(1)}, u32[]{:S(2)}, u32[]{:S(2)}) collective-permute-start(bf16[520,128]{1,0:T(8,128)(2,1)S(1)} %add_convert_fusion), channel_id=1, source_target_pairs={{0,2},{4,0},{8,4},{12,8},{14,12},{10,14},{6,10},{2,6},{1,3},{5,1},... | collective-permute-start | bytes 399368 | tf_op jit(solution)/shard_map/ppermute | solution.py:311
  62.5 2.0 %collective-permute-start.15 = (bf16[128,128]{1,0:T(8,128)(2,1)S(1)}, bf16[128,128]{1,0:T(8,128)(2,1)S(1)}, u32[]{:S(2)}, u32[]{:S(2)}) collective-permute-start(bf16[128,128]{1,0:T(8,128)(2,1)S(1)} %add_convert_fusion.10), channel_id=1, source_target_pairs={{0,1},{1,0},{2,3},{3,2},{4,5},{5,4},{6,7},{7,6},{8,9},{9,8},{10,11... | collective-permute-start | bytes 98312 | tf_op jit(solution)/shard_map/ppermute | solution.py:285

commit v4 on v3

--- a/solution.py
+++ b/solution.py
@@ -77,70 +77,120 @@
     return slice(first, first + rows)
 
 
-def children_kernel(parents_any, green_any, delta_any, other_ref, out0_ref, out1_ref, *scratch):
-    parents_ref, green_ref, delta_ref, green_wide, delta_wide, other_wide, sems = scratch
+def children_kernel(parents_any, green_any, delta_any, chol_any, *refs):
+    out0_ref, out1_ref, chol_ref, change_ref, outside_ref = refs[:5]
+    parents_ref, green_ref, delta_ref, green_wide, delta_wide, sems = refs[5:]
     rows, walkers, width = green_ref.shape
     copies = [
         pltpu.make_async_copy(source, target, sems.at[k])
         for k, (source, target) in enumerate(
-            ((parents_any, parents_ref), (green_any, green_ref), (delta_any, delta_ref))
+            (
+                (parents_any, parents_ref),
+                (green_any, green_ref),
+                (delta_any, delta_ref),
+                (chol_any, chol_ref),
+            )
         )
     ]
     for copy in copies:
         copy.start()
+    for copy in copies[:3]:
+        copy.wait()
     mine = lax.axis_index("pop")
     blocks = [slice(t * 128, t * 128 + 128) for t in range(width // 128)]
     for t, lanes in enumerate(blocks):
-        other_wide[t] = other_ref[:, :, lanes].astype(F32).reshape(rows * walkers, 128)
-    for copy in copies:
-        copy.wait()
-    for t, lanes in enumerate(blocks):
         green_wide[t] = green_ref[:, :, lanes].astype(F32).reshape(rows * walkers, 128)
         delta_wide[t] = delta_ref[:, :, lanes].astype(F32).reshape(rows * walkers, 128)
-    edge = jnp.where(mine == 0, 0, walkers - 1)
+
+    def local_parent(walker):
+        return parents_ref[mine * walkers + walker] - mine * walkers
+
     for group, out_ref in enumerate((out0_ref, out1_ref)):
         size = out_ref.shape[0]
         base = group_base(group, walkers, size)
         for j in range(size):
             walker = base + j
-            parent = parents_ref[mine * walkers + walker] - mine * walkers
-            inside = jnp.logical_and(parent >= 0, parent < walkers)
-            source = jnp.clip(parent, 0, walkers - 1)
+            source = jnp.clip(local_parent(walker), 0, walkers - 1)
             for t, lanes in enumerate(blocks):
                 picked = green_wide[t, pl.ds(source, rows, stride=walkers), :]
-                if group == 0:
-                    outer = other_wide[t, pl.ds(edge, rows, stride=walkers), :]
-                    picked = jnp.where(inside, picked, outer)
                 change = delta_wide[t, pl.ds(walker, rows, stride=walkers), :]
                 out_ref[j, :, lanes] = (picked + change).astype(BF16)
-
-
-def make_children(size, parents, green, delta, other):
+    child = edge_walker(walkers)
+    for t, lanes in enumerate(blocks):
+        change_ref[:, lanes] = delta_wide[t, pl.ds(child, rows, stride=walkers), :]
+    parent = local_parent(child)
+    outside = jnp.where(jnp.logical_or(parent < 0, parent >= walkers), 1.0, 0.0)
+    outside_ref[...] = jnp.full((rows, 128), outside, F32)
+    copies[3].wait()
+
+
+def edge_walker(walkers):
+    return jnp.where(lax.axis_index("pop") == 0, walkers - 1, 0)
+
+
+def edge_kernel(chunk_ref, change_ref, outside_ref, other_ref, out_ref, other_wide):
+    size, rows, width = out_ref.shape
+    walkers = other_ref.shape[1]
+    j = jnp.where(lax.axis_index("pop") == 0, size - 1, 0)
+    row = walkers - 1 - edge_walker(walkers)
+    outside = outside_ref[...] > 0.5
+    out_ref[...] = chunk_ref[...]
+    for t in range(width // 128):
+        lanes = slice(t * 128, t * 128 + 128)
+        other_wide[t] = other_ref[:, :, lanes].astype(F32).reshape(rows * walkers, 128)
+        picked = other_wide[t, pl.ds(row, rows, stride=walkers), :]
+        moved = picked + change_ref[:, lanes]
+        kept = chunk_ref[j, :, lanes].astype(F32)
+        out_ref[j, :, lanes] = jnp.where(outside, moved, kept).astype(BF16)
+
+
+def make_children(size, parents, green, delta, chol):
     rows, walkers, width = green.shape
     wide = pltpu.VMEM((width // 128, rows * walkers, 128), F32)
+    here = [
+        pltpu.with_memory_space_constraint(a, pltpu.HBM) for a in (parents, green, delta, chol)
+    ]
     return pl.pallas_call(
         children_kernel,
         out_shape=[
             jax.ShapeDtypeStruct((size, rows, width), BF16),
             jax.ShapeDtypeStruct((walkers - size, rows, width), BF16),
+            jax.ShapeDtypeStruct(chol.shape, BF16),
+            jax.ShapeDtypeStruct((rows, width), F32),
+            jax.ShapeDtypeStruct((rows, 128), F32),
         ],
-        in_specs=[pl.BlockSpec(memory_space=pltpu.HBM)] * 3 + [VMEM],
-        out_specs=[VMEM, VMEM],
+        in_specs=[pl.BlockSpec(memory_space=pltpu.HBM)] * 4,
+        out_specs=[VMEM] * 5,
         scratch_shapes=[
             pltpu.SMEM(parents.shape, jnp.int32),
             pltpu.VMEM(green.shape, BF16),
             pltpu.VMEM(delta.shape, BF16),
             wide,
             wide,
-            wide,
-            pltpu.SemaphoreType.DMA((3,)),
+            pltpu.SemaphoreType.DMA((4,)),
         ],
         cost_estimate=pl.CostEstimate(
             flops=green.size, bytes_accessed=6 * green.size, transcendentals=0
         ),
         compiler_params=pltpu.CompilerParams(vmem_limit_bytes=8 << 20),
         name="children",
-    )(parents, green, delta, other)
+    )(*here)
+
+
+def finish_edge(chunk, change, outside, other):
+    rows, walkers, width = other.shape
+    return pl.pallas_call(
+        edge_kernel,
+        out_shape=jax.ShapeDtypeStruct(chunk.shape, BF16),
+        in_specs=[VMEM] * 4,
+        out_specs=VMEM,
+        scratch_shapes=[pltpu.VMEM((width // 128, rows * walkers, 128), F32)],
+        cost_estimate=pl.CostEstimate(
+            flops=other.size, bytes_accessed=4 * other.size, transcendentals=0
+        ),
+        compiler_params=pltpu.CompilerParams(vmem_limit_bytes=4 << 20),
+        name="edge",
+    )(chunk, change, outside, other)
 
 
 def force_kernel(factor, energy_scale, n, *refs):
@@ -291,13 +341,15 @@
 
 def hop_order(n):
     half = n // 2
-    order = [("gather", 1, 0, "up"), ("gather", 1, 1, "down")]
+    order = []
     for s in range(1, half):
-        order += [("gather", s, 0, "down"), ("gather", s + 1, 0, "up")]
-        order += [("gather", s, 1, "up"), ("gather", s + 1, 1, "down")]
+        order += [("gather", s, g, way) for g in (0, 1) for way in ("up", "down")]
+    order += [("gather", half, 0, "up"), ("gather", half, 1, "down")]
+    order += [("sum", 1, 0, "up"), ("sum", 1, 1, "down")]
     for s in range(1, half):
-        order += [("sum", s, g, way) for g in (0, 1) for way in ("up", "down")]
-    return order + [("sum", half, 0, "up"), ("sum", half, 1, "down")]
+        order += [("sum", s + 1, 0, "up"), ("sum", s, 0, "down")]
+        order += [("sum", s, 1, "up"), ("sum", s + 1, 1, "down")]
+    return order
 
 
 def ring_shards(green_half, step_delta, chol_vectors, copy_counts, parents):
@@ -311,7 +363,10 @@
         return lax.ppermute(x, "chol", pairs[key[3]])
 
     other = swap_cores(green_half)
-    own = make_children(size, parents, green_half, step_delta, other)
+    *own, chol, change, outside = make_children(
+        size, parents, green_half, step_delta, chol_vectors
+    )
+    own[0] = finish_edge(own[0], change, outside, other)
     chunks = [[own[g]] + [None] * (n - 1) for g in (0, 1)]
     parts = [None, None]
     arrived = [{}, {}]
@@ -322,7 +377,7 @@
             chunks[g][here] = hop(chunks[g][there], key)
             continue
         if parts[g] is None:
-            parts[g] = partial_forces(chol_vectors, chunks[g])
+            parts[g] = partial_forces(chol, chunks[g])
         left = hops[g][way] - s + 1
         send = parts[g][left if way == "up" else n - left]
         if s > 1:

time: 66.3 us -> 70.7 us (1.066)
  waiting for transfers between devices: 21.9 us -> 28.2 us
  local copies, waits for them, and re-layouts: 3.98 us -> 0.02 us
  Pallas kernels: 7 us -> 8.75 us
  other arithmetic: 0.4 us -> 1.31 us
    ppermute x28, waiting for transfers between devices: 20.6 us -> 27 us  [hop(): return lax.ppermute(x, 'chol', pairs[key[3]])]
    unnamed x12 -> x6, local copies, waits for them, and re-layouts: 3.98 us -> 0.02 us
    convert_element_type x10, other arithmetic: 0.38 us -> 1.29 us  [add_low(): return (own.astype(F32) + received.astype(F32)).astype(BF16)]
    pallas_call x2, Pallas kernels: 4.46 us -> 5.36 us  [partial_forces(): pl.pallas_call(functools.partial(force_kernel, -1.0 / total ** 0.5, -0.12...]
    pallas_call x1, Pallas kernels: 0.91 us -> 1.65 us  [make_children(): pl.pallas_call(children_kernel, out_shape=[jax.ShapeDtypeStruct((size, ro...]
  transfers between devices with their start and end apart: 30 -> 30, of which waited for: 14 -> 14; matrix products, arithmetic and copies ran while one was open for 1% -> 2% of each run, Pallas kernels for 7% -> 8%
where the time goes in v4:
time: 70.7 us; the launch traced here: 70.5 us
  starting transfers between devices  31.4 us (44%)
  waiting for transfers between devices  28.2 us (40%)
  Pallas kernels  8.75 us (12%)
  other arithmetic  1.31 us (2%)
  between operations  0.81 us (1%)
    ppermute x28, starting transfers between devices, hop(): return lax.ppermute(x, 'chol', pairs[key[3]])  31.4 us
    ppermute x28, waiting for transfers between devices, hop(): return lax.ppermute(x, 'chol', pairs[key[3]])  27 us
    pallas_call x2, Pallas kernels, partial_forces(): pl.pallas_call(functools.partial(force_kernel, -1.0 / total ** 0.5, -0.12...  5.36 us
    pallas_call x1, Pallas kernels, make_children(): pl.pallas_call(children_kernel, out_shape=[jax.ShapeDtypeStruct((size, ro...  1.65 us
    pallas_call x1, Pallas kernels, parent_forces(): pl.pallas_call(functools.partial(parents_kernel, size), out_shape=[jax.Sh...  1.64 us
  transfers between devices with their start and end apart: 30, of which 14 were waited for; matrix products, arithmetic and copies ran while one was open for 2% of the time, Pallas kernels for 8%

profile of v4, /device:TPU:0, one launch (start us, length us, event | category | flops | bytes accessed | tf_op | source)
XLA Modules:
  0.0 70.5 jit_solution(16562007454454822386)
XLA Ops:
  0.6 1.6 %children.1 = (bf16[4,16,1024]{2,1,0:T(8,128)(2,1)S(1)}, bf16[4,16,1024]{2,1,0:T(8,128)(2,1)S(1)}, bf16[6,128,1024]{2,1,0:T(8,128)(2,1)S(1)}, f32[16,1024]{1,0:T(8,128)S(1)}, f32[16,128]{1,0:T(8,128)S(1)}) custom-call(s32[16]{0:T(128)} %parents_ref.1, bf16[16,8,1024]{2,1,0:T(8,128)(2,1)} %green_any.1, bf16[16,8,1024]{2,1,0:T(8,128)(2,1)} %delta_any.1, ...), custom_call_target="tpu_custom_call" | custom-call | flops 131072 | bytes 786432 | tf_op jit(solution)/shard_map/children/pallas_call | solution.py:153
  2.3 3.0 %collective-permute-start.16 = (bf16[4,16,1024]{2,1,0:T(8,128)(2,1)S(1)}, bf16[4,16,1024]{2,1,0:T(8,128)(2,1)S(1)}, u32[]{:S(2)}, u32[]{:S(2)}) collective-permute-start(bf16[4,16,1024]{2,1,0:T(8,128)(2,1)S(1)} %get-tuple-element.37.refs_1_), channel_id=1, source_target_pairs={{0,2},{4,0},{8,4},{12,8},{14,12},{10,14},{6,10},{2,6},{1,3},{5,1},... | collective-permute-start | bytes 393224 | tf_op jit(solution)/shard_map/ppermute | solution.py:363
  5.3 0.0 collective-permute-start
  5.3 0.2 collective-permute-start.20
  5.6 3.3 %collective-permute-done.16.refs_2_ = bf16[4,16,1024]{2,1,0:T(8,128)(2,1)S(1)} collective-permute-done((bf16[4,16,1024]{2,1,0:T(8,128)(2,1)S(1)}, bf16[4,16,1024]{2,1,0:T(8,128)(2,1)S(1)}, u32[]{:S(2)}, u32[]{:S(2)}) %collective-permute-start.16) | collective-permute-done | bytes 131104 | tf_op jit(solution)/shard_map/ppermute | solution.py:363
  8.9 1.7 %collective-permute-start.17 = (bf16[4,16,1024]{2,1,0:T(8,128)(2,1)S(1)}, bf16[4,16,1024]{2,1,0:T(8,128)(2,1)S(1)}, u32[]{:S(2)}, u32[]{:S(2)}) collective-permute-start(bf16[4,16,1024]{2,1,0:T(8,128)(2,1)S(1)} %collective-permute-done.16.refs_2_), channel_id=1, source_target_pairs={{0,2},{4,0},{8,4},{12,8},{14,12},{10,14},{6,10},{2,6},{1,3},{5,1},... | collective-permute-start | bytes 393224 | tf_op jit(solution)/shard_map/ppermute | solution.py:363
  10.6 0.7 collective-permute-done.20.refs_8_
  11.2 0.3 collective-permute-start.21
  11.5 2.4 %collective-permute-done.17.refs_3_ = bf16[4,16,1024]{2,1,0:T(8,128)(2,1)S(1)} collective-permute-done((bf16[4,16,1024]{2,1,0:T(8,128)(2,1)S(1)}, bf16[4,16,1024]{2,1,0:T(8,128)(2,1)S(1)}, u32[]{:S(2)}, u32[]{:S(2)}) %collective-permute-start.17) | collective-permute-done | bytes 131104 | tf_op jit(solution)/shard_map/ppermute | solution.py:363
  13.9 1.7 %collective-permute-start.18 = (bf16[4,16,1024]{2,1,0:T(8,128)(2,1)S(1)}, bf16[4,16,1024]{2,1,0:T(8,128)(2,1)S(1)}, u32[]{:S(2)}, u32[]{:S(2)}) collective-permute-start(bf16[4,16,1024]{2,1,0:T(8,128)(2,1)S(1)} %collective-permute-done.17.refs_3_), channel_id=1, source_target_pairs={{0,2},{4,0},{8,4},{12,8},{14,12},{10,14},{6,10},{2,6},{1,3},{5,1},... | collective-permute-start | bytes 393224 | tf_op jit(solution)/shard_map/ppermute | solution.py:363
  15.5 0.0 collective-permute-done.other_ref
  15.5 0.1 edge.1.refs_1_
  15.6 0.4 collective-permute-start.4
  16.1 0.7 collective-permute-done.21.refs_7_
  16.7 1.1 %collective-permute-start.22 = (bf16[4,16,1024]{2,1,0:T(8,128)(2,1)S(1)}, bf16[4,16,1024]{2,1,0:T(8,128)(2,1)S(1)}, u32[]{:S(2)}, u32[]{:S(2)}) collective-permute-start(bf16[4,16,1024]{2,1,0:T(8,128)(2,1)S(1)} %collective-permute-done.21.refs_7_), channel_id=1, source_target_pairs={{0,4},{4,8},{8,12},{12,14},{14,10},{10,6},{6,2},{2,0},{1,5},{5,9},... | collective-permute-start | bytes 393224 | tf_op jit(solution)/shard_map/ppermute | solution.py:363
  17.8 1.2 %collective-permute-done.18.refs_4_ = bf16[4,16,1024]{2,1,0:T(8,128)(2,1)S(1)} collective-permute-done((bf16[4,16,1024]{2,1,0:T(8,128)(2,1)S(1)}, bf16[4,16,1024]{2,1,0:T(8,128)(2,1)S(1)}, u32[]{:S(2)}, u32[]{:S(2)}) %collective-permute-start.18) | collective-permute-done | bytes 131104 | tf_op jit(solution)/shard_map/ppermute | solution.py:363
  19.0 1.9 %collective-permute-start.19 = (bf16[4,16,1024]{2,1,0:T(8,128)(2,1)S(1)}, bf16[4,16,1024]{2,1,0:T(8,128)(2,1)S(1)}, u32[]{:S(2)}, u32[]{:S(2)}) collective-permute-start(bf16[4,16,1024]{2,1,0:T(8,128)(2,1)S(1)} %collective-permute-done.18.refs_4_), channel_id=1, source_target_pairs={{0,2},{4,0},{8,4},{12,8},{14,12},{10,14},{6,10},{2,6},{1,3},{5,1},... | collective-permute-start | bytes 393224 | tf_op jit(solution)/shard_map/ppermute | solution.py:363
  20.9 1.6 %collective-permute-start.1 = (bf16[4,16,1024]{2,1,0:T(8,128)(2,1)S(1)}, bf16[4,16,1024]{2,1,0:T(8,128)(2,1)S(1)}, u32[]{:S(2)}, u32[]{:S(2)}) collective-permute-start(bf16[4,16,1024]{2,1,0:T(8,128)(2,1)S(1)} %edge.1.refs_1_), channel_id=1, source_target_pairs={{0,2},{4,0},{8,4},{12,8},{14,12},{10,14},{6,10},{2,6},{1,3},{5,1},... | collective-permute-start | bytes 393224 | tf_op jit(solution)/shard_map/ppermute | solution.py:363
  22.5 0.0 collective-permute-done.4.refs_8_
  22.5 0.5 collective-permute-start.5
  22.9 0.1 collective-permute-done.22.refs_6_
  23.0 1.2 %collective-permute-done.19.refs_5_ = bf16[4,16,1024]{2,1,0:T(8,128)(2,1)S(1)} collective-permute-done((bf16[4,16,1024]{2,1,0:T(8,128)(2,1)S(1)}, bf16[4,16,1024]{2,1,0:T(8,128)(2,1)S(1)}, u32[]{:S(2)}, u32[]{:S(2)}) %collective-permute-start.19) | collective-permute-done | bytes 131104 | tf_op jit(solution)/shard_map/ppermute | solution.py:363
  24.2 2.2 %shard_map.69 = (f32[520,128]{1,0:T(8,128)S(1)}, bf16[520,128]{1,0:T(8,128)(2,1)S(1)}, bf16[520,128]{1,0:T(8,128)(2,1)S(1)}, bf16[520,128]{1,0:T(8,128)(2,1)S(1)...) custom-call(bf16[6,128,1024]{2,1,0:T(8,128)(2,1)S(1)} %get-tuple-ele, ...), custom_call_target="tpu_custom_call" | custom-call | flops 1610612736 | bytes 3670016 | tf_op jit(solution)/shard_map/pallas_call | solution.py:247
  26.5 1.6 %collective-permute-start.26 = (bf16[520,128]{1,0:T(8,128)(2,1)S(1)}, bf16[520,128]{1,0:T(8,128)(2,1)}, u32[]{:S(2)}, u32[]{:S(2)}) collective-permute-start(bf16[520,128]{1,0:T(8,128)(2,1)S(1)} %get-tuple-element.45), channel_id=1, source_target_pairs={{0,2},{4,0},{8,4},{12,8},{14,12},{10,14},{6,10},{2,6},{1,3},{5,1},... | collective-permute-start | bytes 399368 | tf_op jit(solution)/shard_map/ppermute | solution.py:363
  28.1 0.0 collective-permute-done.1.refs_2_
  28.1 1.6 %collective-permute-start.2 = (bf16[4,16,1024]{2,1,0:T(8,128)(2,1)S(1)}, bf16[4,16,1024]{2,1,0:T(8,128)(2,1)S(1)}, u32[]{:S(2)}, u32[]{:S(2)}) collective-permute-start(bf16[4,16,1024]{2,1,0:T(8,128)(2,1)S(1)} %collective-permute-done.1.refs_2_), channel_id=1, source_target_pairs={{0,2},{4,0},{8,4},{12,8},{14,12},{10,14},{6,10},{2,6},{1,3},{5,1},... | collective-permute-start | bytes 393224 | tf_op jit(solution)/shard_map/ppermute | solution.py:363
  29.7 0.5 collective-permute-start.6
  30.2 0.4 collective-permute-start.23
  30.6 4.0 %collective-permute-done.2.refs_3_ = bf16[4,16,1024]{2,1,0:T(8,128)(2,1)S(1)} collective-permute-done((bf16[4,16,1024]{2,1,0:T(8,128)(2,1)S(1)}, bf16[4,16,1024]{2,1,0:T(8,128)(2,1)S(1)}, u32[]{:S(2)}, u32[]{:S(2)}) %collective-permute-start.2) | collective-permute-done | bytes 131104 | tf_op jit(solution)/shard_map/ppermute | solution.py:363
  34.6 1.7 %collective-permute-start.3 = (bf16[4,16,1024]{2,1,0:T(8,128)(2,1)S(1)}, bf16[4,16,1024]{2,1,0:T(8,128)(2,1)S(1)}, u32[]{:S(2)}, u32[]{:S(2)}) collective-permute-start(bf16[4,16,1024]{2,1,0:T(8,128)(2,1)S(1)} %collective-permute-done.2.refs_3_), channel_id=1, source_target_pairs={{0,2},{4,0},{8,4},{12,8},{14,12},{10,14},{6,10},{2,6},{1,3},{5,1},... | collective-permute-start | bytes 393224 | tf_op jit(solution)/shard_map/ppermute | solution.py:363
  36.3 0.0 collective-permute-done.6.refs_6_
  36.3 0.6 collective-permute-start.7
  36.9 0.0 collective-permute-done.26
  36.9 0.9 %add_convert_fusion.2 = bf16[520,128]{1,0:T(8,128)(2,1)S(1)} fusion(bf16[520,128]{1,0:T(8,128)(2,1)} %collective-permute-done.26, bf16[520,128]{1,0:T(8,128)(2,1)S(1)} %get-tuple-element.44), kind=kLoop, calls=%fused_computation.2 | loop fusion | flops 266240 | bytes 399360 | tf_op jit(solution)/shard_map/convert_element_type | solution.py:339
  37.8 1.5 %collective-permute-start.27 = (bf16[520,128]{1,0:T(8,128)(2,1)S(1)}, bf16[520,128]{1,0:T(8,128)(2,1)S(1)}, u32[]{:S(2)}, u32[]{:S(2)}) collective-permute-start(bf16[520,128]{1,0:T(8,128)(2,1)S(1)} %add_convert_fusion.2), channel_id=1, source_target_pairs={{0,2},{4,0},{8,4},{12,8},{14,12},{10,14},{6,10},{2,6},{1,3},{5,1},... | collective-permute-start | bytes 399368 | tf_op jit(solution)/shard_map/ppermute | solution.py:363
  39.4 0.6 collective-permute-start.24
  40.0 0.0 collective-permute-done.3.refs_4_
  40.0 2.2 %collective-permute-done.7.refs_5_ = bf16[4,16,1024]{2,1,0:T(8,128)(2,1)S(1)} collective-permute-done((bf16[4,16,1024]{2,1,0:T(8,128)(2,1)}, bf16[4,16,1024]{2,1,0:T(8,128)(2,1)S(1)}, u32[]{:S(2)}, u32[]{:S(2)}) %collective-permute-start.7) | collective-permute-done | bytes 131104 | tf_op jit(solution)/shard_map/ppermute | solution.py:363
  42.2 3.1 %shard_map.68 = (f32[520,128]{1,0:T(8,128)S(1)}, bf16[520,128]{1,0:T(8,128)(2,1)S(1)}, bf16[520,128]{1,0:T(8,128)(2,1)S(1)}, bf16[520,128]{1,0:T(8,128)(2,1)S(1)...) custom-call(bf16[6,128,1024]{2,1,0:T(8,128)(2,1)S(1)} %get-tuple-ele, ...), custom_call_target="tpu_custom_call" | custom-call | flops 1610612736 | bytes 3670016 | tf_op jit(solution)/shard_map/pallas_call | solution.py:247
  45.4 0.2 collective-permute-start.8
  45.6 1.8 %collective-permute-start.12 = (bf16[520,128]{1,0:T(8,128)(2,1)S(1)}, bf16[520,128]{1,0:T(8,128)(2,1)S(1)}, u32[]{:S(2)}, u32[]{:S(2)}) collective-permute-start(bf16[520,128]{1,0:T(8,128)(2,1)S(1)} %get-tuple-element.36), channel_id=1, source_target_pairs={{0,2},{4,0},{8,4},{12,8},{14,12},{10,14},{6,10},{2,6},{1,3},{5,1},... | collective-permute-start | bytes 399368 | tf_op jit(solution)/shard_map/ppermute | solution.py:363
  47.4 0.0 collective-permute-done.27
  47.4 0.0 copy-start
  47.4 0.0 copy-start.1
  47.5 1.6 %collective-permute-start.28 = (bf16[520,128]{1,0:T(8,128)(2,1)S(1)}, bf16[520,128]{1,0:T(8,128)(2,1)S(1)}, u32[]{:S(2)}, u32[]{:S(2)}) collective-permute-start(bf16[520,128]{1,0:T(8,128)(2,1)S(1)} %add_convert_fusion.1), channel_id=1, source_target_pairs={{0,2},{4,0},{8,4},{12,8},{14,12},{10,14},{6,10},{2,6},{1,3},{5,1},... | collective-permute-start | bytes 399368 | tf_op jit(solution)/shard_map/ppermute | solution.py:363
  49.1 0.0 collective-permute-done.24
  49.1 0.5 collective-permute-start.25
  49.6 1.3 %collective-permute-done.8 = bf16[520,128]{1,0:T(8,128)(2,1)S(1)} collective-permute-done((bf16[520,128]{1,0:T(8,128)(2,1)S(1)}, bf16[520,128]{1,0:T(8,128)(2,1)S(1)}, u32[]{:S(2)}, u32[]{:S(2)}) %collective-permute-start.8) | collective-permute-done | bytes 133152 | tf_op jit(solution)/shard_map/ppermute | solution.py:363
  50.9 0.1 collective-permute-start.9
  51.1 2.1 %collective-permute-start.13 = (bf16[520,128]{1,0:T(8,128)(2,1)S(1)}, bf16[520,128]{1,0:T(8,128)(2,1)S(1)}, u32[]{:S(2)}, u32[]{:S(2)}) collective-permute-start(bf16[520,128]{1,0:T(8,128)(2,1)S(1)} %add_convert_fusion.6), channel_id=1, source_target_pairs={{0,2},{4,0},{8,4},{12,8},{14,12},{10,14},{6,10},{2,6},{1,3},{5,1},... | collective-permute-start | bytes 399368 | tf_op jit(solution)/shard_map/ppermute | solution.py:363
  53.1 4.3 %collective-permute-done.9 = bf16[520,128]{1,0:T(8,128)(2,1)S(1)} collective-permute-done((bf16[520,128]{1,0:T(8,128)(2,1)S(1)}, bf16[520,128]{1,0:T(8,128)(2,1)S(1)}, u32[]{:S(2)}, u32[]{:S(2)}) %collective-permute-start.9) | collective-permute-done | bytes 133152 | tf_op jit(solution)/shard_map/ppermute | solution.py:363
  57.4 0.1 collective-permute-start.10
  57.5 2.1 %collective-permute-start.14 = (bf16[520,128]{1,0:T(8,128)(2,1)S(1)}, bf16[520,128]{1,0:T(8,128)(2,1)S(1)}, u32[]{:S(2)}, u32[]{:S(2)}) collective-permute-start(bf16[520,128]{1,0:T(8,128)(2,1)S(1)} %add_convert_fusion.5), channel_id=1, source_target_pairs={{0,2},{4,0},{8,4},{12,8},{14,12},{10,14},{6,10},{2,6},{1,3},{5,1},... | collective-permute-start | bytes 399368 | tf_op jit(solution)/shard_map/ppermute | solution.py:363
  59.6 2.9 %collective-permute-done.10 = bf16[520,128]{1,0:T(8,128)(2,1)S(1)} collective-permute-done((bf16[520,128]{1,0:T(8,128)(2,1)S(1)}, bf16[520,128]{1,0:T(8,128)(2,1)S(1)}, u32[]{:S(2)}, u32[]{:S(2)}) %collective-permute-start.10) | collective-permute-done | bytes 133152 | tf_op jit(solution)/shard_map/ppermute | solution.py:363
  62.5 0.1 collective-permute-start.11
  62.6 0.0 collective-permute-done.28
  62.6 2.1 %collective-permute-start.29 = (bf16[520,128]{1,0:T(8,128)(2,1)S(1)}, bf16[520,128]{1,0:T(8,128)(2,1)S(1)}, u32[]{:S(2)}, u32[]{:S(2)}) collective-permute-start(bf16[520,128]{1,0:T(8,128)(2,1)S(1)} %add_convert_fusion), channel_id=1, source_target_pairs={{0,2},{4,0},{8,4},{12,8},{14,12},{10,14},{6,10},{2,6},{1,3},{5,1},... | collective-permute-start | bytes 399368 | tf_op jit(solution)/shard_map/ppermute | solution.py:363
  64.7 0.0 collective-permute-done.14.refs_2_
  64.7 2.9 %collective-permute-done.11.refs_1_ = bf16[520,128]{1,0:T(8,128)(2,1)S(1)} collective-permute-done((bf16[520,128]{1,0:T(8,128)(2,1)S(1)}, bf16[520,128]{1,0:T(8,128)(2,1)S(1)}, u32[]{:S(2)}, u32[]{:S(2)}) %collective-permute-start.11) | collective-permute-done | bytes 133152 | tf_op jit(solution)/shard_map/ppermute | solution.py:363
  67.6 0.1 collective-permute-start.15
  67.7 0.0 collective-permute-done.25.refs_4_
  67.7 0.0 collective-permute-done.29.refs_5_
  67.7 1.2 %collective-permute-done.15.edge_ref = bf16[128,128]{1,0:T(8,128)(2,1)S(1)} collective-permute-done((bf16[128,128]{1,0:T(8,128)(2,1)S(1)}, bf16[128,128]{1,0:T(8,128)(2,1)S(1)}, u32[]{:S(2)}, u32[]{:S(2)}) %collective-permute-start.15) | collective-permute-done | bytes 32800 | tf_op jit(solution)/shard_map/ppermute | solution.py:335
  68.8 1.6 %parents.1 = (bf16[16,8,1024]{2,1,0:T(8,128)(2,1)}, f32[1,8]{1,0:T(1,128)}) custom-call(s32[16]{0:T(128)S(1)} %copy-done, s32[8]{0:T(128)S(1)} %copy-done.1, bf16[128,128]{1,0:T(8,128)(2,1)S(1)} %collective-permute-done.15.edge_ref, f32[520,128]{1,0:T(8,128)S(1)} %get-tuple-element.29.refs_0_, bf16[520,128]{1,0:T(8,128)(2,1)S(1)} %collective-permute-done.11.refs_1_, ...), custom_call_target="tpu_custom_call" | custom-call | flops 786432 | bytes 1310720 | tf_op jit(solution)/shard_map/parents/pallas_call | solution.py:312
  (18 shorter events, 0.4 us)
Async XLA Ops:
  0.6 4.7 %copy-start.2 = (bf16[16,8,1024]{2,1,0:T(8,128)(2,1)S(1)}, bf16[16,8,1024]{2,1,0:T(8,128)(2,1)}, u32[]{:S(2)}) copy-start(bf16[16,8,1024]{2,1,0:T(8,128)(2,1)} %green_any.1) | copy-start | bytes 786436
  2.3 6.6 %collective-permute-start.16 = (bf16[4,16,1024]{2,1,0:T(8,128)(2,1)S(1)}, bf16[4,16,1024]{2,1,0:T(8,128)(2,1)S(1)}, u32[]{:S(2)}, u32[]{:S(2)}) collective-permute-start(bf16[4,16,1024]{2,1,0:T(8,128)(2,1)S(1)} %get-tuple-element.37.refs_1_), channel_id=1, source_target_pairs={{0,2},{4,0},{8,4},{12,8},{14,12},{10,14},{6,10},{2,6},{1,3},{5,1},... | collective-permute-start | bytes 393224 | tf_op jit(solution)/shard_map/ppermute | solution.py:363
  5.3 10.2 %collective-permute-start = (bf16[16,8,1024]{2,1,0:T(8,128)(2,1)S(1)}, bf16[16,8,1024]{2,1,0:T(8,128)(2,1)S(1)}, u32[]{:S(2)}, u32[]{:S(2)}) collective-permute-start(bf16[16,8,1024]{2,1,0:T(8,128)(2,1)S(1)} %copy-done.2), channel_id=1, source_target_pairs={{0,1},{1,0},{2,3},{3,2},{4,5},{5,4},{6,7},{7,6},{8,9},{9,8},{10,11... | collective-permute-start | bytes 786440 | tf_op jit(solution)/shard_map/ppermute | solution.py:335
  5.3 5.9 %collective-permute-start.20 = (bf16[4,16,1024]{2,1,0:T(8,128)(2,1)S(1)}, bf16[4,16,1024]{2,1,0:T(8,128)(2,1)S(1)}, u32[]{:S(2)}, u32[]{:S(2)}) collective-permute-start(bf16[4,16,1024]{2,1,0:T(8,128)(2,1)S(1)} %get-tuple-element.37.refs_1_), channel_id=1, source_target_pairs={{0,4},{4,8},{8,12},{12,14},{14,10},{10,6},{6,2},{2,0},{1,5},{5,9},... | collective-permute-start | bytes 393224 | tf_op jit(solution)/shard_map/ppermute | solution.py:363
  8.9 5.0 %collective-permute-start.17 = (bf16[4,16,1024]{2,1,0:T(8,128)(2,1)S(1)}, bf16[4,16,1024]{2,1,0:T(8,128)(2,1)S(1)}, u32[]{:S(2)}, u32[]{:S(2)}) collective-permute-start(bf16[4,16,1024]{2,1,0:T(8,128)(2,1)S(1)} %collective-permute-done.16.refs_2_), channel_id=1, source_target_pairs={{0,2},{4,0},{8,4},{12,8},{14,12},{10,14},{6,10},{2,6},{1,3},{5,1},... | collective-permute-start | bytes 393224 | tf_op jit(solution)/shard_map/ppermute | solution.py:363
  11.2 5.5 %collective-permute-start.21 = (bf16[4,16,1024]{2,1,0:T(8,128)(2,1)S(1)}, bf16[4,16,1024]{2,1,0:T(8,128)(2,1)S(1)}, u32[]{:S(2)}, u32[]{:S(2)}) collective-permute-start(bf16[4,16,1024]{2,1,0:T(8,128)(2,1)S(1)} %collective-permute-done.20.refs_8_), channel_id=1, source_target_pairs={{0,4},{4,8},{8,12},{12,14},{14,10},{10,6},{6,2},{2,0},{1,5},{5,9},... | collective-permute-start | bytes 393224 | tf_op jit(solution)/shard_map/ppermute | solution.py:363
  13.9 5.1 %collective-permute-start.18 = (bf16[4,16,1024]{2,1,0:T(8,128)(2,1)S(1)}, bf16[4,16,1024]{2,1,0:T(8,128)(2,1)S(1)}, u32[]{:S(2)}, u32[]{:S(2)}) collective-permute-start(bf16[4,16,1024]{2,1,0:T(8,128)(2,1)S(1)} %collective-permute-done.17.refs_3_), channel_id=1, source_target_pairs={{0,2},{4,0},{8,4},{12,8},{14,12},{10,14},{6,10},{2,6},{1,3},{5,1},... | collective-permute-start | bytes 393224 | tf_op jit(solution)/shard_map/ppermute | solution.py:363
  15.6 6.9 %collective-permute-start.4 = (bf16[4,16,1024]{2,1,0:T(8,128)(2,1)S(1)}, bf16[4,16,1024]{2,1,0:T(8,128)(2,1)S(1)}, u32[]{:S(2)}, u32[]{:S(2)}) collective-permute-start(bf16[4,16,1024]{2,1,0:T(8,128)(2,1)S(1)} %edge.1.refs_1_), channel_id=1, source_target_pairs={{0,4},{4,8},{8,12},{12,14},{14,10},{10,6},{6,2},{2,0},{1,5},{5,9},... | collective-permute-start | bytes 393224 | tf_op jit(solution)/shard_map/ppermute | solution.py:363
  16.7 6.3 %collective-permute-start.22 = (bf16[4,16,1024]{2,1,0:T(8,128)(2,1)S(1)}, bf16[4,16,1024]{2,1,0:T(8,128)(2,1)S(1)}, u32[]{:S(2)}, u32[]{:S(2)}) collective-permute-start(bf16[4,16,1024]{2,1,0:T(8,128)(2,1)S(1)} %collective-permute-done.21.refs_7_), channel_id=1, source_target_pairs={{0,4},{4,8},{8,12},{12,14},{14,10},{10,6},{6,2},{2,0},{1,5},{5,9},... | collective-permute-start | bytes 393224 | tf_op jit(solution)/shard_map/ppermute | solution.py:363
  19.0 5.3 %collective-permute-start.19 = (bf16[4,16,1024]{2,1,0:T(8,128)(2,1)S(1)}, bf16[4,16,1024]{2,1,0:T(8,128)(2,1)S(1)}, u32[]{:S(2)}, u32[]{:S(2)}) collective-permute-start(bf16[4,16,1024]{2,1,0:T(8,128)(2,1)S(1)} %collective-permute-done.18.refs_4_), channel_id=1, source_target_pairs={{0,2},{4,0},{8,4},{12,8},{14,12},{10,14},{6,10},{2,6},{1,3},{5,1},... | collective-permute-start | bytes 393224 | tf_op jit(solution)/shard_map/ppermute | solution.py:363
  20.9 7.2 %collective-permute-start.1 = (bf16[4,16,1024]{2,1,0:T(8,128)(2,1)S(1)}, bf16[4,16,1024]{2,1,0:T(8,128)(2,1)S(1)}, u32[]{:S(2)}, u32[]{:S(2)}) collective-permute-start(bf16[4,16,1024]{2,1,0:T(8,128)(2,1)S(1)} %edge.1.refs_1_), channel_id=1, source_target_pairs={{0,2},{4,0},{8,4},{12,8},{14,12},{10,14},{6,10},{2,6},{1,3},{5,1},... | collective-permute-start | bytes 393224 | tf_op jit(solution)/shard_map/ppermute | solution.py:363
  22.5 7.2 %collective-permute-start.5 = (bf16[4,16,1024]{2,1,0:T(8,128)(2,1)S(1)}, bf16[4,16,1024]{2,1,0:T(8,128)(2,1)S(1)}, u32[]{:S(2)}, u32[]{:S(2)}) collective-permute-start(bf16[4,16,1024]{2,1,0:T(8,128)(2,1)S(1)} %collective-permute-done.4.refs_8_), channel_id=1, source_target_pairs={{0,4},{4,8},{8,12},{12,14},{14,10},{10,6},{6,2},{2,0},{1,5},{5,9},... | collective-permute-start | bytes 393224 | tf_op jit(solution)/shard_map/ppermute | solution.py:363
  26.5 10.4 %collective-permute-start.26 = (bf16[520,128]{1,0:T(8,128)(2,1)S(1)}, bf16[520,128]{1,0:T(8,128)(2,1)}, u32[]{:S(2)}, u32[]{:S(2)}) collective-permute-start(bf16[520,128]{1,0:T(8,128)(2,1)S(1)} %get-tuple-element.45), channel_id=1, source_target_pairs={{0,2},{4,0},{8,4},{12,8},{14,12},{10,14},{6,10},{2,6},{1,3},{5,1},... | collective-permute-start | bytes 399368 | tf_op jit(solution)/shard_map/ppermute | solution.py:363
  28.1 6.4 %collective-permute-start.2 = (bf16[4,16,1024]{2,1,0:T(8,128)(2,1)S(1)}, bf16[4,16,1024]{2,1,0:T(8,128)(2,1)S(1)}, u32[]{:S(2)}, u32[]{:S(2)}) collective-permute-start(bf16[4,16,1024]{2,1,0:T(8,128)(2,1)S(1)} %collective-permute-done.1.refs_2_), channel_id=1, source_target_pairs={{0,2},{4,0},{8,4},{12,8},{14,12},{10,14},{6,10},{2,6},{1,3},{5,1},... | collective-permute-start | bytes 393224 | tf_op jit(solution)/shard_map/ppermute | solution.py:363
  29.7 6.6 %collective-permute-start.6 = (bf16[4,16,1024]{2,1,0:T(8,128)(2,1)S(1)}, bf16[4,16,1024]{2,1,0:T(8,128)(2,1)}, u32[]{:S(2)}, u32[]{:S(2)}) collective-permute-start(bf16[4,16,1024]{2,1,0:T(8,128)(2,1)S(1)} %collective-permute-done.5.refs_7_), channel_id=1, source_target_pairs={{0,4},{4,8},{8,12},{12,14},{14,10},{10,6},{6,2},{2,0},{1,5},{5,9},... | collective-permute-start | bytes 393224 | tf_op jit(solution)/shard_map/ppermute | solution.py:363
  30.2 9.2 %collective-permute-start.23 = (bf16[520,128]{1,0:T(8,128)(2,1)S(1)}, bf16[520,128]{1,0:T(8,128)(2,1)S(1)}, u32[]{:S(2)}, u32[]{:S(2)}) collective-permute-start(bf16[520,128]{1,0:T(8,128)(2,1)S(1)} %get-tuple-element.41), channel_id=1, source_target_pairs={{0,4},{4,8},{8,12},{12,14},{14,10},{10,6},{6,2},{2,0},{1,5},{5,9},... | collective-permute-start | bytes 399368 | tf_op jit(solution)/shard_map/ppermute | solution.py:363
  34.6 5.5 %collective-permute-start.3 = (bf16[4,16,1024]{2,1,0:T(8,128)(2,1)S(1)}, bf16[4,16,1024]{2,1,0:T(8,128)(2,1)S(1)}, u32[]{:S(2)}, u32[]{:S(2)}) collective-permute-start(bf16[4,16,1024]{2,1,0:T(8,128)(2,1)S(1)} %collective-permute-done.2.refs_3_), channel_id=1, source_target_pairs={{0,2},{4,0},{8,4},{12,8},{14,12},{10,14},{6,10},{2,6},{1,3},{5,1},... | collective-permute-start | bytes 393224 | tf_op jit(solution)/shard_map/ppermute | solution.py:363
  36.3 5.9 %collective-permute-start.7 = (bf16[4,16,1024]{2,1,0:T(8,128)(2,1)}, bf16[4,16,1024]{2,1,0:T(8,128)(2,1)S(1)}, u32[]{:S(2)}, u32[]{:S(2)}) collective-permute-start(bf16[4,16,1024]{2,1,0:T(8,128)(2,1)} %collective-permute-done.6.refs_6_), channel_id=1, source_target_pairs={{0,4},{4,8},{8,12},{12,14},{14,10},{10,6},{6,2},{2,0},{1,5},{5,9},... | collective-permute-start | bytes 393224 | tf_op jit(solution)/shard_map/ppermute | solution.py:363
  37.8 9.6 %collective-permute-start.27 = (bf16[520,128]{1,0:T(8,128)(2,1)S(1)}, bf16[520,128]{1,0:T(8,128)(2,1)S(1)}, u32[]{:S(2)}, u32[]{:S(2)}) collective-permute-start(bf16[520,128]{1,0:T(8,128)(2,1)S(1)} %add_convert_fusion.2), channel_id=1, source_target_pairs={{0,2},{4,0},{8,4},{12,8},{14,12},{10,14},{6,10},{2,6},{1,3},{5,1},... | collective-permute-start | bytes 399368 | tf_op jit(solution)/shard_map/ppermute | solution.py:363
  39.4 9.7 %collective-permute-start.24 = (bf16[520,128]{1,0:T(8,128)(2,1)S(1)}, bf16[520,128]{1,0:T(8,128)(2,1)S(1)}, u32[]{:S(2)}, u32[]{:S(2)}) collective-permute-start(bf16[520,128]{1,0:T(8,128)(2,1)S(1)} %add_convert_fusion.4), channel_id=1, source_target_pairs={{0,4},{4,8},{8,12},{12,14},{14,10},{10,6},{6,2},{2,0},{1,5},{5,9},... | collective-permute-start | bytes 399368 | tf_op jit(solution)/shard_map/ppermute | solution.py:363
  45.4 5.5 %collective-permute-start.8 = (bf16[520,128]{1,0:T(8,128)(2,1)S(1)}, bf16[520,128]{1,0:T(8,128)(2,1)S(1)}, u32[]{:S(2)}, u32[]{:S(2)}) collective-permute-start(bf16[520,128]{1,0:T(8,128)(2,1)S(1)} %get-tuple-element.33), channel_id=1, source_target_pairs={{0,4},{4,8},{8,12},{12,14},{14,10},{10,6},{6,2},{2,0},{1,5},{5,9},... | collective-permute-start | bytes 399368 | tf_op jit(solution)/shard_map/ppermute | solution.py:363
  45.6 5.4 %collective-permute-start.12 = (bf16[520,128]{1,0:T(8,128)(2,1)S(1)}, bf16[520,128]{1,0:T(8,128)(2,1)S(1)}, u32[]{:S(2)}, u32[]{:S(2)}) collective-permute-start(bf16[520,128]{1,0:T(8,128)(2,1)S(1)} %get-tuple-element.36), channel_id=1, source_target_pairs={{0,2},{4,0},{8,4},{12,8},{14,12},{10,14},{6,10},{2,6},{1,3},{5,1},... | collective-permute-start | bytes 399368 | tf_op jit(solution)/shard_map/ppermute | solution.py:363
  47.4 21.4 %copy-start = (s32[16]{0:T(128)S(1)}, s32[16]{0:T(128)}, u32[]{:S(2)}) copy-start(s32[16]{0:T(128)} %parents_ref.1) | copy-start | bytes 196
  47.4 21.4 %copy-start.1 = (s32[8]{0:T(128)S(1)}, s32[8]{0:T(128)}, u32[]{:S(2)}) copy-start(s32[8]{0:T(128)} %counts_ref.1) | copy-start | bytes 100
  47.5 15.1 %collective-permute-start.28 = (bf16[520,128]{1,0:T(8,128)(2,1)S(1)}, bf16[520,128]{1,0:T(8,128)(2,1)S(1)}, u32[]{:S(2)}, u32[]{:S(2)}) collective-permute-start(bf16[520,128]{1,0:T(8,128)(2,1)S(1)} %add_convert_fusion.1), channel_id=1, source_target_pairs={{0,2},{4,0},{8,4},{12,8},{14,12},{10,14},{6,10},{2,6},{1,3},{5,1},... | collective-permute-start | bytes 399368 | tf_op jit(solution)/shard_map/ppermute | solution.py:363
  49.1 18.5 %collective-permute-start.25 = (bf16[520,128]{1,0:T(8,128)(2,1)S(1)}, bf16[520,128]{1,0:T(8,128)(2,1)S(1)}, u32[]{:S(2)}, u32[]{:S(2)}) collective-permute-start(bf16[520,128]{1,0:T(8,128)(2,1)S(1)} %add_convert_fusion.3), channel_id=1, source_target_pairs={{0,4},{4,8},{8,12},{12,14},{14,10},{10,6},{6,2},{2,0},{1,5},{5,9},... | collective-permute-start | bytes 399368 | tf_op jit(solution)/shard_map/ppermute | solution.py:363
  50.9 6.4 %collective-permute-start.9 = (bf16[520,128]{1,0:T(8,128)(2,1)S(1)}, bf16[520,128]{1,0:T(8,128)(2,1)S(1)}, u32[]{:S(2)}, u32[]{:S(2)}) collective-permute-start(bf16[520,128]{1,0:T(8,128)(2,1)S(1)} %add_convert_fusion.9), channel_id=1, source_target_pairs={{0,4},{4,8},{8,12},{12,14},{14,10},{10,6},{6,2},{2,0},{1,5},{5,9},... | collective-permute-start | bytes 399368 | tf_op jit(solution)/shard_map/ppermute | solution.py:363
  51.1 6.4 %collective-permute-start.13 = (bf16[520,128]{1,0:T(8,128)(2,1)S(1)}, bf16[520,128]{1,0:T(8,128)(2,1)S(1)}, u32[]{:S(2)}, u32[]{:S(2)}) collective-permute-start(bf16[520,128]{1,0:T(8,128)(2,1)S(1)} %add_convert_fusion.6), channel_id=1, source_target_pairs={{0,2},{4,0},{8,4},{12,8},{14,12},{10,14},{6,10},{2,6},{1,3},{5,1},... | collective-permute-start | bytes 399368 | tf_op jit(solution)/shard_map/ppermute | solution.py:363
  57.4 5.0 %collective-permute-start.10 = (bf16[520,128]{1,0:T(8,128)(2,1)S(1)}, bf16[520,128]{1,0:T(8,128)(2,1)S(1)}, u32[]{:S(2)}, u32[]{:S(2)}) collective-permute-start(bf16[520,128]{1,0:T(8,128)(2,1)S(1)} %add_convert_fusion.8), channel_id=1, source_target_pairs={{0,4},{4,8},{8,12},{12,14},{14,10},{10,6},{6,2},{2,0},{1,5},{5,9},... | collective-permute-start | bytes 399368 | tf_op jit(solution)/shard_map/ppermute | solution.py:363
  57.5 7.1 %collective-permute-start.14 = (bf16[520,128]{1,0:T(8,128)(2,1)S(1)}, bf16[520,128]{1,0:T(8,128)(2,1)S(1)}, u32[]{:S(2)}, u32[]{:S(2)}) collective-permute-start(bf16[520,128]{1,0:T(8,128)(2,1)S(1)} %add_convert_fusion.5), channel_id=1, source_target_pairs={{0,2},{4,0},{8,4},{12,8},{14,12},{10,14},{6,10},{2,6},{1,3},{5,1},... | collective-permute-start | bytes 399368 | tf_op jit(solution)/shard_map/ppermute | solution.py:363
  62.5 5.0 %collective-permute-start.11 = (bf16[520,128]{1,0:T(8,128)(2,1)S(1)}, bf16[520,128]{1,0:T(8,128)(2,1)S(1)}, u32[]{:S(2)}, u32[]{:S(2)}) collective-permute-start(bf16[520,128]{1,0:T(8,128)(2,1)S(1)} %add_convert_fusion.7), channel_id=1, source_target_pairs={{0,4},{4,8},{8,12},{12,14},{14,10},{10,6},{6,2},{2,0},{1,5},{5,9},... | collective-permute-start | bytes 399368 | tf_op jit(solution)/shard_map/ppermute | solution.py:363
  62.6 5.0 %collective-permute-start.29 = (bf16[520,128]{1,0:T(8,128)(2,1)S(1)}, bf16[520,128]{1,0:T(8,128)(2,1)S(1)}, u32[]{:S(2)}, u32[]{:S(2)}) collective-permute-start(bf16[520,128]{1,0:T(8,128)(2,1)S(1)} %add_convert_fusion), channel_id=1, source_target_pairs={{0,2},{4,0},{8,4},{12,8},{14,12},{10,14},{6,10},{2,6},{1,3},{5,1},... | collective-permute-start | bytes 399368 | tf_op jit(solution)/shard_map/ppermute | solution.py:363
  67.6 1.3 %collective-permute-start.15 = (bf16[128,128]{1,0:T(8,128)(2,1)S(1)}, bf16[128,128]{1,0:T(8,128)(2,1)S(1)}, u32[]{:S(2)}, u32[]{:S(2)}) collective-permute-start(bf16[128,128]{1,0:T(8,128)(2,1)S(1)} %add_convert_fusion.10), channel_id=1, source_target_pairs={{0,1},{1,0},{2,3},{3,2},{4,5},{5,4},{6,7},{7,6},{8,9},{9,8},{10,11... | collective-permute-start | bytes 98312 | tf_op jit(solution)/shard_map/ppermute | solution.py:335

commit v5 on v4

--- a/solution.py
+++ b/solution.py
@@ -77,20 +77,19 @@
     return slice(first, first + rows)
 
 
-def children_kernel(parents_any, green_any, delta_any, chol_any, *refs):
+def children_kernel(n, parents_any, green_any, delta_any, chol_any, *refs):
     out0_ref, out1_ref, chol_ref, change_ref, outside_ref = refs[:5]
     parents_ref, green_ref, delta_ref, green_wide, delta_wide, sems = refs[5:]
     rows, walkers, width = green_ref.shape
+    moves = [(parents_any, parents_ref), (green_any, green_ref), (delta_any, delta_ref)]
+    for r in range(n):
+        first = pl.multiple_of(block_at(n, r) * rows, rows)
+        moves.append(
+            (chol_any.at[:, pl.ds(first, rows), :], chol_ref.at[:, pl.ds(r * rows, rows), :])
+        )
     copies = [
         pltpu.make_async_copy(source, target, sems.at[k])
-        for k, (source, target) in enumerate(
-            (
-                (parents_any, parents_ref),
-                (green_any, green_ref),
-                (delta_any, delta_ref),
-                (chol_any, chol_ref),
-            )
-        )
+        for k, (source, target) in enumerate(moves)
     ]
     for copy in copies:
         copy.start()
@@ -121,7 +120,8 @@
     parent = local_parent(child)
     outside = jnp.where(jnp.logical_or(parent < 0, parent >= walkers), 1.0, 0.0)
     outside_ref[...] = jnp.full((rows, 128), outside, F32)
-    copies[3].wait()
+    for copy in copies[3:]:
+        copy.wait()
 
 
 def edge_walker(walkers):
@@ -146,12 +146,13 @@
 
 def make_children(size, parents, green, delta, chol):
     rows, walkers, width = green.shape
+    n = chol.shape[1] // rows
     wide = pltpu.VMEM((width // 128, rows * walkers, 128), F32)
     here = [
         pltpu.with_memory_space_constraint(a, pltpu.HBM) for a in (parents, green, delta, chol)
     ]
     return pl.pallas_call(
-        children_kernel,
+        functools.partial(children_kernel, n),
         out_shape=[
             jax.ShapeDtypeStruct((size, rows, width), BF16),
             jax.ShapeDtypeStruct((walkers - size, rows, width), BF16),
@@ -167,7 +168,7 @@
             pltpu.VMEM(delta.shape, BF16),
             wide,
             wide,
-            pltpu.SemaphoreType.DMA((4,)),
+            pltpu.SemaphoreType.DMA((3 + n,)),
         ],
         cost_estimate=pl.CostEstimate(
             flops=green.size, bytes_accessed=6 * green.size, transcendentals=0
@@ -193,48 +194,52 @@
     )(chunk, change, outside, other)
 
 
-def force_kernel(factor, energy_scale, n, *refs):
+def force_kernel(energy_scale, n, *refs):
     chol_ref, chunks, outs = refs[0], refs[1 : n + 1], refs[n + 1 : 2 * n + 1]
-    child, low, force = refs[2 * n + 1 :]
+    low = refs[2 * n + 1]
     size, rows, width = chunks[0].shape
     vectors, orbitals, _ = chol_ref.shape
-    starts = [pl.multiple_of(block_at(n, r) * rows, rows) for r in range(n)]
-    for c in range(size):
-        for r in range(n):
-            child[c, pl.ds(starts[r], rows), :] = chunks[r][c]
-    chol = chol_ref[...].reshape(vectors * orbitals, width)
-    step = 2 if size % 2 == 0 else 1
-    for c in range(0, size, step):
+    terms = vectors * orbitals
+
+    def child(c, lanes):
+        return jnp.concatenate([chunks[r][c, :, lanes] for r in range(n)], axis=0)
+
+    for c in range(0, size, 2):
+        pair = range(c, min(c + 2, size))
         cross = lax.dot_general(
-            chol,
-            child[c : c + step].reshape(step * orbitals, width),
+            chol_ref[...].reshape(terms, width),
+            jnp.concatenate([child(w, slice(None)) for w in pair], axis=0),
             (((1,), (1,)), ((), ())),
             preferred_element_type=F32,
         ).astype(BF16)
-        for d in range(step):
+        for d, w in enumerate(pair):
             for g in range(vectors):
-                low[c + d, :, g * orbitals : (g + 1) * orbitals] = cross[
+                low[w, :, g * orbitals : (g + 1) * orbitals] = cross[
                     g * orbitals : (g + 1) * orbitals, d * orbitals : (d + 1) * orbitals
                 ]
-    force[...] = jnp.dot(
-        low[...].reshape(size * orbitals, vectors * orbitals), chol, preferred_element_type=F32
-    ).reshape(size, orbitals, width)
-    sums = []
-    for c in range(size):
-        product = jnp.sum(child[c].astype(F32) * force[c], axis=0, keepdims=True)
-        sums.append(sum(product[:, s : s + 128] for s in range(0, width, 128)))
+    sums = [jnp.zeros((1, 128), F32)] * size
+    span = 256 if width % 256 == 0 else 128
+    for first in range(0, width, span):
+        force = jnp.dot(
+            low[...].reshape(size * orbitals, terms),
+            chol_ref[:, :, first : first + span].reshape(terms, span),
+            preferred_element_type=F32,
+        )
+        for c in range(size):
+            for lane in range(0, span, 128):
+                lanes = slice(first + lane, first + lane + 128)
+                block = force[c * orbitals : (c + 1) * orbitals, lane : lane + 128]
+                product = child(c, lanes).astype(F32) * block
+                sums[c] = sums[c] + jnp.sum(product, axis=0, keepdims=True)
+                for r in range(n):
+                    place = message_block(c, (first + lane) // 128, rows, width)
+                    outs[r][place, :] = block[r * rows : (r + 1) * rows, :].astype(outs[r].dtype)
     sums = jnp.concatenate(sums + [jnp.zeros((8 - size, 128), F32)], axis=0)
     energy = jnp.sum(sums, axis=1, keepdims=True) * energy_scale
     high = energy.astype(BF16).astype(F32)
     lane = lax.broadcasted_iota(jnp.int32, (8, 128), 1) - 2 * lax.axis_index("chol")
     tile = jnp.where(lane == 0, high, 0.0) + jnp.where(lane == 1, energy - high, 0.0)
     for r in range(n):
-        for c in range(size):
-            for t in range(width // 128):
-                block = force[c, pl.ds(starts[r], rows), t * 128 : t * 128 + 128]
-                outs[r][message_block(c, t, rows, width), :] = (block * factor).astype(
-                    outs[r].dtype
-                )
         outs[r][message_rows(size, rows, width) - 8 :, :] = tile.astype(outs[r].dtype)
 
 
@@ -245,17 +250,13 @@
     total = n * vectors
     shape = (message_rows(size, rows, width), 128)
     return pl.pallas_call(
-        functools.partial(
-            force_kernel, -1.0 / total**0.5, -0.125 / (total * orbitals), n
-        ),
+        functools.partial(force_kernel, -0.125 / (total * orbitals), n),
         out_shape=[jax.ShapeDtypeStruct(shape, F32)]
         + [jax.ShapeDtypeStruct(shape, BF16)] * (n - 1),
         in_specs=[VMEM] * (1 + n),
         out_specs=[VMEM] * n,
         scratch_shapes=[
-            pltpu.VMEM((size, orbitals, width), BF16),
             pltpu.VMEM((size, orbitals, vectors * orbitals), BF16),
-            pltpu.VMEM((size, orbitals, width), F32),
         ],
         cost_estimate=pl.CostEstimate(
             flops=4 * size * orbitals * width * vectors * orbitals,
@@ -266,7 +267,7 @@
     )(chol, *chunks)
 
 
-def parents_kernel(size, parents_ref, counts_ref, edge_ref, *refs):
+def parents_kernel(factor, size, parents_ref, counts_ref, edge_ref, *refs):
     groups = (refs[0:3], refs[3:6])
     out_ref, energy_ref, total, spread = refs[6:]
     rows, walkers, width = out_ref.shape
@@ -299,7 +300,7 @@
             valid = jnp.logical_and(child >= 0, child <= last)
             found = parents_ref[jnp.clip(child, 0, last)] == parent
             summed = summed + jnp.where(jnp.logical_and(valid, found), edge, 0.0)
-        mean = summed * (1.0 / jnp.maximum(counts_ref[p], 1).astype(F32))
+        mean = summed * (factor / jnp.maximum(counts_ref[p], 1).astype(F32))
         for t in range(blocks):
             spread[t, pl.ds(p, rows, stride=walkers), :] = mean[t * rows : (t + 1) * rows, :]
     for t in range(blocks):
@@ -307,10 +308,10 @@
         out_ref[:, :, t * 128 : t * 128 + 128] = block
 
 
-def parent_forces(shape, size, parents, counts, edge, group0, group1):
+def parent_forces(shape, size, factor, parents, counts, edge, group0, group1):
     rows, walkers, width = shape
     return pl.pallas_call(
-        functools.partial(parents_kernel, size),
+        functools.partial(parents_kernel, factor, size),
         out_shape=[
             jax.ShapeDtypeStruct(shape, BF16),
             jax.ShapeDtypeStruct((1, walkers), F32),
@@ -362,6 +363,8 @@
     def hop(x, key):
         return lax.ppermute(x, "chol", pairs[key[3]])
 
+    factor = -1.0 / (n * chol_vectors.shape[0]) ** 0.5
+
     other = swap_cores(green_half)
     *own, chol, change, outside = make_children(
         size, parents, green_half, step_delta, chol_vectors
@@ -392,7 +395,7 @@
     ]
     edge = swap_cores((own + up + down).astype(BF16))
     parent_force, energy = parent_forces(
-        green_half.shape, size, parents, copy_counts, edge, group0, group1
+        green_half.shape, size, factor, parents, copy_counts, edge, group0, group1
     )
     return parent_force, energy.reshape(walkers)
 

time: 70.7 us -> 68.7 us (0.972)
  waiting for transfers between devices: 28.2 us -> 26.7 us
    ppermute x28, waiting for transfers between devices: 27 us -> 25.9 us  [hop(): return lax.ppermute(x, 'chol', pairs[key[3]])]
  transfers between devices with their start and end apart: 30 -> 30, of which waited for: 14 -> 17; matrix products, arithmetic and copies ran while one was open for 2% -> 2% of each run, Pallas kernels for 8% -> 7%
where the time goes in v5:
time: 68.7 us; the launch traced here: 68.5 us
  starting transfers between devices  31.5 us (46%)
  waiting for transfers between devices  26.7 us (39%)
  Pallas kernels  8.22 us (12%)
  other arithmetic  1.3 us (2%)
  between operations  0.75 us (1%)
    ppermute x28, starting transfers between devices, hop(): return lax.ppermute(x, 'chol', pairs[key[3]])  31.4 us
    ppermute x28, waiting for transfers between devices, hop(): return lax.ppermute(x, 'chol', pairs[key[3]])  25.9 us
    pallas_call x2, Pallas kernels, partial_forces(): pl.pallas_call(functools.partial(force_kernel, -0.125 / (total * orbitals...  4.84 us
    pallas_call x1, Pallas kernels, make_children(): pl.pallas_call(functools.partial(children_kernel, n), out_shape=[jax.Shap...  1.64 us
    pallas_call x1, Pallas kernels, parent_forces(): pl.pallas_call(functools.partial(parents_kernel, factor, size), out_shape...  1.64 us
  transfers between devices with their start and end apart: 30, of which 17 were waited for; matrix products, arithmetic and copies ran while one was open for 2% of the time, Pallas kernels for 7%

profile of v5, /device:TPU:0, one launch (start us, length us, event | category | flops | bytes accessed | tf_op | source)
XLA Modules:
  0.0 68.5 jit_solution(31094511024166597)
XLA Ops:
  0.6 1.6 %children.1 = (bf16[4,16,1024]{2,1,0:T(8,128)(2,1)S(1)}, bf16[4,16,1024]{2,1,0:T(8,128)(2,1)S(1)}, bf16[6,128,1024]{2,1,0:T(8,128)(2,1)S(1)}, f32[16,1024]{1,0:T(8,128)S(1)}, f32[16,128]{1,0:T(8,128)S(1)}) custom-call(s32[16]{0:T(128)} %parents_ref.1, bf16[16,8,1024]{2,1,0:T(8,128)(2,1)} %green_any.1, bf16[16,8,1024]{2,1,0:T(8,128)(2,1)} %delta_any.1, ...), custom_call_target="tpu_custom_call" | custom-call | flops 131072 | bytes 786432 | tf_op jit(solution)/shard_map/children/pallas_call | solution.py:154
  2.3 3.0 %collective-permute-start.16 = (bf16[4,16,1024]{2,1,0:T(8,128)(2,1)S(1)}, bf16[4,16,1024]{2,1,0:T(8,128)(2,1)S(1)}, u32[]{:S(2)}, u32[]{:S(2)}) collective-permute-start(bf16[4,16,1024]{2,1,0:T(8,128)(2,1)S(1)} %get-tuple-element.37.refs_1_), channel_id=1, source_target_pairs={{0,2},{4,0},{8,4},{12,8},{14,12},{10,14},{6,10},{2,6},{1,3},{5,1},... | collective-permute-start | bytes 393224 | tf_op jit(solution)/shard_map/ppermute | solution.py:364
  5.3 0.0 collective-permute-start
  5.3 0.2 collective-permute-start.20
  5.6 3.3 %collective-permute-done.16.refs_2_ = bf16[4,16,1024]{2,1,0:T(8,128)(2,1)S(1)} collective-permute-done((bf16[4,16,1024]{2,1,0:T(8,128)(2,1)S(1)}, bf16[4,16,1024]{2,1,0:T(8,128)(2,1)S(1)}, u32[]{:S(2)}, u32[]{:S(2)}) %collective-permute-start.16) | collective-permute-done | bytes 131104 | tf_op jit(solution)/shard_map/ppermute | solution.py:364
  8.9 1.7 %collective-permute-start.17 = (bf16[4,16,1024]{2,1,0:T(8,128)(2,1)S(1)}, bf16[4,16,1024]{2,1,0:T(8,128)(2,1)S(1)}, u32[]{:S(2)}, u32[]{:S(2)}) collective-permute-start(bf16[4,16,1024]{2,1,0:T(8,128)(2,1)S(1)} %collective-permute-done.16.refs_2_), channel_id=1, source_target_pairs={{0,2},{4,0},{8,4},{12,8},{14,12},{10,14},{6,10},{2,6},{1,3},{5,1},... | collective-permute-start | bytes 393224 | tf_op jit(solution)/shard_map/ppermute | solution.py:364
  10.5 0.7 collective-permute-done.20.refs_8_
  11.2 0.3 collective-permute-start.21
  11.5 2.4 %collective-permute-done.17.refs_3_ = bf16[4,16,1024]{2,1,0:T(8,128)(2,1)S(1)} collective-permute-done((bf16[4,16,1024]{2,1,0:T(8,128)(2,1)S(1)}, bf16[4,16,1024]{2,1,0:T(8,128)(2,1)S(1)}, u32[]{:S(2)}, u32[]{:S(2)}) %collective-permute-start.17) | collective-permute-done | bytes 131104 | tf_op jit(solution)/shard_map/ppermute | solution.py:364
  13.9 1.7 %collective-permute-start.18 = (bf16[4,16,1024]{2,1,0:T(8,128)(2,1)S(1)}, bf16[4,16,1024]{2,1,0:T(8,128)(2,1)S(1)}, u32[]{:S(2)}, u32[]{:S(2)}) collective-permute-start(bf16[4,16,1024]{2,1,0:T(8,128)(2,1)S(1)} %collective-permute-done.17.refs_3_), channel_id=1, source_target_pairs={{0,2},{4,0},{8,4},{12,8},{14,12},{10,14},{6,10},{2,6},{1,3},{5,1},... | collective-permute-start | bytes 393224 | tf_op jit(solution)/shard_map/ppermute | solution.py:364
  15.5 0.0 collective-permute-done.other_ref
  15.5 0.1 edge.1.refs_1_
  15.6 0.4 collective-permute-start.4
  16.0 0.7 collective-permute-done.21.refs_7_
  16.7 1.1 %collective-permute-start.22 = (bf16[4,16,1024]{2,1,0:T(8,128)(2,1)S(1)}, bf16[4,16,1024]{2,1,0:T(8,128)(2,1)S(1)}, u32[]{:S(2)}, u32[]{:S(2)}) collective-permute-start(bf16[4,16,1024]{2,1,0:T(8,128)(2,1)S(1)} %collective-permute-done.21.refs_7_), channel_id=1, source_target_pairs={{0,4},{4,8},{8,12},{12,14},{14,10},{10,6},{6,2},{2,0},{1,5},{5,9},... | collective-permute-start | bytes 393224 | tf_op jit(solution)/shard_map/ppermute | solution.py:364
  17.8 1.2 %collective-permute-done.18.refs_4_ = bf16[4,16,1024]{2,1,0:T(8,128)(2,1)S(1)} collective-permute-done((bf16[4,16,1024]{2,1,0:T(8,128)(2,1)S(1)}, bf16[4,16,1024]{2,1,0:T(8,128)(2,1)S(1)}, u32[]{:S(2)}, u32[]{:S(2)}) %collective-permute-start.18) | collective-permute-done | bytes 131104 | tf_op jit(solution)/shard_map/ppermute | solution.py:364
  19.0 1.9 %collective-permute-start.19 = (bf16[4,16,1024]{2,1,0:T(8,128)(2,1)S(1)}, bf16[4,16,1024]{2,1,0:T(8,128)(2,1)S(1)}, u32[]{:S(2)}, u32[]{:S(2)}) collective-permute-start(bf16[4,16,1024]{2,1,0:T(8,128)(2,1)S(1)} %collective-permute-done.18.refs_4_), channel_id=1, source_target_pairs={{0,2},{4,0},{8,4},{12,8},{14,12},{10,14},{6,10},{2,6},{1,3},{5,1},... | collective-permute-start | bytes 393224 | tf_op jit(solution)/shard_map/ppermute | solution.py:364
  20.9 1.6 %collective-permute-start.1 = (bf16[4,16,1024]{2,1,0:T(8,128)(2,1)S(1)}, bf16[4,16,1024]{2,1,0:T(8,128)(2,1)S(1)}, u32[]{:S(2)}, u32[]{:S(2)}) collective-permute-start(bf16[4,16,1024]{2,1,0:T(8,128)(2,1)S(1)} %edge.1.refs_1_), channel_id=1, source_target_pairs={{0,2},{4,0},{8,4},{12,8},{14,12},{10,14},{6,10},{2,6},{1,3},{5,1},... | collective-permute-start | bytes 393224 | tf_op jit(solution)/shard_map/ppermute | solution.py:364
  22.5 0.0 collective-permute-done.4.refs_8_
  22.5 0.5 collective-permute-start.5
  22.9 0.1 collective-permute-done.22.refs_6_
  23.0 1.2 %collective-permute-done.19.refs_5_ = bf16[4,16,1024]{2,1,0:T(8,128)(2,1)S(1)} collective-permute-done((bf16[4,16,1024]{2,1,0:T(8,128)(2,1)S(1)}, bf16[4,16,1024]{2,1,0:T(8,128)(2,1)S(1)}, u32[]{:S(2)}, u32[]{:S(2)}) %collective-permute-start.19) | collective-permute-done | bytes 131104 | tf_op jit(solution)/shard_map/ppermute | solution.py:364
  24.2 2.0 %shard_map.69 = (f32[520,128]{1,0:T(8,128)S(1)}, bf16[520,128]{1,0:T(8,128)(2,1)S(1)}, bf16[520,128]{1,0:T(8,128)(2,1)S(1)}, bf16[520,128]{1,0:T(8,128)(2,1)S(1)...) custom-call(bf16[6,128,1024]{2,1,0:T(8,128)(2,1)S(1)} %get-tuple-ele, ...), custom_call_target="tpu_custom_call" | custom-call | flops 1610612736 | bytes 3670016 | tf_op jit(solution)/shard_map/pallas_call | solution.py:252
  26.2 1.6 %collective-permute-start.26 = (bf16[520,128]{1,0:T(8,128)(2,1)S(1)}, bf16[520,128]{1,0:T(8,128)(2,1)}, u32[]{:S(2)}, u32[]{:S(2)}) collective-permute-start(bf16[520,128]{1,0:T(8,128)(2,1)S(1)} %get-tuple-element.45), channel_id=1, source_target_pairs={{0,2},{4,0},{8,4},{12,8},{14,12},{10,14},{6,10},{2,6},{1,3},{5,1},... | collective-permute-start | bytes 399368 | tf_op jit(solution)/shard_map/ppermute | solution.py:364
  27.9 0.0 collective-permute-done.1.refs_2_
  27.9 1.6 %collective-permute-start.2 = (bf16[4,16,1024]{2,1,0:T(8,128)(2,1)S(1)}, bf16[4,16,1024]{2,1,0:T(8,128)(2,1)S(1)}, u32[]{:S(2)}, u32[]{:S(2)}) collective-permute-start(bf16[4,16,1024]{2,1,0:T(8,128)(2,1)S(1)} %collective-permute-done.1.refs_2_), channel_id=1, source_target_pairs={{0,2},{4,0},{8,4},{12,8},{14,12},{10,14},{6,10},{2,6},{1,3},{5,1},... | collective-permute-start | bytes 393224 | tf_op jit(solution)/shard_map/ppermute | solution.py:364
  29.4 0.0 collective-permute-done.5.refs_7_
  29.4 0.4 collective-permute-start.6
  29.9 0.8 %collective-permute-start.23 = (bf16[520,128]{1,0:T(8,128)(2,1)S(1)}, bf16[520,128]{1,0:T(8,128)(2,1)S(1)}, u32[]{:S(2)}, u32[]{:S(2)}) collective-permute-start(bf16[520,128]{1,0:T(8,128)(2,1)S(1)} %get-tuple-element.41), channel_id=1, source_target_pairs={{0,4},{4,8},{8,12},{12,14},{14,10},{10,6},{6,2},{2,0},{1,5},{5,9},... | collective-permute-start | bytes 399368 | tf_op jit(solution)/shard_map/ppermute | solution.py:364
  30.7 3.5 %collective-permute-done.2.refs_3_ = bf16[4,16,1024]{2,1,0:T(8,128)(2,1)S(1)} collective-permute-done((bf16[4,16,1024]{2,1,0:T(8,128)(2,1)S(1)}, bf16[4,16,1024]{2,1,0:T(8,128)(2,1)S(1)}, u32[]{:S(2)}, u32[]{:S(2)}) %collective-permute-start.2) | collective-permute-done | bytes 131104 | tf_op jit(solution)/shard_map/ppermute | solution.py:364
  34.2 1.6 %collective-permute-start.3 = (bf16[4,16,1024]{2,1,0:T(8,128)(2,1)S(1)}, bf16[4,16,1024]{2,1,0:T(8,128)(2,1)S(1)}, u32[]{:S(2)}, u32[]{:S(2)}) collective-permute-start(bf16[4,16,1024]{2,1,0:T(8,128)(2,1)S(1)} %collective-permute-done.2.refs_3_), channel_id=1, source_target_pairs={{0,2},{4,0},{8,4},{12,8},{14,12},{10,14},{6,10},{2,6},{1,3},{5,1},... | collective-permute-start | bytes 393224 | tf_op jit(solution)/shard_map/ppermute | solution.py:364
  35.8 0.1 collective-permute-done.6.refs_6_
  35.9 0.4 collective-permute-start.7
  36.4 0.0 collective-permute-done.26
  36.4 0.9 %add_convert_fusion.2 = bf16[520,128]{1,0:T(8,128)(2,1)S(1)} fusion(bf16[520,128]{1,0:T(8,128)(2,1)} %collective-permute-done.26, bf16[520,128]{1,0:T(8,128)(2,1)S(1)} %get-tuple-element.44), kind=kLoop, calls=%fused_computation.2 | loop fusion | flops 266240 | bytes 399360 | tf_op jit(solution)/shard_map/convert_element_type | solution.py:340
  37.3 1.6 %collective-permute-start.27 = (bf16[520,128]{1,0:T(8,128)(2,1)S(1)}, bf16[520,128]{1,0:T(8,128)(2,1)S(1)}, u32[]{:S(2)}, u32[]{:S(2)}) collective-permute-start(bf16[520,128]{1,0:T(8,128)(2,1)S(1)} %add_convert_fusion.2), channel_id=1, source_target_pairs={{0,2},{4,0},{8,4},{12,8},{14,12},{10,14},{6,10},{2,6},{1,3},{5,1},... | collective-permute-start | bytes 399368 | tf_op jit(solution)/shard_map/ppermute | solution.py:364
  38.9 0.0 collective-permute-done.23
  39.0 0.5 collective-permute-start.24
  39.5 0.0 collective-permute-done.3.refs_4_
  39.5 1.9 %collective-permute-done.7.refs_5_ = bf16[4,16,1024]{2,1,0:T(8,128)(2,1)S(1)} collective-permute-done((bf16[4,16,1024]{2,1,0:T(8,128)(2,1)}, bf16[4,16,1024]{2,1,0:T(8,128)(2,1)S(1)}, u32[]{:S(2)}, u32[]{:S(2)}) %collective-permute-start.7) | collective-permute-done | bytes 131104 | tf_op jit(solution)/shard_map/ppermute | solution.py:364
  41.4 2.9 %shard_map.68 = (f32[520,128]{1,0:T(8,128)S(1)}, bf16[520,128]{1,0:T(8,128)(2,1)S(1)}, bf16[520,128]{1,0:T(8,128)(2,1)S(1)}, bf16[520,128]{1,0:T(8,128)(2,1)S(1)...) custom-call(bf16[6,128,1024]{2,1,0:T(8,128)(2,1)S(1)} %get-tuple-ele, ...), custom_call_target="tpu_custom_call" | custom-call | flops 1610612736 | bytes 3670016 | tf_op jit(solution)/shard_map/pallas_call | solution.py:252
  44.3 0.2 collective-permute-start.8
  44.5 1.8 %collective-permute-start.12 = (bf16[520,128]{1,0:T(8,128)(2,1)S(1)}, bf16[520,128]{1,0:T(8,128)(2,1)S(1)}, u32[]{:S(2)}, u32[]{:S(2)}) collective-permute-start(bf16[520,128]{1,0:T(8,128)(2,1)S(1)} %get-tuple-element.36), channel_id=1, source_target_pairs={{0,2},{4,0},{8,4},{12,8},{14,12},{10,14},{6,10},{2,6},{1,3},{5,1},... | collective-permute-start | bytes 399368 | tf_op jit(solution)/shard_map/ppermute | solution.py:364
  46.4 0.0 copy-start
  46.4 0.0 copy-start.1
  46.4 1.6 %collective-permute-start.28 = (bf16[520,128]{1,0:T(8,128)(2,1)S(1)}, bf16[520,128]{1,0:T(8,128)(2,1)S(1)}, u32[]{:S(2)}, u32[]{:S(2)}) collective-permute-start(bf16[520,128]{1,0:T(8,128)(2,1)S(1)} %add_convert_fusion.1), channel_id=1, source_target_pairs={{0,2},{4,0},{8,4},{12,8},{14,12},{10,14},{6,10},{2,6},{1,3},{5,1},... | collective-permute-start | bytes 399368 | tf_op jit(solution)/shard_map/ppermute | solution.py:364
  48.1 0.5 collective-permute-start.25
  48.6 0.7 %collective-permute-done.8 = bf16[520,128]{1,0:T(8,128)(2,1)S(1)} collective-permute-done((bf16[520,128]{1,0:T(8,128)(2,1)S(1)}, bf16[520,128]{1,0:T(8,128)(2,1)S(1)}, u32[]{:S(2)}, u32[]{:S(2)}) %collective-permute-start.8) | collective-permute-done | bytes 133152 | tf_op jit(solution)/shard_map/ppermute | solution.py:364
  49.3 0.3 collective-permute-start.9
  49.6 0.1 collective-permute-done.12
  49.7 1.8 %collective-permute-start.13 = (bf16[520,128]{1,0:T(8,128)(2,1)S(1)}, bf16[520,128]{1,0:T(8,128)(2,1)S(1)}, u32[]{:S(2)}, u32[]{:S(2)}) collective-permute-start(bf16[520,128]{1,0:T(8,128)(2,1)S(1)} %add_convert_fusion.6), channel_id=1, source_target_pairs={{0,2},{4,0},{8,4},{12,8},{14,12},{10,14},{6,10},{2,6},{1,3},{5,1},... | collective-permute-start | bytes 399368 | tf_op jit(solution)/shard_map/ppermute | solution.py:364
  51.5 3.9 %collective-permute-done.9 = bf16[520,128]{1,0:T(8,128)(2,1)S(1)} collective-permute-done((bf16[520,128]{1,0:T(8,128)(2,1)S(1)}, bf16[520,128]{1,0:T(8,128)(2,1)S(1)}, u32[]{:S(2)}, u32[]{:S(2)}) %collective-permute-start.9) | collective-permute-done | bytes 133152 | tf_op jit(solution)/shard_map/ppermute | solution.py:364
  55.5 0.4 collective-permute-start.10
  55.9 0.0 collective-permute-done.13
  55.9 1.7 %collective-permute-start.14 = (bf16[520,128]{1,0:T(8,128)(2,1)S(1)}, bf16[520,128]{1,0:T(8,128)(2,1)S(1)}, u32[]{:S(2)}, u32[]{:S(2)}) collective-permute-start(bf16[520,128]{1,0:T(8,128)(2,1)S(1)} %add_convert_fusion.5), channel_id=1, source_target_pairs={{0,2},{4,0},{8,4},{12,8},{14,12},{10,14},{6,10},{2,6},{1,3},{5,1},... | collective-permute-start | bytes 399368 | tf_op jit(solution)/shard_map/ppermute | solution.py:364
  57.7 2.9 %collective-permute-done.10 = bf16[520,128]{1,0:T(8,128)(2,1)S(1)} collective-permute-done((bf16[520,128]{1,0:T(8,128)(2,1)S(1)}, bf16[520,128]{1,0:T(8,128)(2,1)S(1)}, u32[]{:S(2)}, u32[]{:S(2)}) %collective-permute-start.10) | collective-permute-done | bytes 133152 | tf_op jit(solution)/shard_map/ppermute | solution.py:364
  60.6 0.4 collective-permute-start.11
  61.0 1.7 %collective-permute-start.29 = (bf16[520,128]{1,0:T(8,128)(2,1)S(1)}, bf16[520,128]{1,0:T(8,128)(2,1)S(1)}, u32[]{:S(2)}, u32[]{:S(2)}) collective-permute-start(bf16[520,128]{1,0:T(8,128)(2,1)S(1)} %add_convert_fusion), channel_id=1, source_target_pairs={{0,2},{4,0},{8,4},{12,8},{14,12},{10,14},{6,10},{2,6},{1,3},{5,1},... | collective-permute-start | bytes 399368 | tf_op jit(solution)/shard_map/ppermute | solution.py:364
  62.7 2.9 %collective-permute-done.11.refs_1_ = bf16[520,128]{1,0:T(8,128)(2,1)S(1)} collective-permute-done((bf16[520,128]{1,0:T(8,128)(2,1)S(1)}, bf16[520,128]{1,0:T(8,128)(2,1)S(1)}, u32[]{:S(2)}, u32[]{:S(2)}) %collective-permute-start.11) | collective-permute-done | bytes 133152 | tf_op jit(solution)/shard_map/ppermute | solution.py:364
  65.6 0.1 collective-permute-start.15
  65.7 0.0 collective-permute-done.25.refs_4_
  65.7 0.4 collective-permute-done.29.refs_5_
  66.1 0.8 %collective-permute-done.15.edge_ref = bf16[128,128]{1,0:T(8,128)(2,1)S(1)} collective-permute-done((bf16[128,128]{1,0:T(8,128)(2,1)S(1)}, bf16[128,128]{1,0:T(8,128)(2,1)S(1)}, u32[]{:S(2)}, u32[]{:S(2)}) %collective-permute-start.15) | collective-permute-done | bytes 32800 | tf_op jit(solution)/shard_map/ppermute | solution.py:336
  66.9 1.6 %parents.1 = (bf16[16,8,1024]{2,1,0:T(8,128)(2,1)}, f32[1,8]{1,0:T(1,128)}) custom-call(s32[16]{0:T(128)S(1)} %copy-done, s32[8]{0:T(128)S(1)} %copy-done.1, bf16[128,128]{1,0:T(8,128)(2,1)S(1)} %collective-permute-done.15.edge_ref, f32[520,128]{1,0:T(8,128)S(1)} %get-tuple-element.29.refs_0_, bf16[520,128]{1,0:T(8,128)(2,1)S(1)} %collective-permute-done.11.refs_1_, ...), custom_call_target="tpu_custom_call" | custom-call | flops 786432 | bytes 1310720 | tf_op jit(solution)/shard_map/parents/pallas_call | solution.py:313
  (18 shorter events, 0.4 us)
Async XLA Ops:
  0.6 4.7 %copy-start.2 = (bf16[16,8,1024]{2,1,0:T(8,128)(2,1)S(1)}, bf16[16,8,1024]{2,1,0:T(8,128)(2,1)}, u32[]{:S(2)}) copy-start(bf16[16,8,1024]{2,1,0:T(8,128)(2,1)} %green_any.1) | copy-start | bytes 786436
  2.3 6.6 %collective-permute-start.16 = (bf16[4,16,1024]{2,1,0:T(8,128)(2,1)S(1)}, bf16[4,16,1024]{2,1,0:T(8,128)(2,1)S(1)}, u32[]{:S(2)}, u32[]{:S(2)}) collective-permute-start(bf16[4,16,1024]{2,1,0:T(8,128)(2,1)S(1)} %get-tuple-element.37.refs_1_), channel_id=1, source_target_pairs={{0,2},{4,0},{8,4},{12,8},{14,12},{10,14},{6,10},{2,6},{1,3},{5,1},... | collective-permute-start | bytes 393224 | tf_op jit(solution)/shard_map/ppermute | solution.py:364
  5.3 10.2 %collective-permute-start = (bf16[16,8,1024]{2,1,0:T(8,128)(2,1)S(1)}, bf16[16,8,1024]{2,1,0:T(8,128)(2,1)S(1)}, u32[]{:S(2)}, u32[]{:S(2)}) collective-permute-start(bf16[16,8,1024]{2,1,0:T(8,128)(2,1)S(1)} %copy-done.2), channel_id=1, source_target_pairs={{0,1},{1,0},{2,3},{3,2},{4,5},{5,4},{6,7},{7,6},{8,9},{9,8},{10,11... | collective-permute-start | bytes 786440 | tf_op jit(solution)/shard_map/ppermute | solution.py:336
  5.3 5.9 %collective-permute-start.20 = (bf16[4,16,1024]{2,1,0:T(8,128)(2,1)S(1)}, bf16[4,16,1024]{2,1,0:T(8,128)(2,1)S(1)}, u32[]{:S(2)}, u32[]{:S(2)}) collective-permute-start(bf16[4,16,1024]{2,1,0:T(8,128)(2,1)S(1)} %get-tuple-element.37.refs_1_), channel_id=1, source_target_pairs={{0,4},{4,8},{8,12},{12,14},{14,10},{10,6},{6,2},{2,0},{1,5},{5,9},... | collective-permute-start | bytes 393224 | tf_op jit(solution)/shard_map/ppermute | solution.py:364
  8.9 5.0 %collective-permute-start.17 = (bf16[4,16,1024]{2,1,0:T(8,128)(2,1)S(1)}, bf16[4,16,1024]{2,1,0:T(8,128)(2,1)S(1)}, u32[]{:S(2)}, u32[]{:S(2)}) collective-permute-start(bf16[4,16,1024]{2,1,0:T(8,128)(2,1)S(1)} %collective-permute-done.16.refs_2_), channel_id=1, source_target_pairs={{0,2},{4,0},{8,4},{12,8},{14,12},{10,14},{6,10},{2,6},{1,3},{5,1},... | collective-permute-start | bytes 393224 | tf_op jit(solution)/shard_map/ppermute | solution.py:364
  11.2 5.5 %collective-permute-start.21 = (bf16[4,16,1024]{2,1,0:T(8,128)(2,1)S(1)}, bf16[4,16,1024]{2,1,0:T(8,128)(2,1)S(1)}, u32[]{:S(2)}, u32[]{:S(2)}) collective-permute-start(bf16[4,16,1024]{2,1,0:T(8,128)(2,1)S(1)} %collective-permute-done.20.refs_8_), channel_id=1, source_target_pairs={{0,4},{4,8},{8,12},{12,14},{14,10},{10,6},{6,2},{2,0},{1,5},{5,9},... | collective-permute-start | bytes 393224 | tf_op jit(solution)/shard_map/ppermute | solution.py:364
  13.9 5.1 %collective-permute-start.18 = (bf16[4,16,1024]{2,1,0:T(8,128)(2,1)S(1)}, bf16[4,16,1024]{2,1,0:T(8,128)(2,1)S(1)}, u32[]{:S(2)}, u32[]{:S(2)}) collective-permute-start(bf16[4,16,1024]{2,1,0:T(8,128)(2,1)S(1)} %collective-permute-done.17.refs_3_), channel_id=1, source_target_pairs={{0,2},{4,0},{8,4},{12,8},{14,12},{10,14},{6,10},{2,6},{1,3},{5,1},... | collective-permute-start | bytes 393224 | tf_op jit(solution)/shard_map/ppermute | solution.py:364
  15.6 6.9 %collective-permute-start.4 = (bf16[4,16,1024]{2,1,0:T(8,128)(2,1)S(1)}, bf16[4,16,1024]{2,1,0:T(8,128)(2,1)S(1)}, u32[]{:S(2)}, u32[]{:S(2)}) collective-permute-start(bf16[4,16,1024]{2,1,0:T(8,128)(2,1)S(1)} %edge.1.refs_1_), channel_id=1, source_target_pairs={{0,4},{4,8},{8,12},{12,14},{14,10},{10,6},{6,2},{2,0},{1,5},{5,9},... | collective-permute-start | bytes 393224 | tf_op jit(solution)/shard_map/ppermute | solution.py:364
  16.7 6.3 %collective-permute-start.22 = (bf16[4,16,1024]{2,1,0:T(8,128)(2,1)S(1)}, bf16[4,16,1024]{2,1,0:T(8,128)(2,1)S(1)}, u32[]{:S(2)}, u32[]{:S(2)}) collective-permute-start(bf16[4,16,1024]{2,1,0:T(8,128)(2,1)S(1)} %collective-permute-done.21.refs_7_), channel_id=1, source_target_pairs={{0,4},{4,8},{8,12},{12,14},{14,10},{10,6},{6,2},{2,0},{1,5},{5,9},... | collective-permute-start | bytes 393224 | tf_op jit(solution)/shard_map/ppermute | solution.py:364
  19.0 5.3 %collective-permute-start.19 = (bf16[4,16,1024]{2,1,0:T(8,128)(2,1)S(1)}, bf16[4,16,1024]{2,1,0:T(8,128)(2,1)S(1)}, u32[]{:S(2)}, u32[]{:S(2)}) collective-permute-start(bf16[4,16,1024]{2,1,0:T(8,128)(2,1)S(1)} %collective-permute-done.18.refs_4_), channel_id=1, source_target_pairs={{0,2},{4,0},{8,4},{12,8},{14,12},{10,14},{6,10},{2,6},{1,3},{5,1},... | collective-permute-start | bytes 393224 | tf_op jit(solution)/shard_map/ppermute | solution.py:364
  20.9 6.9 %collective-permute-start.1 = (bf16[4,16,1024]{2,1,0:T(8,128)(2,1)S(1)}, bf16[4,16,1024]{2,1,0:T(8,128)(2,1)S(1)}, u32[]{:S(2)}, u32[]{:S(2)}) collective-permute-start(bf16[4,16,1024]{2,1,0:T(8,128)(2,1)S(1)} %edge.1.refs_1_), channel_id=1, source_target_pairs={{0,2},{4,0},{8,4},{12,8},{14,12},{10,14},{6,10},{2,6},{1,3},{5,1},... | collective-permute-start | bytes 393224 | tf_op jit(solution)/shard_map/ppermute | solution.py:364
  22.5 6.9 %collective-permute-start.5 = (bf16[4,16,1024]{2,1,0:T(8,128)(2,1)S(1)}, bf16[4,16,1024]{2,1,0:T(8,128)(2,1)S(1)}, u32[]{:S(2)}, u32[]{:S(2)}) collective-permute-start(bf16[4,16,1024]{2,1,0:T(8,128)(2,1)S(1)} %collective-permute-done.4.refs_8_), channel_id=1, source_target_pairs={{0,4},{4,8},{8,12},{12,14},{14,10},{10,6},{6,2},{2,0},{1,5},{5,9},... | collective-permute-start | bytes 393224 | tf_op jit(solution)/shard_map/ppermute | solution.py:364
  26.2 10.2 %collective-permute-start.26 = (bf16[520,128]{1,0:T(8,128)(2,1)S(1)}, bf16[520,128]{1,0:T(8,128)(2,1)}, u32[]{:S(2)}, u32[]{:S(2)}) collective-permute-start(bf16[520,128]{1,0:T(8,128)(2,1)S(1)} %get-tuple-element.45), channel_id=1, source_target_pairs={{0,2},{4,0},{8,4},{12,8},{14,12},{10,14},{6,10},{2,6},{1,3},{5,1},... | collective-permute-start | bytes 399368 | tf_op jit(solution)/shard_map/ppermute | solution.py:364
  27.9 6.4 %collective-permute-start.2 = (bf16[4,16,1024]{2,1,0:T(8,128)(2,1)S(1)}, bf16[4,16,1024]{2,1,0:T(8,128)(2,1)S(1)}, u32[]{:S(2)}, u32[]{:S(2)}) collective-permute-start(bf16[4,16,1024]{2,1,0:T(8,128)(2,1)S(1)} %collective-permute-done.1.refs_2_), channel_id=1, source_target_pairs={{0,2},{4,0},{8,4},{12,8},{14,12},{10,14},{6,10},{2,6},{1,3},{5,1},... | collective-permute-start | bytes 393224 | tf_op jit(solution)/shard_map/ppermute | solution.py:364
  29.4 6.5 %collective-permute-start.6 = (bf16[4,16,1024]{2,1,0:T(8,128)(2,1)S(1)}, bf16[4,16,1024]{2,1,0:T(8,128)(2,1)}, u32[]{:S(2)}, u32[]{:S(2)}) collective-permute-start(bf16[4,16,1024]{2,1,0:T(8,128)(2,1)S(1)} %collective-permute-done.5.refs_7_), channel_id=1, source_target_pairs={{0,4},{4,8},{8,12},{12,14},{14,10},{10,6},{6,2},{2,0},{1,5},{5,9},... | collective-permute-start | bytes 393224 | tf_op jit(solution)/shard_map/ppermute | solution.py:364
  29.9 9.1 %collective-permute-start.23 = (bf16[520,128]{1,0:T(8,128)(2,1)S(1)}, bf16[520,128]{1,0:T(8,128)(2,1)S(1)}, u32[]{:S(2)}, u32[]{:S(2)}) collective-permute-start(bf16[520,128]{1,0:T(8,128)(2,1)S(1)} %get-tuple-element.41), channel_id=1, source_target_pairs={{0,4},{4,8},{8,12},{12,14},{14,10},{10,6},{6,2},{2,0},{1,5},{5,9},... | collective-permute-start | bytes 399368 | tf_op jit(solution)/shard_map/ppermute | solution.py:364
  34.2 5.3 %collective-permute-start.3 = (bf16[4,16,1024]{2,1,0:T(8,128)(2,1)S(1)}, bf16[4,16,1024]{2,1,0:T(8,128)(2,1)S(1)}, u32[]{:S(2)}, u32[]{:S(2)}) collective-permute-start(bf16[4,16,1024]{2,1,0:T(8,128)(2,1)S(1)} %collective-permute-done.2.refs_3_), channel_id=1, source_target_pairs={{0,2},{4,0},{8,4},{12,8},{14,12},{10,14},{6,10},{2,6},{1,3},{5,1},... | collective-permute-start | bytes 393224 | tf_op jit(solution)/shard_map/ppermute | solution.py:364
  35.9 5.5 %collective-permute-start.7 = (bf16[4,16,1024]{2,1,0:T(8,128)(2,1)}, bf16[4,16,1024]{2,1,0:T(8,128)(2,1)S(1)}, u32[]{:S(2)}, u32[]{:S(2)}) collective-permute-start(bf16[4,16,1024]{2,1,0:T(8,128)(2,1)} %collective-permute-done.6.refs_6_), channel_id=1, source_target_pairs={{0,4},{4,8},{8,12},{12,14},{14,10},{10,6},{6,2},{2,0},{1,5},{5,9},... | collective-permute-start | bytes 393224 | tf_op jit(solution)/shard_map/ppermute | solution.py:364
  37.3 9.0 %collective-permute-start.27 = (bf16[520,128]{1,0:T(8,128)(2,1)S(1)}, bf16[520,128]{1,0:T(8,128)(2,1)S(1)}, u32[]{:S(2)}, u32[]{:S(2)}) collective-permute-start(bf16[520,128]{1,0:T(8,128)(2,1)S(1)} %add_convert_fusion.2), channel_id=1, source_target_pairs={{0,2},{4,0},{8,4},{12,8},{14,12},{10,14},{6,10},{2,6},{1,3},{5,1},... | collective-permute-start | bytes 399368 | tf_op jit(solution)/shard_map/ppermute | solution.py:364
  39.0 9.0 %collective-permute-start.24 = (bf16[520,128]{1,0:T(8,128)(2,1)S(1)}, bf16[520,128]{1,0:T(8,128)(2,1)S(1)}, u32[]{:S(2)}, u32[]{:S(2)}) collective-permute-start(bf16[520,128]{1,0:T(8,128)(2,1)S(1)} %add_convert_fusion.4), channel_id=1, source_target_pairs={{0,4},{4,8},{8,12},{12,14},{14,10},{10,6},{6,2},{2,0},{1,5},{5,9},... | collective-permute-start | bytes 399368 | tf_op jit(solution)/shard_map/ppermute | solution.py:364
  44.3 5.0 %collective-permute-start.8 = (bf16[520,128]{1,0:T(8,128)(2,1)S(1)}, bf16[520,128]{1,0:T(8,128)(2,1)S(1)}, u32[]{:S(2)}, u32[]{:S(2)}) collective-permute-start(bf16[520,128]{1,0:T(8,128)(2,1)S(1)} %get-tuple-element.33), channel_id=1, source_target_pairs={{0,4},{4,8},{8,12},{12,14},{14,10},{10,6},{6,2},{2,0},{1,5},{5,9},... | collective-permute-start | bytes 399368 | tf_op jit(solution)/shard_map/ppermute | solution.py:364
  44.5 5.2 %collective-permute-start.12 = (bf16[520,128]{1,0:T(8,128)(2,1)S(1)}, bf16[520,128]{1,0:T(8,128)(2,1)S(1)}, u32[]{:S(2)}, u32[]{:S(2)}) collective-permute-start(bf16[520,128]{1,0:T(8,128)(2,1)S(1)} %get-tuple-element.36), channel_id=1, source_target_pairs={{0,2},{4,0},{8,4},{12,8},{14,12},{10,14},{6,10},{2,6},{1,3},{5,1},... | collective-permute-start | bytes 399368 | tf_op jit(solution)/shard_map/ppermute | solution.py:364
  46.4 20.5 %copy-start = (s32[16]{0:T(128)S(1)}, s32[16]{0:T(128)}, u32[]{:S(2)}) copy-start(s32[16]{0:T(128)} %parents_ref.1) | copy-start | bytes 196
  46.4 20.5 %copy-start.1 = (s32[8]{0:T(128)S(1)}, s32[8]{0:T(128)}, u32[]{:S(2)}) copy-start(s32[8]{0:T(128)} %counts_ref.1) | copy-start | bytes 100
  46.4 14.6 %collective-permute-start.28 = (bf16[520,128]{1,0:T(8,128)(2,1)S(1)}, bf16[520,128]{1,0:T(8,128)(2,1)S(1)}, u32[]{:S(2)}, u32[]{:S(2)}) collective-permute-start(bf16[520,128]{1,0:T(8,128)(2,1)S(1)} %add_convert_fusion.1), channel_id=1, source_target_pairs={{0,2},{4,0},{8,4},{12,8},{14,12},{10,14},{6,10},{2,6},{1,3},{5,1},... | collective-permute-start | bytes 399368 | tf_op jit(solution)/shard_map/ppermute | solution.py:364
  48.1 17.6 %collective-permute-start.25 = (bf16[520,128]{1,0:T(8,128)(2,1)S(1)}, bf16[520,128]{1,0:T(8,128)(2,1)S(1)}, u32[]{:S(2)}, u32[]{:S(2)}) collective-permute-start(bf16[520,128]{1,0:T(8,128)(2,1)S(1)} %add_convert_fusion.3), channel_id=1, source_target_pairs={{0,4},{4,8},{8,12},{12,14},{14,10},{10,6},{6,2},{2,0},{1,5},{5,9},... | collective-permute-start | bytes 399368 | tf_op jit(solution)/shard_map/ppermute | solution.py:364
  49.3 6.1 %collective-permute-start.9 = (bf16[520,128]{1,0:T(8,128)(2,1)S(1)}, bf16[520,128]{1,0:T(8,128)(2,1)S(1)}, u32[]{:S(2)}, u32[]{:S(2)}) collective-permute-start(bf16[520,128]{1,0:T(8,128)(2,1)S(1)} %add_convert_fusion.9), channel_id=1, source_target_pairs={{0,4},{4,8},{8,12},{12,14},{14,10},{10,6},{6,2},{2,0},{1,5},{5,9},... | collective-permute-start | bytes 399368 | tf_op jit(solution)/shard_map/ppermute | solution.py:364
  49.7 6.2 %collective-permute-start.13 = (bf16[520,128]{1,0:T(8,128)(2,1)S(1)}, bf16[520,128]{1,0:T(8,128)(2,1)S(1)}, u32[]{:S(2)}, u32[]{:S(2)}) collective-permute-start(bf16[520,128]{1,0:T(8,128)(2,1)S(1)} %add_convert_fusion.6), channel_id=1, source_target_pairs={{0,2},{4,0},{8,4},{12,8},{14,12},{10,14},{6,10},{2,6},{1,3},{5,1},... | collective-permute-start | bytes 399368 | tf_op jit(solution)/shard_map/ppermute | solution.py:364
  55.5 5.0 %collective-permute-start.10 = (bf16[520,128]{1,0:T(8,128)(2,1)S(1)}, bf16[520,128]{1,0:T(8,128)(2,1)S(1)}, u32[]{:S(2)}, u32[]{:S(2)}) collective-permute-start(bf16[520,128]{1,0:T(8,128)(2,1)S(1)} %add_convert_fusion.8), channel_id=1, source_target_pairs={{0,4},{4,8},{8,12},{12,14},{14,10},{10,6},{6,2},{2,0},{1,5},{5,9},... | collective-permute-start | bytes 399368 | tf_op jit(solution)/shard_map/ppermute | solution.py:364
  55.9 6.8 %collective-permute-start.14 = (bf16[520,128]{1,0:T(8,128)(2,1)S(1)}, bf16[520,128]{1,0:T(8,128)(2,1)S(1)}, u32[]{:S(2)}, u32[]{:S(2)}) collective-permute-start(bf16[520,128]{1,0:T(8,128)(2,1)S(1)} %add_convert_fusion.5), channel_id=1, source_target_pairs={{0,2},{4,0},{8,4},{12,8},{14,12},{10,14},{6,10},{2,6},{1,3},{5,1},... | collective-permute-start | bytes 399368 | tf_op jit(solution)/shard_map/ppermute | solution.py:364
  60.6 5.0 %collective-permute-start.11 = (bf16[520,128]{1,0:T(8,128)(2,1)S(1)}, bf16[520,128]{1,0:T(8,128)(2,1)S(1)}, u32[]{:S(2)}, u32[]{:S(2)}) collective-permute-start(bf16[520,128]{1,0:T(8,128)(2,1)S(1)} %add_convert_fusion.7), channel_id=1, source_target_pairs={{0,4},{4,8},{8,12},{12,14},{14,10},{10,6},{6,2},{2,0},{1,5},{5,9},... | collective-permute-start | bytes 399368 | tf_op jit(solution)/shard_map/ppermute | solution.py:364
  61.0 5.0 %collective-permute-start.29 = (bf16[520,128]{1,0:T(8,128)(2,1)S(1)}, bf16[520,128]{1,0:T(8,128)(2,1)S(1)}, u32[]{:S(2)}, u32[]{:S(2)}) collective-permute-start(bf16[520,128]{1,0:T(8,128)(2,1)S(1)} %add_convert_fusion), channel_id=1, source_target_pairs={{0,2},{4,0},{8,4},{12,8},{14,12},{10,14},{6,10},{2,6},{1,3},{5,1},... | collective-permute-start | bytes 399368 | tf_op jit(solution)/shard_map/ppermute | solution.py:364
  65.6 1.3 %collective-permute-start.15 = (bf16[128,128]{1,0:T(8,128)(2,1)S(1)}, bf16[128,128]{1,0:T(8,128)(2,1)S(1)}, u32[]{:S(2)}, u32[]{:S(2)}) collective-permute-start(bf16[128,128]{1,0:T(8,128)(2,1)S(1)} %add_convert_fusion.10), channel_id=1, source_target_pairs={{0,1},{1,0},{2,3},{3,2},{4,5},{5,4},{6,7},{7,6},{8,9},{9,8},{10,11... | collective-permute-start | bytes 98312 | tf_op jit(solution)/shard_map/ppermute | solution.py:336

commit v6 on v5

--- a/solution.py
+++ b/solution.py
@@ -346,10 +346,10 @@
     for s in range(1, half):
         order += [("gather", s, g, way) for g in (0, 1) for way in ("up", "down")]
     order += [("gather", half, 0, "up"), ("gather", half, 1, "down")]
-    order += [("sum", 1, 0, "up"), ("sum", 1, 1, "down")]
     for s in range(1, half):
-        order += [("sum", s + 1, 0, "up"), ("sum", s, 0, "down")]
-        order += [("sum", s, 1, "up"), ("sum", s + 1, 1, "down")]
+        order += [("sum", s, 0, "up"), ("sum", s, 1, "down")]
+        order += [("sum", s, 1, "up"), ("sum", s, 0, "down")]
+    order += [("sum", half, 0, "up"), ("sum", half, 1, "down")]
     return order
 
 

time: 68.7 us -> 68.7 us (level)
  no operation moved by 1% of the time
where the time goes in v6:
time: 68.7 us; the launch traced here: 68.5 us
  starting transfers between devices  31.5 us (46%)
  waiting for transfers between devices  26.7 us (39%)
  Pallas kernels  8.22 us (12%)
  other arithmetic  1.3 us (2%)
  between operations  0.75 us (1%)
    ppermute x28, starting transfers between devices, hop(): return lax.ppermute(x, 'chol', pairs[key[3]])  31.4 us
    ppermute x28, waiting for transfers between devices, hop(): return lax.ppermute(x, 'chol', pairs[key[3]])  25.9 us
    pallas_call x2, Pallas kernels, partial_forces(): pl.pallas_call(functools.partial(force_kernel, -0.125 / (total * orbitals...  4.84 us
    pallas_call x1, Pallas kernels, make_children(): pl.pallas_call(functools.partial(children_kernel, n), out_shape=[jax.Shap...  1.64 us
    pallas_call x1, Pallas kernels, parent_forces(): pl.pallas_call(functools.partial(parents_kernel, factor, size), out_shape...  1.64 us
  transfers between devices with their start and end apart: 30, of which 17 were waited for; matrix products, arithmetic and copies ran while one was open for 2% of the time, Pallas kernels for 7%

profile of v6, /device:TPU:0, one launch (start us, length us, event | category | flops | bytes accessed | tf_op | source)
XLA Modules:
  0.0 68.5 jit_solution(31094511024166597)
XLA Ops:
  0.6 1.6 %children.1 = (bf16[4,16,1024]{2,1,0:T(8,128)(2,1)S(1)}, bf16[4,16,1024]{2,1,0:T(8,128)(2,1)S(1)}, bf16[6,128,1024]{2,1,0:T(8,128)(2,1)S(1)}, f32[16,1024]{1,0:T(8,128)S(1)}, f32[16,128]{1,0:T(8,128)S(1)}) custom-call(s32[16]{0:T(128)} %parents_ref.1, bf16[16,8,1024]{2,1,0:T(8,128)(2,1)} %green_any.1, bf16[16,8,1024]{2,1,0:T(8,128)(2,1)} %delta_any.1, ...), custom_call_target="tpu_custom_call" | custom-call | flops 131072 | bytes 786432 | tf_op jit(solution)/shard_map/children/pallas_call | solution.py:154
  2.3 3.0 %collective-permute-start.16 = (bf16[4,16,1024]{2,1,0:T(8,128)(2,1)S(1)}, bf16[4,16,1024]{2,1,0:T(8,128)(2,1)S(1)}, u32[]{:S(2)}, u32[]{:S(2)}) collective-permute-start(bf16[4,16,1024]{2,1,0:T(8,128)(2,1)S(1)} %get-tuple-element.37.refs_1_), channel_id=1, source_target_pairs={{0,2},{4,0},{8,4},{12,8},{14,12},{10,14},{6,10},{2,6},{1,3},{5,1},... | collective-permute-start | bytes 393224 | tf_op jit(solution)/shard_map/ppermute | solution.py:364
  5.3 0.0 collective-permute-start
  5.3 0.2 collective-permute-start.20
  5.6 3.3 %collective-permute-done.16.refs_2_ = bf16[4,16,1024]{2,1,0:T(8,128)(2,1)S(1)} collective-permute-done((bf16[4,16,1024]{2,1,0:T(8,128)(2,1)S(1)}, bf16[4,16,1024]{2,1,0:T(8,128)(2,1)S(1)}, u32[]{:S(2)}, u32[]{:S(2)}) %collective-permute-start.16) | collective-permute-done | bytes 131104 | tf_op jit(solution)/shard_map/ppermute | solution.py:364
  8.9 1.7 %collective-permute-start.17 = (bf16[4,16,1024]{2,1,0:T(8,128)(2,1)S(1)}, bf16[4,16,1024]{2,1,0:T(8,128)(2,1)S(1)}, u32[]{:S(2)}, u32[]{:S(2)}) collective-permute-start(bf16[4,16,1024]{2,1,0:T(8,128)(2,1)S(1)} %collective-permute-done.16.refs_2_), channel_id=1, source_target_pairs={{0,2},{4,0},{8,4},{12,8},{14,12},{10,14},{6,10},{2,6},{1,3},{5,1},... | collective-permute-start | bytes 393224 | tf_op jit(solution)/shard_map/ppermute | solution.py:364
  10.5 0.7 collective-permute-done.20.refs_8_
  11.2 0.3 collective-permute-start.21
  11.5 2.4 %collective-permute-done.17.refs_3_ = bf16[4,16,1024]{2,1,0:T(8,128)(2,1)S(1)} collective-permute-done((bf16[4,16,1024]{2,1,0:T(8,128)(2,1)S(1)}, bf16[4,16,1024]{2,1,0:T(8,128)(2,1)S(1)}, u32[]{:S(2)}, u32[]{:S(2)}) %collective-permute-start.17) | collective-permute-done | bytes 131104 | tf_op jit(solution)/shard_map/ppermute | solution.py:364
  13.9 1.7 %collective-permute-start.18 = (bf16[4,16,1024]{2,1,0:T(8,128)(2,1)S(1)}, bf16[4,16,1024]{2,1,0:T(8,128)(2,1)S(1)}, u32[]{:S(2)}, u32[]{:S(2)}) collective-permute-start(bf16[4,16,1024]{2,1,0:T(8,128)(2,1)S(1)} %collective-permute-done.17.refs_3_), channel_id=1, source_target_pairs={{0,2},{4,0},{8,4},{12,8},{14,12},{10,14},{6,10},{2,6},{1,3},{5,1},... | collective-permute-start | bytes 393224 | tf_op jit(solution)/shard_map/ppermute | solution.py:364
  15.5 0.0 collective-permute-done.other_ref
  15.5 0.1 edge.1.refs_1_
  15.6 0.4 collective-permute-start.4
  16.0 0.7 collective-permute-done.21.refs_7_
  16.7 1.1 %collective-permute-start.22 = (bf16[4,16,1024]{2,1,0:T(8,128)(2,1)S(1)}, bf16[4,16,1024]{2,1,0:T(8,128)(2,1)S(1)}, u32[]{:S(2)}, u32[]{:S(2)}) collective-permute-start(bf16[4,16,1024]{2,1,0:T(8,128)(2,1)S(1)} %collective-permute-done.21.refs_7_), channel_id=1, source_target_pairs={{0,4},{4,8},{8,12},{12,14},{14,10},{10,6},{6,2},{2,0},{1,5},{5,9},... | collective-permute-start | bytes 393224 | tf_op jit(solution)/shard_map/ppermute | solution.py:364
  17.8 1.2 %collective-permute-done.18.refs_4_ = bf16[4,16,1024]{2,1,0:T(8,128)(2,1)S(1)} collective-permute-done((bf16[4,16,1024]{2,1,0:T(8,128)(2,1)S(1)}, bf16[4,16,1024]{2,1,0:T(8,128)(2,1)S(1)}, u32[]{:S(2)}, u32[]{:S(2)}) %collective-permute-start.18) | collective-permute-done | bytes 131104 | tf_op jit(solution)/shard_map/ppermute | solution.py:364
  19.0 1.9 %collective-permute-start.19 = (bf16[4,16,1024]{2,1,0:T(8,128)(2,1)S(1)}, bf16[4,16,1024]{2,1,0:T(8,128)(2,1)S(1)}, u32[]{:S(2)}, u32[]{:S(2)}) collective-permute-start(bf16[4,16,1024]{2,1,0:T(8,128)(2,1)S(1)} %collective-permute-done.18.refs_4_), channel_id=1, source_target_pairs={{0,2},{4,0},{8,4},{12,8},{14,12},{10,14},{6,10},{2,6},{1,3},{5,1},... | collective-permute-start | bytes 393224 | tf_op jit(solution)/shard_map/ppermute | solution.py:364
  20.9 1.6 %collective-permute-start.1 = (bf16[4,16,1024]{2,1,0:T(8,128)(2,1)S(1)}, bf16[4,16,1024]{2,1,0:T(8,128)(2,1)S(1)}, u32[]{:S(2)}, u32[]{:S(2)}) collective-permute-start(bf16[4,16,1024]{2,1,0:T(8,128)(2,1)S(1)} %edge.1.refs_1_), channel_id=1, source_target_pairs={{0,2},{4,0},{8,4},{12,8},{14,12},{10,14},{6,10},{2,6},{1,3},{5,1},... | collective-permute-start | bytes 393224 | tf_op jit(solution)/shard_map/ppermute | solution.py:364
  22.5 0.0 collective-permute-done.4.refs_8_
  22.5 0.5 collective-permute-start.5
  22.9 0.1 collective-permute-done.22.refs_6_
  23.0 1.2 %collective-permute-done.19.refs_5_ = bf16[4,16,1024]{2,1,0:T(8,128)(2,1)S(1)} collective-permute-done((bf16[4,16,1024]{2,1,0:T(8,128)(2,1)S(1)}, bf16[4,16,1024]{2,1,0:T(8,128)(2,1)S(1)}, u32[]{:S(2)}, u32[]{:S(2)}) %collective-permute-start.19) | collective-permute-done | bytes 131104 | tf_op jit(solution)/shard_map/ppermute | solution.py:364
  24.2 2.0 %shard_map.69 = (f32[520,128]{1,0:T(8,128)S(1)}, bf16[520,128]{1,0:T(8,128)(2,1)S(1)}, bf16[520,128]{1,0:T(8,128)(2,1)S(1)}, bf16[520,128]{1,0:T(8,128)(2,1)S(1)...) custom-call(bf16[6,128,1024]{2,1,0:T(8,128)(2,1)S(1)} %get-tuple-ele, ...), custom_call_target="tpu_custom_call" | custom-call | flops 1610612736 | bytes 3670016 | tf_op jit(solution)/shard_map/pallas_call | solution.py:252
  26.2 1.6 %collective-permute-start.26 = (bf16[520,128]{1,0:T(8,128)(2,1)S(1)}, bf16[520,128]{1,0:T(8,128)(2,1)}, u32[]{:S(2)}, u32[]{:S(2)}) collective-permute-start(bf16[520,128]{1,0:T(8,128)(2,1)S(1)} %get-tuple-element.45), channel_id=1, source_target_pairs={{0,2},{4,0},{8,4},{12,8},{14,12},{10,14},{6,10},{2,6},{1,3},{5,1},... | collective-permute-start | bytes 399368 | tf_op jit(solution)/shard_map/ppermute | solution.py:364
  27.9 0.0 collective-permute-done.1.refs_2_
  27.9 1.6 %collective-permute-start.2 = (bf16[4,16,1024]{2,1,0:T(8,128)(2,1)S(1)}, bf16[4,16,1024]{2,1,0:T(8,128)(2,1)S(1)}, u32[]{:S(2)}, u32[]{:S(2)}) collective-permute-start(bf16[4,16,1024]{2,1,0:T(8,128)(2,1)S(1)} %collective-permute-done.1.refs_2_), channel_id=1, source_target_pairs={{0,2},{4,0},{8,4},{12,8},{14,12},{10,14},{6,10},{2,6},{1,3},{5,1},... | collective-permute-start | bytes 393224 | tf_op jit(solution)/shard_map/ppermute | solution.py:364
  29.4 0.0 collective-permute-done.5.refs_7_
  29.4 0.4 collective-permute-start.6
  29.9 0.8 %collective-permute-start.23 = (bf16[520,128]{1,0:T(8,128)(2,1)S(1)}, bf16[520,128]{1,0:T(8,128)(2,1)S(1)}, u32[]{:S(2)}, u32[]{:S(2)}) collective-permute-start(bf16[520,128]{1,0:T(8,128)(2,1)S(1)} %get-tuple-element.41), channel_id=1, source_target_pairs={{0,4},{4,8},{8,12},{12,14},{14,10},{10,6},{6,2},{2,0},{1,5},{5,9},... | collective-permute-start | bytes 399368 | tf_op jit(solution)/shard_map/ppermute | solution.py:364
  30.7 3.5 %collective-permute-done.2.refs_3_ = bf16[4,16,1024]{2,1,0:T(8,128)(2,1)S(1)} collective-permute-done((bf16[4,16,1024]{2,1,0:T(8,128)(2,1)S(1)}, bf16[4,16,1024]{2,1,0:T(8,128)(2,1)S(1)}, u32[]{:S(2)}, u32[]{:S(2)}) %collective-permute-start.2) | collective-permute-done | bytes 131104 | tf_op jit(solution)/shard_map/ppermute | solution.py:364
  34.2 1.6 %collective-permute-start.3 = (bf16[4,16,1024]{2,1,0:T(8,128)(2,1)S(1)}, bf16[4,16,1024]{2,1,0:T(8,128)(2,1)S(1)}, u32[]{:S(2)}, u32[]{:S(2)}) collective-permute-start(bf16[4,16,1024]{2,1,0:T(8,128)(2,1)S(1)} %collective-permute-done.2.refs_3_), channel_id=1, source_target_pairs={{0,2},{4,0},{8,4},{12,8},{14,12},{10,14},{6,10},{2,6},{1,3},{5,1},... | collective-permute-start | bytes 393224 | tf_op jit(solution)/shard_map/ppermute | solution.py:364
  35.8 0.1 collective-permute-done.6.refs_6_
  35.9 0.4 collective-permute-start.7
  36.4 0.0 collective-permute-done.26
  36.4 0.9 %add_convert_fusion.2 = bf16[520,128]{1,0:T(8,128)(2,1)S(1)} fusion(bf16[520,128]{1,0:T(8,128)(2,1)} %collective-permute-done.26, bf16[520,128]{1,0:T(8,128)(2,1)S(1)} %get-tuple-element.44), kind=kLoop, calls=%fused_computation.2 | loop fusion | flops 266240 | bytes 399360 | tf_op jit(solution)/shard_map/convert_element_type | solution.py:340
  37.3 1.6 %collective-permute-start.27 = (bf16[520,128]{1,0:T(8,128)(2,1)S(1)}, bf16[520,128]{1,0:T(8,128)(2,1)S(1)}, u32[]{:S(2)}, u32[]{:S(2)}) collective-permute-start(bf16[520,128]{1,0:T(8,128)(2,1)S(1)} %add_convert_fusion.2), channel_id=1, source_target_pairs={{0,2},{4,0},{8,4},{12,8},{14,12},{10,14},{6,10},{2,6},{1,3},{5,1},... | collective-permute-start | bytes 399368 | tf_op jit(solution)/shard_map/ppermute | solution.py:364
  38.9 0.0 collective-permute-done.23
  39.0 0.5 collective-permute-start.24
  39.5 0.0 collective-permute-done.3.refs_4_
  39.5 1.9 %collective-permute-done.7.refs_5_ = bf16[4,16,1024]{2,1,0:T(8,128)(2,1)S(1)} collective-permute-done((bf16[4,16,1024]{2,1,0:T(8,128)(2,1)}, bf16[4,16,1024]{2,1,0:T(8,128)(2,1)S(1)}, u32[]{:S(2)}, u32[]{:S(2)}) %collective-permute-start.7) | collective-permute-done | bytes 131104 | tf_op jit(solution)/shard_map/ppermute | solution.py:364
  41.4 2.9 %shard_map.68 = (f32[520,128]{1,0:T(8,128)S(1)}, bf16[520,128]{1,0:T(8,128)(2,1)S(1)}, bf16[520,128]{1,0:T(8,128)(2,1)S(1)}, bf16[520,128]{1,0:T(8,128)(2,1)S(1)...) custom-call(bf16[6,128,1024]{2,1,0:T(8,128)(2,1)S(1)} %get-tuple-ele, ...), custom_call_target="tpu_custom_call" | custom-call | flops 1610612736 | bytes 3670016 | tf_op jit(solution)/shard_map/pallas_call | solution.py:252
  44.3 0.2 collective-permute-start.8
  44.5 1.8 %collective-permute-start.12 = (bf16[520,128]{1,0:T(8,128)(2,1)S(1)}, bf16[520,128]{1,0:T(8,128)(2,1)S(1)}, u32[]{:S(2)}, u32[]{:S(2)}) collective-permute-start(bf16[520,128]{1,0:T(8,128)(2,1)S(1)} %get-tuple-element.36), channel_id=1, source_target_pairs={{0,2},{4,0},{8,4},{12,8},{14,12},{10,14},{6,10},{2,6},{1,3},{5,1},... | collective-permute-start | bytes 399368 | tf_op jit(solution)/shard_map/ppermute | solution.py:364
  46.4 0.0 copy-start
  46.4 0.0 copy-start.1
  46.4 1.6 %collective-permute-start.28 = (bf16[520,128]{1,0:T(8,128)(2,1)S(1)}, bf16[520,128]{1,0:T(8,128)(2,1)S(1)}, u32[]{:S(2)}, u32[]{:S(2)}) collective-permute-start(bf16[520,128]{1,0:T(8,128)(2,1)S(1)} %add_convert_fusion.1), channel_id=1, source_target_pairs={{0,2},{4,0},{8,4},{12,8},{14,12},{10,14},{6,10},{2,6},{1,3},{5,1},... | collective-permute-start | bytes 399368 | tf_op jit(solution)/shard_map/ppermute | solution.py:364
  48.1 0.5 collective-permute-start.25
  48.6 0.7 %collective-permute-done.8 = bf16[520,128]{1,0:T(8,128)(2,1)S(1)} collective-permute-done((bf16[520,128]{1,0:T(8,128)(2,1)S(1)}, bf16[520,128]{1,0:T(8,128)(2,1)S(1)}, u32[]{:S(2)}, u32[]{:S(2)}) %collective-permute-start.8) | collective-permute-done | bytes 133152 | tf_op jit(solution)/shard_map/ppermute | solution.py:364
  49.3 0.3 collective-permute-start.9
  49.6 0.1 collective-permute-done.12
  49.7 1.8 %collective-permute-start.13 = (bf16[520,128]{1,0:T(8,128)(2,1)S(1)}, bf16[520,128]{1,0:T(8,128)(2,1)S(1)}, u32[]{:S(2)}, u32[]{:S(2)}) collective-permute-start(bf16[520,128]{1,0:T(8,128)(2,1)S(1)} %add_convert_fusion.6), channel_id=1, source_target_pairs={{0,2},{4,0},{8,4},{12,8},{14,12},{10,14},{6,10},{2,6},{1,3},{5,1},... | collective-permute-start | bytes 399368 | tf_op jit(solution)/shard_map/ppermute | solution.py:364
  51.5 3.9 %collective-permute-done.9 = bf16[520,128]{1,0:T(8,128)(2,1)S(1)} collective-permute-done((bf16[520,128]{1,0:T(8,128)(2,1)S(1)}, bf16[520,128]{1,0:T(8,128)(2,1)S(1)}, u32[]{:S(2)}, u32[]{:S(2)}) %collective-permute-start.9) | collective-permute-done | bytes 133152 | tf_op jit(solution)/shard_map/ppermute | solution.py:364
  55.5 0.4 collective-permute-start.10
  55.9 0.0 collective-permute-done.13
  55.9 1.7 %collective-permute-start.14 = (bf16[520,128]{1,0:T(8,128)(2,1)S(1)}, bf16[520,128]{1,0:T(8,128)(2,1)S(1)}, u32[]{:S(2)}, u32[]{:S(2)}) collective-permute-start(bf16[520,128]{1,0:T(8,128)(2,1)S(1)} %add_convert_fusion.5), channel_id=1, source_target_pairs={{0,2},{4,0},{8,4},{12,8},{14,12},{10,14},{6,10},{2,6},{1,3},{5,1},... | collective-permute-start | bytes 399368 | tf_op jit(solution)/shard_map/ppermute | solution.py:364
  57.7 2.9 %collective-permute-done.10 = bf16[520,128]{1,0:T(8,128)(2,1)S(1)} collective-permute-done((bf16[520,128]{1,0:T(8,128)(2,1)S(1)}, bf16[520,128]{1,0:T(8,128)(2,1)S(1)}, u32[]{:S(2)}, u32[]{:S(2)}) %collective-permute-start.10) | collective-permute-done | bytes 133152 | tf_op jit(solution)/shard_map/ppermute | solution.py:364
  60.6 0.4 collective-permute-start.11
  61.0 1.7 %collective-permute-start.29 = (bf16[520,128]{1,0:T(8,128)(2,1)S(1)}, bf16[520,128]{1,0:T(8,128)(2,1)S(1)}, u32[]{:S(2)}, u32[]{:S(2)}) collective-permute-start(bf16[520,128]{1,0:T(8,128)(2,1)S(1)} %add_convert_fusion), channel_id=1, source_target_pairs={{0,2},{4,0},{8,4},{12,8},{14,12},{10,14},{6,10},{2,6},{1,3},{5,1},... | collective-permute-start | bytes 399368 | tf_op jit(solution)/shard_map/ppermute | solution.py:364
  62.7 2.9 %collective-permute-done.11.refs_1_ = bf16[520,128]{1,0:T(8,128)(2,1)S(1)} collective-permute-done((bf16[520,128]{1,0:T(8,128)(2,1)S(1)}, bf16[520,128]{1,0:T(8,128)(2,1)S(1)}, u32[]{:S(2)}, u32[]{:S(2)}) %collective-permute-start.11) | collective-permute-done | bytes 133152 | tf_op jit(solution)/shard_map/ppermute | solution.py:364
  65.6 0.1 collective-permute-start.15
  65.7 0.0 collective-permute-done.25.refs_4_
  65.7 0.4 collective-permute-done.29.refs_5_
  66.1 0.8 %collective-permute-done.15.edge_ref = bf16[128,128]{1,0:T(8,128)(2,1)S(1)} collective-permute-done((bf16[128,128]{1,0:T(8,128)(2,1)S(1)}, bf16[128,128]{1,0:T(8,128)(2,1)S(1)}, u32[]{:S(2)}, u32[]{:S(2)}) %collective-permute-start.15) | collective-permute-done | bytes 32800 | tf_op jit(solution)/shard_map/ppermute | solution.py:336
  66.9 1.6 %parents.1 = (bf16[16,8,1024]{2,1,0:T(8,128)(2,1)}, f32[1,8]{1,0:T(1,128)}) custom-call(s32[16]{0:T(128)S(1)} %copy-done, s32[8]{0:T(128)S(1)} %copy-done.1, bf16[128,128]{1,0:T(8,128)(2,1)S(1)} %collective-permute-done.15.edge_ref, f32[520,128]{1,0:T(8,128)S(1)} %get-tuple-element.29.refs_0_, bf16[520,128]{1,0:T(8,128)(2,1)S(1)} %collective-permute-done.11.refs_1_, ...), custom_call_target="tpu_custom_call" | custom-call | flops 786432 | bytes 1310720 | tf_op jit(solution)/shard_map/parents/pallas_call | solution.py:313
  (18 shorter events, 0.4 us)
Async XLA Ops:
  0.6 4.7 %copy-start.2 = (bf16[16,8,1024]{2,1,0:T(8,128)(2,1)S(1)}, bf16[16,8,1024]{2,1,0:T(8,128)(2,1)}, u32[]{:S(2)}) copy-start(bf16[16,8,1024]{2,1,0:T(8,128)(2,1)} %green_any.1) | copy-start | bytes 786436
  2.3 6.6 %collective-permute-start.16 = (bf16[4,16,1024]{2,1,0:T(8,128)(2,1)S(1)}, bf16[4,16,1024]{2,1,0:T(8,128)(2,1)S(1)}, u32[]{:S(2)}, u32[]{:S(2)}) collective-permute-start(bf16[4,16,1024]{2,1,0:T(8,128)(2,1)S(1)} %get-tuple-element.37.refs_1_), channel_id=1, source_target_pairs={{0,2},{4,0},{8,4},{12,8},{14,12},{10,14},{6,10},{2,6},{1,3},{5,1},... | collective-permute-start | bytes 393224 | tf_op jit(solution)/shard_map/ppermute | solution.py:364
  5.3 10.2 %collective-permute-start = (bf16[16,8,1024]{2,1,0:T(8,128)(2,1)S(1)}, bf16[16,8,1024]{2,1,0:T(8,128)(2,1)S(1)}, u32[]{:S(2)}, u32[]{:S(2)}) collective-permute-start(bf16[16,8,1024]{2,1,0:T(8,128)(2,1)S(1)} %copy-done.2), channel_id=1, source_target_pairs={{0,1},{1,0},{2,3},{3,2},{4,5},{5,4},{6,7},{7,6},{8,9},{9,8},{10,11... | collective-permute-start | bytes 786440 | tf_op jit(solution)/shard_map/ppermute | solution.py:336
  5.3 5.9 %collective-permute-start.20 = (bf16[4,16,1024]{2,1,0:T(8,128)(2,1)S(1)}, bf16[4,16,1024]{2,1,0:T(8,128)(2,1)S(1)}, u32[]{:S(2)}, u32[]{:S(2)}) collective-permute-start(bf16[4,16,1024]{2,1,0:T(8,128)(2,1)S(1)} %get-tuple-element.37.refs_1_), channel_id=1, source_target_pairs={{0,4},{4,8},{8,12},{12,14},{14,10},{10,6},{6,2},{2,0},{1,5},{5,9},... | collective-permute-start | bytes 393224 | tf_op jit(solution)/shard_map/ppermute | solution.py:364
  8.9 5.0 %collective-permute-start.17 = (bf16[4,16,1024]{2,1,0:T(8,128)(2,1)S(1)}, bf16[4,16,1024]{2,1,0:T(8,128)(2,1)S(1)}, u32[]{:S(2)}, u32[]{:S(2)}) collective-permute-start(bf16[4,16,1024]{2,1,0:T(8,128)(2,1)S(1)} %collective-permute-done.16.refs_2_), channel_id=1, source_target_pairs={{0,2},{4,0},{8,4},{12,8},{14,12},{10,14},{6,10},{2,6},{1,3},{5,1},... | collective-permute-start | bytes 393224 | tf_op jit(solution)/shard_map/ppermute | solution.py:364
  11.2 5.5 %collective-permute-start.21 = (bf16[4,16,1024]{2,1,0:T(8,128)(2,1)S(1)}, bf16[4,16,1024]{2,1,0:T(8,128)(2,1)S(1)}, u32[]{:S(2)}, u32[]{:S(2)}) collective-permute-start(bf16[4,16,1024]{2,1,0:T(8,128)(2,1)S(1)} %collective-permute-done.20.refs_8_), channel_id=1, source_target_pairs={{0,4},{4,8},{8,12},{12,14},{14,10},{10,6},{6,2},{2,0},{1,5},{5,9},... | collective-permute-start | bytes 393224 | tf_op jit(solution)/shard_map/ppermute | solution.py:364
  13.9 5.1 %collective-permute-start.18 = (bf16[4,16,1024]{2,1,0:T(8,128)(2,1)S(1)}, bf16[4,16,1024]{2,1,0:T(8,128)(2,1)S(1)}, u32[]{:S(2)}, u32[]{:S(2)}) collective-permute-start(bf16[4,16,1024]{2,1,0:T(8,128)(2,1)S(1)} %collective-permute-done.17.refs_3_), channel_id=1, source_target_pairs={{0,2},{4,0},{8,4},{12,8},{14,12},{10,14},{6,10},{2,6},{1,3},{5,1},... | collective-permute-start | bytes 393224 | tf_op jit(solution)/shard_map/ppermute | solution.py:364
  15.6 6.9 %collective-permute-start.4 = (bf16[4,16,1024]{2,1,0:T(8,128)(2,1)S(1)}, bf16[4,16,1024]{2,1,0:T(8,128)(2,1)S(1)}, u32[]{:S(2)}, u32[]{:S(2)}) collective-permute-start(bf16[4,16,1024]{2,1,0:T(8,128)(2,1)S(1)} %edge.1.refs_1_), channel_id=1, source_target_pairs={{0,4},{4,8},{8,12},{12,14},{14,10},{10,6},{6,2},{2,0},{1,5},{5,9},... | collective-permute-start | bytes 393224 | tf_op jit(solution)/shard_map/ppermute | solution.py:364
  16.7 6.3 %collective-permute-start.22 = (bf16[4,16,1024]{2,1,0:T(8,128)(2,1)S(1)}, bf16[4,16,1024]{2,1,0:T(8,128)(2,1)S(1)}, u32[]{:S(2)}, u32[]{:S(2)}) collective-permute-start(bf16[4,16,1024]{2,1,0:T(8,128)(2,1)S(1)} %collective-permute-done.21.refs_7_), channel_id=1, source_target_pairs={{0,4},{4,8},{8,12},{12,14},{14,10},{10,6},{6,2},{2,0},{1,5},{5,9},... | collective-permute-start | bytes 393224 | tf_op jit(solution)/shard_map/ppermute | solution.py:364
  19.0 5.3 %collective-permute-start.19 = (bf16[4,16,1024]{2,1,0:T(8,128)(2,1)S(1)}, bf16[4,16,1024]{2,1,0:T(8,128)(2,1)S(1)}, u32[]{:S(2)}, u32[]{:S(2)}) collective-permute-start(bf16[4,16,1024]{2,1,0:T(8,128)(2,1)S(1)} %collective-permute-done.18.refs_4_), channel_id=1, source_target_pairs={{0,2},{4,0},{8,4},{12,8},{14,12},{10,14},{6,10},{2,6},{1,3},{5,1},... | collective-permute-start | bytes 393224 | tf_op jit(solution)/shard_map/ppermute | solution.py:364
  20.9 6.9 %collective-permute-start.1 = (bf16[4,16,1024]{2,1,0:T(8,128)(2,1)S(1)}, bf16[4,16,1024]{2,1,0:T(8,128)(2,1)S(1)}, u32[]{:S(2)}, u32[]{:S(2)}) collective-permute-start(bf16[4,16,1024]{2,1,0:T(8,128)(2,1)S(1)} %edge.1.refs_1_), channel_id=1, source_target_pairs={{0,2},{4,0},{8,4},{12,8},{14,12},{10,14},{6,10},{2,6},{1,3},{5,1},... | collective-permute-start | bytes 393224 | tf_op jit(solution)/shard_map/ppermute | solution.py:364
  22.5 6.9 %collective-permute-start.5 = (bf16[4,16,1024]{2,1,0:T(8,128)(2,1)S(1)}, bf16[4,16,1024]{2,1,0:T(8,128)(2,1)S(1)}, u32[]{:S(2)}, u32[]{:S(2)}) collective-permute-start(bf16[4,16,1024]{2,1,0:T(8,128)(2,1)S(1)} %collective-permute-done.4.refs_8_), channel_id=1, source_target_pairs={{0,4},{4,8},{8,12},{12,14},{14,10},{10,6},{6,2},{2,0},{1,5},{5,9},... | collective-permute-start | bytes 393224 | tf_op jit(solution)/shard_map/ppermute | solution.py:364
  26.2 10.2 %collective-permute-start.26 = (bf16[520,128]{1,0:T(8,128)(2,1)S(1)}, bf16[520,128]{1,0:T(8,128)(2,1)}, u32[]{:S(2)}, u32[]{:S(2)}) collective-permute-start(bf16[520,128]{1,0:T(8,128)(2,1)S(1)} %get-tuple-element.45), channel_id=1, source_target_pairs={{0,2},{4,0},{8,4},{12,8},{14,12},{10,14},{6,10},{2,6},{1,3},{5,1},... | collective-permute-start | bytes 399368 | tf_op jit(solution)/shard_map/ppermute | solution.py:364
  27.9 6.4 %collective-permute-start.2 = (bf16[4,16,1024]{2,1,0:T(8,128)(2,1)S(1)}, bf16[4,16,1024]{2,1,0:T(8,128)(2,1)S(1)}, u32[]{:S(2)}, u32[]{:S(2)}) collective-permute-start(bf16[4,16,1024]{2,1,0:T(8,128)(2,1)S(1)} %collective-permute-done.1.refs_2_), channel_id=1, source_target_pairs={{0,2},{4,0},{8,4},{12,8},{14,12},{10,14},{6,10},{2,6},{1,3},{5,1},... | collective-permute-start | bytes 393224 | tf_op jit(solution)/shard_map/ppermute | solution.py:364
  29.4 6.5 %collective-permute-start.6 = (bf16[4,16,1024]{2,1,0:T(8,128)(2,1)S(1)}, bf16[4,16,1024]{2,1,0:T(8,128)(2,1)}, u32[]{:S(2)}, u32[]{:S(2)}) collective-permute-start(bf16[4,16,1024]{2,1,0:T(8,128)(2,1)S(1)} %collective-permute-done.5.refs_7_), channel_id=1, source_target_pairs={{0,4},{4,8},{8,12},{12,14},{14,10},{10,6},{6,2},{2,0},{1,5},{5,9},... | collective-permute-start | bytes 393224 | tf_op jit(solution)/shard_map/ppermute | solution.py:364
  29.9 9.1 %collective-permute-start.23 = (bf16[520,128]{1,0:T(8,128)(2,1)S(1)}, bf16[520,128]{1,0:T(8,128)(2,1)S(1)}, u32[]{:S(2)}, u32[]{:S(2)}) collective-permute-start(bf16[520,128]{1,0:T(8,128)(2,1)S(1)} %get-tuple-element.41), channel_id=1, source_target_pairs={{0,4},{4,8},{8,12},{12,14},{14,10},{10,6},{6,2},{2,0},{1,5},{5,9},... | collective-permute-start | bytes 399368 | tf_op jit(solution)/shard_map/ppermute | solution.py:364
  34.2 5.3 %collective-permute-start.3 = (bf16[4,16,1024]{2,1,0:T(8,128)(2,1)S(1)}, bf16[4,16,1024]{2,1,0:T(8,128)(2,1)S(1)}, u32[]{:S(2)}, u32[]{:S(2)}) collective-permute-start(bf16[4,16,1024]{2,1,0:T(8,128)(2,1)S(1)} %collective-permute-done.2.refs_3_), channel_id=1, source_target_pairs={{0,2},{4,0},{8,4},{12,8},{14,12},{10,14},{6,10},{2,6},{1,3},{5,1},... | collective-permute-start | bytes 393224 | tf_op jit(solution)/shard_map/ppermute | solution.py:364
  35.9 5.5 %collective-permute-start.7 = (bf16[4,16,1024]{2,1,0:T(8,128)(2,1)}, bf16[4,16,1024]{2,1,0:T(8,128)(2,1)S(1)}, u32[]{:S(2)}, u32[]{:S(2)}) collective-permute-start(bf16[4,16,1024]{2,1,0:T(8,128)(2,1)} %collective-permute-done.6.refs_6_), channel_id=1, source_target_pairs={{0,4},{4,8},{8,12},{12,14},{14,10},{10,6},{6,2},{2,0},{1,5},{5,9},... | collective-permute-start | bytes 393224 | tf_op jit(solution)/shard_map/ppermute | solution.py:364
  37.3 9.0 %collective-permute-start.27 = (bf16[520,128]{1,0:T(8,128)(2,1)S(1)}, bf16[520,128]{1,0:T(8,128)(2,1)S(1)}, u32[]{:S(2)}, u32[]{:S(2)}) collective-permute-start(bf16[520,128]{1,0:T(8,128)(2,1)S(1)} %add_convert_fusion.2), channel_id=1, source_target_pairs={{0,2},{4,0},{8,4},{12,8},{14,12},{10,14},{6,10},{2,6},{1,3},{5,1},... | collective-permute-start | bytes 399368 | tf_op jit(solution)/shard_map/ppermute | solution.py:364
  39.0 9.0 %collective-permute-start.24 = (bf16[520,128]{1,0:T(8,128)(2,1)S(1)}, bf16[520,128]{1,0:T(8,128)(2,1)S(1)}, u32[]{:S(2)}, u32[]{:S(2)}) collective-permute-start(bf16[520,128]{1,0:T(8,128)(2,1)S(1)} %add_convert_fusion.4), channel_id=1, source_target_pairs={{0,4},{4,8},{8,12},{12,14},{14,10},{10,6},{6,2},{2,0},{1,5},{5,9},... | collective-permute-start | bytes 399368 | tf_op jit(solution)/shard_map/ppermute | solution.py:364
  44.3 5.0 %collective-permute-start.8 = (bf16[520,128]{1,0:T(8,128)(2,1)S(1)}, bf16[520,128]{1,0:T(8,128)(2,1)S(1)}, u32[]{:S(2)}, u32[]{:S(2)}) collective-permute-start(bf16[520,128]{1,0:T(8,128)(2,1)S(1)} %get-tuple-element.33), channel_id=1, source_target_pairs={{0,4},{4,8},{8,12},{12,14},{14,10},{10,6},{6,2},{2,0},{1,5},{5,9},... | collective-permute-start | bytes 399368 | tf_op jit(solution)/shard_map/ppermute | solution.py:364
  44.5 5.2 %collective-permute-start.12 = (bf16[520,128]{1,0:T(8,128)(2,1)S(1)}, bf16[520,128]{1,0:T(8,128)(2,1)S(1)}, u32[]{:S(2)}, u32[]{:S(2)}) collective-permute-start(bf16[520,128]{1,0:T(8,128)(2,1)S(1)} %get-tuple-element.36), channel_id=1, source_target_pairs={{0,2},{4,0},{8,4},{12,8},{14,12},{10,14},{6,10},{2,6},{1,3},{5,1},... | collective-permute-start | bytes 399368 | tf_op jit(solution)/shard_map/ppermute | solution.py:364
  46.4 20.5 %copy-start = (s32[16]{0:T(128)S(1)}, s32[16]{0:T(128)}, u32[]{:S(2)}) copy-start(s32[16]{0:T(128)} %parents_ref.1) | copy-start | bytes 196
  46.4 20.5 %copy-start.1 = (s32[8]{0:T(128)S(1)}, s32[8]{0:T(128)}, u32[]{:S(2)}) copy-start(s32[8]{0:T(128)} %counts_ref.1) | copy-start | bytes 100
  46.4 14.6 %collective-permute-start.28 = (bf16[520,128]{1,0:T(8,128)(2,1)S(1)}, bf16[520,128]{1,0:T(8,128)(2,1)S(1)}, u32[]{:S(2)}, u32[]{:S(2)}) collective-permute-start(bf16[520,128]{1,0:T(8,128)(2,1)S(1)} %add_convert_fusion.1), channel_id=1, source_target_pairs={{0,2},{4,0},{8,4},{12,8},{14,12},{10,14},{6,10},{2,6},{1,3},{5,1},... | collective-permute-start | bytes 399368 | tf_op jit(solution)/shard_map/ppermute | solution.py:364
  48.1 17.6 %collective-permute-start.25 = (bf16[520,128]{1,0:T(8,128)(2,1)S(1)}, bf16[520,128]{1,0:T(8,128)(2,1)S(1)}, u32[]{:S(2)}, u32[]{:S(2)}) collective-permute-start(bf16[520,128]{1,0:T(8,128)(2,1)S(1)} %add_convert_fusion.3), channel_id=1, source_target_pairs={{0,4},{4,8},{8,12},{12,14},{14,10},{10,6},{6,2},{2,0},{1,5},{5,9},... | collective-permute-start | bytes 399368 | tf_op jit(solution)/shard_map/ppermute | solution.py:364
  49.3 6.1 %collective-permute-start.9 = (bf16[520,128]{1,0:T(8,128)(2,1)S(1)}, bf16[520,128]{1,0:T(8,128)(2,1)S(1)}, u32[]{:S(2)}, u32[]{:S(2)}) collective-permute-start(bf16[520,128]{1,0:T(8,128)(2,1)S(1)} %add_convert_fusion.9), channel_id=1, source_target_pairs={{0,4},{4,8},{8,12},{12,14},{14,10},{10,6},{6,2},{2,0},{1,5},{5,9},... | collective-permute-start | bytes 399368 | tf_op jit(solution)/shard_map/ppermute | solution.py:364
  49.7 6.2 %collective-permute-start.13 = (bf16[520,128]{1,0:T(8,128)(2,1)S(1)}, bf16[520,128]{1,0:T(8,128)(2,1)S(1)}, u32[]{:S(2)}, u32[]{:S(2)}) collective-permute-start(bf16[520,128]{1,0:T(8,128)(2,1)S(1)} %add_convert_fusion.6), channel_id=1, source_target_pairs={{0,2},{4,0},{8,4},{12,8},{14,12},{10,14},{6,10},{2,6},{1,3},{5,1},... | collective-permute-start | bytes 399368 | tf_op jit(solution)/shard_map/ppermute | solution.py:364
  55.5 5.0 %collective-permute-start.10 = (bf16[520,128]{1,0:T(8,128)(2,1)S(1)}, bf16[520,128]{1,0:T(8,128)(2,1)S(1)}, u32[]{:S(2)}, u32[]{:S(2)}) collective-permute-start(bf16[520,128]{1,0:T(8,128)(2,1)S(1)} %add_convert_fusion.8), channel_id=1, source_target_pairs={{0,4},{4,8},{8,12},{12,14},{14,10},{10,6},{6,2},{2,0},{1,5},{5,9},... | collective-permute-start | bytes 399368 | tf_op jit(solution)/shard_map/ppermute | solution.py:364
  55.9 6.8 %collective-permute-start.14 = (bf16[520,128]{1,0:T(8,128)(2,1)S(1)}, bf16[520,128]{1,0:T(8,128)(2,1)S(1)}, u32[]{:S(2)}, u32[]{:S(2)}) collective-permute-start(bf16[520,128]{1,0:T(8,128)(2,1)S(1)} %add_convert_fusion.5), channel_id=1, source_target_pairs={{0,2},{4,0},{8,4},{12,8},{14,12},{10,14},{6,10},{2,6},{1,3},{5,1},... | collective-permute-start | bytes 399368 | tf_op jit(solution)/shard_map/ppermute | solution.py:364
  60.6 5.0 %collective-permute-start.11 = (bf16[520,128]{1,0:T(8,128)(2,1)S(1)}, bf16[520,128]{1,0:T(8,128)(2,1)S(1)}, u32[]{:S(2)}, u32[]{:S(2)}) collective-permute-start(bf16[520,128]{1,0:T(8,128)(2,1)S(1)} %add_convert_fusion.7), channel_id=1, source_target_pairs={{0,4},{4,8},{8,12},{12,14},{14,10},{10,6},{6,2},{2,0},{1,5},{5,9},... | collective-permute-start | bytes 399368 | tf_op jit(solution)/shard_map/ppermute | solution.py:364
  61.0 5.0 %collective-permute-start.29 = (bf16[520,128]{1,0:T(8,128)(2,1)S(1)}, bf16[520,128]{1,0:T(8,128)(2,1)S(1)}, u32[]{:S(2)}, u32[]{:S(2)}) collective-permute-start(bf16[520,128]{1,0:T(8,128)(2,1)S(1)} %add_convert_fusion), channel_id=1, source_target_pairs={{0,2},{4,0},{8,4},{12,8},{14,12},{10,14},{6,10},{2,6},{1,3},{5,1},... | collective-permute-start | bytes 399368 | tf_op jit(solution)/shard_map/ppermute | solution.py:364
  65.6 1.3 %collective-permute-start.15 = (bf16[128,128]{1,0:T(8,128)(2,1)S(1)}, bf16[128,128]{1,0:T(8,128)(2,1)S(1)}, u32[]{:S(2)}, u32[]{:S(2)}) collective-permute-start(bf16[128,128]{1,0:T(8,128)(2,1)S(1)} %add_convert_fusion.10), channel_id=1, source_target_pairs={{0,1},{1,0},{2,3},{3,2},{4,5},{5,4},{6,7},{7,6},{8,9},{9,8},{10,11... | collective-permute-start | bytes 98312 | tf_op jit(solution)/shard_map/ppermute | solution.py:336

commit v7 on v6

--- a/solution.py
+++ b/solution.py
@@ -271,45 +271,52 @@
     groups = (refs[0:3], refs[3:6])
     out_ref, energy_ref, total, spread = refs[6:]
     rows, walkers, width = out_ref.shape
-    blocks = width // 128
     mine = lax.axis_index("pop")
+    last = parents_ref.shape[0] - 1
+    hits, edge_hits, scales = {}, {}, []
+    for p in range(walkers):
+        parent = mine * walkers + p
+        for c in range(max(p - 1, 0), min(p + 2, walkers)):
+            hits[c, p] = parents_ref[mine * walkers + c] == parent
+        if p in (0, walkers - 1):
+            child = parent + (1 if p else -1)
+            valid = jnp.logical_and(child >= 0, child <= last)
+            found = parents_ref[jnp.clip(child, 0, last)] == parent
+            edge_hits[p] = jnp.logical_and(valid, found)
+        scales.append(factor / jnp.maximum(counts_ref[p], 1).astype(F32))
+    for t in range(width // 128):
+        for group, (own, up, down) in enumerate(groups):
+            base = group_base(group, walkers, size)
+            for j in range(size):
+                place = message_block(j, t, rows, width)
+                total[t, base + j] = (
+                    own[place, :] + up[place, :].astype(F32) + down[place, :].astype(F32)
+                )
+        edge = edge_ref[t * rows : (t + 1) * rows, :].astype(F32)
+        for p in range(walkers):
+            summed = jnp.zeros((rows, 128), F32)
+            for c in range(max(p - 1, 0), min(p + 2, walkers)):
+                summed = summed + jnp.where(hits[c, p], total[t, c], 0.0)
+            if p in edge_hits:
+                summed = summed + jnp.where(edge_hits[p], edge, 0.0)
+            spread[t, pl.ds(p, rows, stride=walkers), :] = summed * scales[p]
+        lanes = slice(t * 128, t * 128 + 128)
+        out_ref[:, :, lanes] = spread[t].astype(BF16).reshape(rows, walkers, 128)
     row = lax.broadcasted_iota(jnp.int32, (8, 128), 0)
     lane = lax.broadcasted_iota(jnp.int32, (8, 128), 1)
     energies = jnp.zeros((1, 128), F32)
     for group, (own, up, down) in enumerate(groups):
-        base = group_base(group, walkers, size)
-        for j in range(size):
-            span = slice(j * blocks * rows, (j + 1) * blocks * rows)
-            total[base + j] = own[span, :] + up[span, :].astype(F32) + down[span, :].astype(F32)
-        tail = slice(size * blocks * rows, size * blocks * rows + 8)
+        tail = slice(message_rows(size, rows, width) - 8, message_rows(size, rows, width))
         halves = own[tail, :] + up[tail, :].astype(F32) + down[tail, :].astype(F32)
         column = jnp.sum(halves, axis=1, keepdims=True)
-        here = jnp.logical_and(lane == row + base, row < size)
+        here = jnp.logical_and(lane == row + group_base(group, walkers, size), row < size)
         energies = energies + jnp.sum(jnp.where(here, column, 0.0), axis=0, keepdims=True)
     energy_ref[...] = energies[:, :walkers]
-    edge = edge_ref[...].astype(F32)
-    last = parents_ref.shape[0] - 1
-    for p in range(walkers):
-        parent = mine * walkers + p
-        summed = jnp.zeros((blocks * rows, 128), F32)
-        for c in range(max(p - 1, 0), min(p + 2, walkers)):
-            hit = parents_ref[mine * walkers + c] == parent
-            summed = summed + jnp.where(hit, total[c], 0.0)
-        if p in (0, walkers - 1):
-            child = parent + (1 if p else -1)
-            valid = jnp.logical_and(child >= 0, child <= last)
-            found = parents_ref[jnp.clip(child, 0, last)] == parent
-            summed = summed + jnp.where(jnp.logical_and(valid, found), edge, 0.0)
-        mean = summed * (factor / jnp.maximum(counts_ref[p], 1).astype(F32))
-        for t in range(blocks):
-            spread[t, pl.ds(p, rows, stride=walkers), :] = mean[t * rows : (t + 1) * rows, :]
-    for t in range(blocks):
-        block = spread[t].astype(BF16).reshape(rows, walkers, 128)
-        out_ref[:, :, t * 128 : t * 128 + 128] = block
 
 
 def parent_forces(shape, size, factor, parents, counts, edge, group0, group1):
     rows, walkers, width = shape
+    blocks = width // 128
     return pl.pallas_call(
         functools.partial(parents_kernel, factor, size),
         out_shape=[
@@ -319,8 +326,8 @@
         in_specs=[SMEM, SMEM] + [VMEM] * 7,
         out_specs=[VMEM, VMEM],
         scratch_shapes=[
-            pltpu.VMEM((walkers, rows * width // 128, 128), F32),
-            pltpu.VMEM((width // 128, rows * walkers, 128), F32),
+            pltpu.VMEM((blocks, walkers, rows, 128), F32),
+            pltpu.VMEM((blocks, rows * walkers, 128), F32),
         ],
         cost_estimate=pl.CostEstimate(
             flops=6 * rows * walkers * width,

time: 68.7 us -> 68.7 us (level)
  no operation moved by 1% of the time
where the time goes in v7:
time: 68.7 us; the launch traced here: 68.5 us
  starting transfers between devices  31.5 us (46%)
  waiting for transfers between devices  26.7 us (39%)
  Pallas kernels  8.2 us (12%)
  other arithmetic  1.3 us (2%)
  between operations  0.75 us (1%)
    ppermute x28, starting transfers between devices, hop(): return lax.ppermute(x, 'chol', pairs[key[3]])  31.4 us
    ppermute x28, waiting for transfers between devices, hop(): return lax.ppermute(x, 'chol', pairs[key[3]])  25.9 us
    pallas_call x2, Pallas kernels, partial_forces(): pl.pallas_call(functools.partial(force_kernel, -0.125 / (total * orbitals...  4.84 us
    pallas_call x1, Pallas kernels, make_children(): pl.pallas_call(functools.partial(children_kernel, n), out_shape=[jax.Shap...  1.64 us
    pallas_call x1, Pallas kernels, parent_forces(): pl.pallas_call(functools.partial(parents_kernel, factor, size), out_shape...  1.61 us
  transfers between devices with their start and end apart: 30, of which 17 were waited for; matrix products, arithmetic and copies ran while one was open for 2% of the time, Pallas kernels for 7%

profile of v7, /device:TPU:0, one launch (start us, length us, event | category | flops | bytes accessed | tf_op | source)
XLA Modules:
  0.0 68.5 jit_solution(2261243978608912549)
XLA Ops:
  0.6 1.6 %children.1 = (bf16[4,16,1024]{2,1,0:T(8,128)(2,1)S(1)}, bf16[4,16,1024]{2,1,0:T(8,128)(2,1)S(1)}, bf16[6,128,1024]{2,1,0:T(8,128)(2,1)S(1)}, f32[16,1024]{1,0:T(8,128)S(1)}, f32[16,128]{1,0:T(8,128)S(1)}) custom-call(s32[16]{0:T(128)} %parents_ref.1, bf16[16,8,1024]{2,1,0:T(8,128)(2,1)} %green_any.1, bf16[16,8,1024]{2,1,0:T(8,128)(2,1)} %delta_any.1, ...), custom_call_target="tpu_custom_call" | custom-call | flops 131072 | bytes 786432 | tf_op jit(solution)/shard_map/children/pallas_call | solution.py:154
  2.3 3.0 %collective-permute-start.16 = (bf16[4,16,1024]{2,1,0:T(8,128)(2,1)S(1)}, bf16[4,16,1024]{2,1,0:T(8,128)(2,1)S(1)}, u32[]{:S(2)}, u32[]{:S(2)}) collective-permute-start(bf16[4,16,1024]{2,1,0:T(8,128)(2,1)S(1)} %get-tuple-element.37.refs_1_), channel_id=1, source_target_pairs={{0,2},{4,0},{8,4},{12,8},{14,12},{10,14},{6,10},{2,6},{1,3},{5,1},... | collective-permute-start | bytes 393224 | tf_op jit(solution)/shard_map/ppermute | solution.py:371
  5.3 0.0 collective-permute-start
  5.3 0.2 collective-permute-start.20
  5.6 3.3 %collective-permute-done.16.refs_2_ = bf16[4,16,1024]{2,1,0:T(8,128)(2,1)S(1)} collective-permute-done((bf16[4,16,1024]{2,1,0:T(8,128)(2,1)S(1)}, bf16[4,16,1024]{2,1,0:T(8,128)(2,1)S(1)}, u32[]{:S(2)}, u32[]{:S(2)}) %collective-permute-start.16) | collective-permute-done | bytes 131104 | tf_op jit(solution)/shard_map/ppermute | solution.py:371
  8.9 1.7 %collective-permute-start.17 = (bf16[4,16,1024]{2,1,0:T(8,128)(2,1)S(1)}, bf16[4,16,1024]{2,1,0:T(8,128)(2,1)S(1)}, u32[]{:S(2)}, u32[]{:S(2)}) collective-permute-start(bf16[4,16,1024]{2,1,0:T(8,128)(2,1)S(1)} %collective-permute-done.16.refs_2_), channel_id=1, source_target_pairs={{0,2},{4,0},{8,4},{12,8},{14,12},{10,14},{6,10},{2,6},{1,3},{5,1},... | collective-permute-start | bytes 393224 | tf_op jit(solution)/shard_map/ppermute | solution.py:371
  10.5 0.7 collective-permute-done.20.refs_8_
  11.2 0.3 collective-permute-start.21
  11.5 2.4 %collective-permute-done.17.refs_3_ = bf16[4,16,1024]{2,1,0:T(8,128)(2,1)S(1)} collective-permute-done((bf16[4,16,1024]{2,1,0:T(8,128)(2,1)S(1)}, bf16[4,16,1024]{2,1,0:T(8,128)(2,1)S(1)}, u32[]{:S(2)}, u32[]{:S(2)}) %collective-permute-start.17) | collective-permute-done | bytes 131104 | tf_op jit(solution)/shard_map/ppermute | solution.py:371
  13.9 1.7 %collective-permute-start.18 = (bf16[4,16,1024]{2,1,0:T(8,128)(2,1)S(1)}, bf16[4,16,1024]{2,1,0:T(8,128)(2,1)S(1)}, u32[]{:S(2)}, u32[]{:S(2)}) collective-permute-start(bf16[4,16,1024]{2,1,0:T(8,128)(2,1)S(1)} %collective-permute-done.17.refs_3_), channel_id=1, source_target_pairs={{0,2},{4,0},{8,4},{12,8},{14,12},{10,14},{6,10},{2,6},{1,3},{5,1},... | collective-permute-start | bytes 393224 | tf_op jit(solution)/shard_map/ppermute | solution.py:371
  15.5 0.0 collective-permute-done.other_ref
  15.5 0.1 edge.1.refs_1_
  15.6 0.4 collective-permute-start.4
  16.0 0.7 collective-permute-done.21.refs_7_
  16.7 1.1 %collective-permute-start.22 = (bf16[4,16,1024]{2,1,0:T(8,128)(2,1)S(1)}, bf16[4,16,1024]{2,1,0:T(8,128)(2,1)S(1)}, u32[]{:S(2)}, u32[]{:S(2)}) collective-permute-start(bf16[4,16,1024]{2,1,0:T(8,128)(2,1)S(1)} %collective-permute-done.21.refs_7_), channel_id=1, source_target_pairs={{0,4},{4,8},{8,12},{12,14},{14,10},{10,6},{6,2},{2,0},{1,5},{5,9},... | collective-permute-start | bytes 393224 | tf_op jit(solution)/shard_map/ppermute | solution.py:371
  17.8 1.2 %collective-permute-done.18.refs_4_ = bf16[4,16,1024]{2,1,0:T(8,128)(2,1)S(1)} collective-permute-done((bf16[4,16,1024]{2,1,0:T(8,128)(2,1)S(1)}, bf16[4,16,1024]{2,1,0:T(8,128)(2,1)S(1)}, u32[]{:S(2)}, u32[]{:S(2)}) %collective-permute-start.18) | collective-permute-done | bytes 131104 | tf_op jit(solution)/shard_map/ppermute | solution.py:371
  19.0 1.9 %collective-permute-start.19 = (bf16[4,16,1024]{2,1,0:T(8,128)(2,1)S(1)}, bf16[4,16,1024]{2,1,0:T(8,128)(2,1)S(1)}, u32[]{:S(2)}, u32[]{:S(2)}) collective-permute-start(bf16[4,16,1024]{2,1,0:T(8,128)(2,1)S(1)} %collective-permute-done.18.refs_4_), channel_id=1, source_target_pairs={{0,2},{4,0},{8,4},{12,8},{14,12},{10,14},{6,10},{2,6},{1,3},{5,1},... | collective-permute-start | bytes 393224 | tf_op jit(solution)/shard_map/ppermute | solution.py:371
  20.9 1.6 %collective-permute-start.1 = (bf16[4,16,1024]{2,1,0:T(8,128)(2,1)S(1)}, bf16[4,16,1024]{2,1,0:T(8,128)(2,1)S(1)}, u32[]{:S(2)}, u32[]{:S(2)}) collective-permute-start(bf16[4,16,1024]{2,1,0:T(8,128)(2,1)S(1)} %edge.1.refs_1_), channel_id=1, source_target_pairs={{0,2},{4,0},{8,4},{12,8},{14,12},{10,14},{6,10},{2,6},{1,3},{5,1},... | collective-permute-start | bytes 393224 | tf_op jit(solution)/shard_map/ppermute | solution.py:371
  22.5 0.0 collective-permute-done.4.refs_8_
  22.5 0.5 collective-permute-start.5
  22.9 0.1 collective-permute-done.22.refs_6_
  23.0 1.2 %collective-permute-done.19.refs_5_ = bf16[4,16,1024]{2,1,0:T(8,128)(2,1)S(1)} collective-permute-done((bf16[4,16,1024]{2,1,0:T(8,128)(2,1)S(1)}, bf16[4,16,1024]{2,1,0:T(8,128)(2,1)S(1)}, u32[]{:S(2)}, u32[]{:S(2)}) %collective-permute-start.19) | collective-permute-done | bytes 131104 | tf_op jit(solution)/shard_map/ppermute | solution.py:371
  24.2 2.0 %shard_map.69 = (f32[520,128]{1,0:T(8,128)S(1)}, bf16[520,128]{1,0:T(8,128)(2,1)S(1)}, bf16[520,128]{1,0:T(8,128)(2,1)S(1)}, bf16[520,128]{1,0:T(8,128)(2,1)S(1)...) custom-call(bf16[6,128,1024]{2,1,0:T(8,128)(2,1)S(1)} %get-tuple-ele, ...), custom_call_target="tpu_custom_call" | custom-call | flops 1610612736 | bytes 3670016 | tf_op jit(solution)/shard_map/pallas_call | solution.py:252
  26.2 1.6 %collective-permute-start.26 = (bf16[520,128]{1,0:T(8,128)(2,1)S(1)}, bf16[520,128]{1,0:T(8,128)(2,1)}, u32[]{:S(2)}, u32[]{:S(2)}) collective-permute-start(bf16[520,128]{1,0:T(8,128)(2,1)S(1)} %get-tuple-element.45), channel_id=1, source_target_pairs={{0,2},{4,0},{8,4},{12,8},{14,12},{10,14},{6,10},{2,6},{1,3},{5,1},... | collective-permute-start | bytes 399368 | tf_op jit(solution)/shard_map/ppermute | solution.py:371
  27.9 0.0 collective-permute-done.1.refs_2_
  27.9 1.6 %collective-permute-start.2 = (bf16[4,16,1024]{2,1,0:T(8,128)(2,1)S(1)}, bf16[4,16,1024]{2,1,0:T(8,128)(2,1)S(1)}, u32[]{:S(2)}, u32[]{:S(2)}) collective-permute-start(bf16[4,16,1024]{2,1,0:T(8,128)(2,1)S(1)} %collective-permute-done.1.refs_2_), channel_id=1, source_target_pairs={{0,2},{4,0},{8,4},{12,8},{14,12},{10,14},{6,10},{2,6},{1,3},{5,1},... | collective-permute-start | bytes 393224 | tf_op jit(solution)/shard_map/ppermute | solution.py:371
  29.4 0.0 collective-permute-done.5.refs_7_
  29.4 0.4 collective-permute-start.6
  29.9 0.8 %collective-permute-start.23 = (bf16[520,128]{1,0:T(8,128)(2,1)S(1)}, bf16[520,128]{1,0:T(8,128)(2,1)S(1)}, u32[]{:S(2)}, u32[]{:S(2)}) collective-permute-start(bf16[520,128]{1,0:T(8,128)(2,1)S(1)} %get-tuple-element.41), channel_id=1, source_target_pairs={{0,4},{4,8},{8,12},{12,14},{14,10},{10,6},{6,2},{2,0},{1,5},{5,9},... | collective-permute-start | bytes 399368 | tf_op jit(solution)/shard_map/ppermute | solution.py:371
  30.7 3.5 %collective-permute-done.2.refs_3_ = bf16[4,16,1024]{2,1,0:T(8,128)(2,1)S(1)} collective-permute-done((bf16[4,16,1024]{2,1,0:T(8,128)(2,1)S(1)}, bf16[4,16,1024]{2,1,0:T(8,128)(2,1)S(1)}, u32[]{:S(2)}, u32[]{:S(2)}) %collective-permute-start.2) | collective-permute-done | bytes 131104 | tf_op jit(solution)/shard_map/ppermute | solution.py:371
  34.2 1.6 %collective-permute-start.3 = (bf16[4,16,1024]{2,1,0:T(8,128)(2,1)S(1)}, bf16[4,16,1024]{2,1,0:T(8,128)(2,1)S(1)}, u32[]{:S(2)}, u32[]{:S(2)}) collective-permute-start(bf16[4,16,1024]{2,1,0:T(8,128)(2,1)S(1)} %collective-permute-done.2.refs_3_), channel_id=1, source_target_pairs={{0,2},{4,0},{8,4},{12,8},{14,12},{10,14},{6,10},{2,6},{1,3},{5,1},... | collective-permute-start | bytes 393224 | tf_op jit(solution)/shard_map/ppermute | solution.py:371
  35.8 0.1 collective-permute-done.6.refs_6_
  35.9 0.4 collective-permute-start.7
  36.4 0.0 collective-permute-done.26
  36.4 0.9 %add_convert_fusion.2 = bf16[520,128]{1,0:T(8,128)(2,1)S(1)} fusion(bf16[520,128]{1,0:T(8,128)(2,1)} %collective-permute-done.26, bf16[520,128]{1,0:T(8,128)(2,1)S(1)} %get-tuple-element.44), kind=kLoop, calls=%fused_computation.2 | loop fusion | flops 266240 | bytes 399360 | tf_op jit(solution)/shard_map/convert_element_type | solution.py:347
  37.3 1.6 %collective-permute-start.27 = (bf16[520,128]{1,0:T(8,128)(2,1)S(1)}, bf16[520,128]{1,0:T(8,128)(2,1)S(1)}, u32[]{:S(2)}, u32[]{:S(2)}) collective-permute-start(bf16[520,128]{1,0:T(8,128)(2,1)S(1)} %add_convert_fusion.2), channel_id=1, source_target_pairs={{0,2},{4,0},{8,4},{12,8},{14,12},{10,14},{6,10},{2,6},{1,3},{5,1},... | collective-permute-start | bytes 399368 | tf_op jit(solution)/shard_map/ppermute | solution.py:371
  38.9 0.0 collective-permute-done.23
  39.0 0.5 collective-permute-start.24
  39.5 0.0 collective-permute-done.3.refs_4_
  39.5 1.9 %collective-permute-done.7.refs_5_ = bf16[4,16,1024]{2,1,0:T(8,128)(2,1)S(1)} collective-permute-done((bf16[4,16,1024]{2,1,0:T(8,128)(2,1)}, bf16[4,16,1024]{2,1,0:T(8,128)(2,1)S(1)}, u32[]{:S(2)}, u32[]{:S(2)}) %collective-permute-start.7) | collective-permute-done | bytes 131104 | tf_op jit(solution)/shard_map/ppermute | solution.py:371
  41.4 2.9 %shard_map.68 = (f32[520,128]{1,0:T(8,128)S(1)}, bf16[520,128]{1,0:T(8,128)(2,1)S(1)}, bf16[520,128]{1,0:T(8,128)(2,1)S(1)}, bf16[520,128]{1,0:T(8,128)(2,1)S(1)...) custom-call(bf16[6,128,1024]{2,1,0:T(8,128)(2,1)S(1)} %get-tuple-ele, ...), custom_call_target="tpu_custom_call" | custom-call | flops 1610612736 | bytes 3670016 | tf_op jit(solution)/shard_map/pallas_call | solution.py:252
  44.3 0.2 collective-permute-start.8
  44.5 1.8 %collective-permute-start.12 = (bf16[520,128]{1,0:T(8,128)(2,1)S(1)}, bf16[520,128]{1,0:T(8,128)(2,1)S(1)}, u32[]{:S(2)}, u32[]{:S(2)}) collective-permute-start(bf16[520,128]{1,0:T(8,128)(2,1)S(1)} %get-tuple-element.36), channel_id=1, source_target_pairs={{0,2},{4,0},{8,4},{12,8},{14,12},{10,14},{6,10},{2,6},{1,3},{5,1},... | collective-permute-start | bytes 399368 | tf_op jit(solution)/shard_map/ppermute | solution.py:371
  46.4 0.0 copy-start
  46.4 0.0 copy-start.1
  46.4 1.6 %collective-permute-start.28 = (bf16[520,128]{1,0:T(8,128)(2,1)S(1)}, bf16[520,128]{1,0:T(8,128)(2,1)S(1)}, u32[]{:S(2)}, u32[]{:S(2)}) collective-permute-start(bf16[520,128]{1,0:T(8,128)(2,1)S(1)} %add_convert_fusion.1), channel_id=1, source_target_pairs={{0,2},{4,0},{8,4},{12,8},{14,12},{10,14},{6,10},{2,6},{1,3},{5,1},... | collective-permute-start | bytes 399368 | tf_op jit(solution)/shard_map/ppermute | solution.py:371
  48.1 0.5 collective-permute-start.25
  48.6 0.7 %collective-permute-done.8 = bf16[520,128]{1,0:T(8,128)(2,1)S(1)} collective-permute-done((bf16[520,128]{1,0:T(8,128)(2,1)S(1)}, bf16[520,128]{1,0:T(8,128)(2,1)S(1)}, u32[]{:S(2)}, u32[]{:S(2)}) %collective-permute-start.8) | collective-permute-done | bytes 133152 | tf_op jit(solution)/shard_map/ppermute | solution.py:371
  49.3 0.3 collective-permute-start.9
  49.6 0.1 collective-permute-done.12
  49.7 1.8 %collective-permute-start.13 = (bf16[520,128]{1,0:T(8,128)(2,1)S(1)}, bf16[520,128]{1,0:T(8,128)(2,1)S(1)}, u32[]{:S(2)}, u32[]{:S(2)}) collective-permute-start(bf16[520,128]{1,0:T(8,128)(2,1)S(1)} %add_convert_fusion.6), channel_id=1, source_target_pairs={{0,2},{4,0},{8,4},{12,8},{14,12},{10,14},{6,10},{2,6},{1,3},{5,1},... | collective-permute-start | bytes 399368 | tf_op jit(solution)/shard_map/ppermute | solution.py:371
  51.5 3.9 %collective-permute-done.9 = bf16[520,128]{1,0:T(8,128)(2,1)S(1)} collective-permute-done((bf16[520,128]{1,0:T(8,128)(2,1)S(1)}, bf16[520,128]{1,0:T(8,128)(2,1)S(1)}, u32[]{:S(2)}, u32[]{:S(2)}) %collective-permute-start.9) | collective-permute-done | bytes 133152 | tf_op jit(solution)/shard_map/ppermute | solution.py:371
  55.5 0.4 collective-permute-start.10
  55.9 0.0 collective-permute-done.13
  55.9 1.7 %collective-permute-start.14 = (bf16[520,128]{1,0:T(8,128)(2,1)S(1)}, bf16[520,128]{1,0:T(8,128)(2,1)S(1)}, u32[]{:S(2)}, u32[]{:S(2)}) collective-permute-start(bf16[520,128]{1,0:T(8,128)(2,1)S(1)} %add_convert_fusion.5), channel_id=1, source_target_pairs={{0,2},{4,0},{8,4},{12,8},{14,12},{10,14},{6,10},{2,6},{1,3},{5,1},... | collective-permute-start | bytes 399368 | tf_op jit(solution)/shard_map/ppermute | solution.py:371
  57.7 2.9 %collective-permute-done.10 = bf16[520,128]{1,0:T(8,128)(2,1)S(1)} collective-permute-done((bf16[520,128]{1,0:T(8,128)(2,1)S(1)}, bf16[520,128]{1,0:T(8,128)(2,1)S(1)}, u32[]{:S(2)}, u32[]{:S(2)}) %collective-permute-start.10) | collective-permute-done | bytes 133152 | tf_op jit(solution)/shard_map/ppermute | solution.py:371
  60.6 0.4 collective-permute-start.11
  61.0 1.7 %collective-permute-start.29 = (bf16[520,128]{1,0:T(8,128)(2,1)S(1)}, bf16[520,128]{1,0:T(8,128)(2,1)S(1)}, u32[]{:S(2)}, u32[]{:S(2)}) collective-permute-start(bf16[520,128]{1,0:T(8,128)(2,1)S(1)} %add_convert_fusion), channel_id=1, source_target_pairs={{0,2},{4,0},{8,4},{12,8},{14,12},{10,14},{6,10},{2,6},{1,3},{5,1},... | collective-permute-start | bytes 399368 | tf_op jit(solution)/shard_map/ppermute | solution.py:371
  62.7 2.9 %collective-permute-done.11.refs_1_ = bf16[520,128]{1,0:T(8,128)(2,1)S(1)} collective-permute-done((bf16[520,128]{1,0:T(8,128)(2,1)S(1)}, bf16[520,128]{1,0:T(8,128)(2,1)S(1)}, u32[]{:S(2)}, u32[]{:S(2)}) %collective-permute-start.11) | collective-permute-done | bytes 133152 | tf_op jit(solution)/shard_map/ppermute | solution.py:371
  65.6 0.1 collective-permute-start.15
  65.7 0.0 collective-permute-done.25.refs_4_
  65.7 0.4 collective-permute-done.29.refs_5_
  66.1 0.8 %collective-permute-done.15.edge_ref = bf16[128,128]{1,0:T(8,128)(2,1)S(1)} collective-permute-done((bf16[128,128]{1,0:T(8,128)(2,1)S(1)}, bf16[128,128]{1,0:T(8,128)(2,1)S(1)}, u32[]{:S(2)}, u32[]{:S(2)}) %collective-permute-start.15) | collective-permute-done | bytes 32800 | tf_op jit(solution)/shard_map/ppermute | solution.py:343
  66.9 1.6 %parents.1 = (bf16[16,8,1024]{2,1,0:T(8,128)(2,1)}, f32[1,8]{1,0:T(1,128)}) custom-call(s32[16]{0:T(128)S(1)} %copy-done, s32[8]{0:T(128)S(1)} %copy-done.1, bf16[128,128]{1,0:T(8,128)(2,1)S(1)} %collective-permute-done.15.edge_ref, f32[520,128]{1,0:T(8,128)S(1)} %get-tuple-element.29.refs_0_, bf16[520,128]{1,0:T(8,128)(2,1)S(1)} %collective-permute-done.11.refs_1_, ...), custom_call_target="tpu_custom_call" | custom-call | flops 786432 | bytes 1310720 | tf_op jit(solution)/shard_map/parents/pallas_call | solution.py:320
  (18 shorter events, 0.4 us)
Async XLA Ops:
  0.6 4.7 %copy-start.2 = (bf16[16,8,1024]{2,1,0:T(8,128)(2,1)S(1)}, bf16[16,8,1024]{2,1,0:T(8,128)(2,1)}, u32[]{:S(2)}) copy-start(bf16[16,8,1024]{2,1,0:T(8,128)(2,1)} %green_any.1) | copy-start | bytes 786436
  2.3 6.6 %collective-permute-start.16 = (bf16[4,16,1024]{2,1,0:T(8,128)(2,1)S(1)}, bf16[4,16,1024]{2,1,0:T(8,128)(2,1)S(1)}, u32[]{:S(2)}, u32[]{:S(2)}) collective-permute-start(bf16[4,16,1024]{2,1,0:T(8,128)(2,1)S(1)} %get-tuple-element.37.refs_1_), channel_id=1, source_target_pairs={{0,2},{4,0},{8,4},{12,8},{14,12},{10,14},{6,10},{2,6},{1,3},{5,1},... | collective-permute-start | bytes 393224 | tf_op jit(solution)/shard_map/ppermute | solution.py:371
  5.3 10.2 %collective-permute-start = (bf16[16,8,1024]{2,1,0:T(8,128)(2,1)S(1)}, bf16[16,8,1024]{2,1,0:T(8,128)(2,1)S(1)}, u32[]{:S(2)}, u32[]{:S(2)}) collective-permute-start(bf16[16,8,1024]{2,1,0:T(8,128)(2,1)S(1)} %copy-done.2), channel_id=1, source_target_pairs={{0,1},{1,0},{2,3},{3,2},{4,5},{5,4},{6,7},{7,6},{8,9},{9,8},{10,11... | collective-permute-start | bytes 786440 | tf_op jit(solution)/shard_map/ppermute | solution.py:343
  5.3 5.9 %collective-permute-start.20 = (bf16[4,16,1024]{2,1,0:T(8,128)(2,1)S(1)}, bf16[4,16,1024]{2,1,0:T(8,128)(2,1)S(1)}, u32[]{:S(2)}, u32[]{:S(2)}) collective-permute-start(bf16[4,16,1024]{2,1,0:T(8,128)(2,1)S(1)} %get-tuple-element.37.refs_1_), channel_id=1, source_target_pairs={{0,4},{4,8},{8,12},{12,14},{14,10},{10,6},{6,2},{2,0},{1,5},{5,9},... | collective-permute-start | bytes 393224 | tf_op jit(solution)/shard_map/ppermute | solution.py:371
  8.9 5.0 %collective-permute-start.17 = (bf16[4,16,1024]{2,1,0:T(8,128)(2,1)S(1)}, bf16[4,16,1024]{2,1,0:T(8,128)(2,1)S(1)}, u32[]{:S(2)}, u32[]{:S(2)}) collective-permute-start(bf16[4,16,1024]{2,1,0:T(8,128)(2,1)S(1)} %collective-permute-done.16.refs_2_), channel_id=1, source_target_pairs={{0,2},{4,0},{8,4},{12,8},{14,12},{10,14},{6,10},{2,6},{1,3},{5,1},... | collective-permute-start | bytes 393224 | tf_op jit(solution)/shard_map/ppermute | solution.py:371
  11.2 5.5 %collective-permute-start.21 = (bf16[4,16,1024]{2,1,0:T(8,128)(2,1)S(1)}, bf16[4,16,1024]{2,1,0:T(8,128)(2,1)S(1)}, u32[]{:S(2)}, u32[]{:S(2)}) collective-permute-start(bf16[4,16,1024]{2,1,0:T(8,128)(2,1)S(1)} %collective-permute-done.20.refs_8_), channel_id=1, source_target_pairs={{0,4},{4,8},{8,12},{12,14},{14,10},{10,6},{6,2},{2,0},{1,5},{5,9},... | collective-permute-start | bytes 393224 | tf_op jit(solution)/shard_map/ppermute | solution.py:371
  13.9 5.1 %collective-permute-start.18 = (bf16[4,16,1024]{2,1,0:T(8,128)(2,1)S(1)}, bf16[4,16,1024]{2,1,0:T(8,128)(2,1)S(1)}, u32[]{:S(2)}, u32[]{:S(2)}) collective-permute-start(bf16[4,16,1024]{2,1,0:T(8,128)(2,1)S(1)} %collective-permute-done.17.refs_3_), channel_id=1, source_target_pairs={{0,2},{4,0},{8,4},{12,8},{14,12},{10,14},{6,10},{2,6},{1,3},{5,1},... | collective-permute-start | bytes 393224 | tf_op jit(solution)/shard_map/ppermute | solution.py:371
  15.6 6.9 %collective-permute-start.4 = (bf16[4,16,1024]{2,1,0:T(8,128)(2,1)S(1)}, bf16[4,16,1024]{2,1,0:T(8,128)(2,1)S(1)}, u32[]{:S(2)}, u32[]{:S(2)}) collective-permute-start(bf16[4,16,1024]{2,1,0:T(8,128)(2,1)S(1)} %edge.1.refs_1_), channel_id=1, source_target_pairs={{0,4},{4,8},{8,12},{12,14},{14,10},{10,6},{6,2},{2,0},{1,5},{5,9},... | collective-permute-start | bytes 393224 | tf_op jit(solution)/shard_map/ppermute | solution.py:371
  16.7 6.3 %collective-permute-start.22 = (bf16[4,16,1024]{2,1,0:T(8,128)(2,1)S(1)}, bf16[4,16,1024]{2,1,0:T(8,128)(2,1)S(1)}, u32[]{:S(2)}, u32[]{:S(2)}) collective-permute-start(bf16[4,16,1024]{2,1,0:T(8,128)(2,1)S(1)} %collective-permute-done.21.refs_7_), channel_id=1, source_target_pairs={{0,4},{4,8},{8,12},{12,14},{14,10},{10,6},{6,2},{2,0},{1,5},{5,9},... | collective-permute-start | bytes 393224 | tf_op jit(solution)/shard_map/ppermute | solution.py:371
  19.0 5.3 %collective-permute-start.19 = (bf16[4,16,1024]{2,1,0:T(8,128)(2,1)S(1)}, bf16[4,16,1024]{2,1,0:T(8,128)(2,1)S(1)}, u32[]{:S(2)}, u32[]{:S(2)}) collective-permute-start(bf16[4,16,1024]{2,1,0:T(8,128)(2,1)S(1)} %collective-permute-done.18.refs_4_), channel_id=1, source_target_pairs={{0,2},{4,0},{8,4},{12,8},{14,12},{10,14},{6,10},{2,6},{1,3},{5,1},... | collective-permute-start | bytes 393224 | tf_op jit(solution)/shard_map/ppermute | solution.py:371
  20.9 6.9 %collective-permute-start.1 = (bf16[4,16,1024]{2,1,0:T(8,128)(2,1)S(1)}, bf16[4,16,1024]{2,1,0:T(8,128)(2,1)S(1)}, u32[]{:S(2)}, u32[]{:S(2)}) collective-permute-start(bf16[4,16,1024]{2,1,0:T(8,128)(2,1)S(1)} %edge.1.refs_1_), channel_id=1, source_target_pairs={{0,2},{4,0},{8,4},{12,8},{14,12},{10,14},{6,10},{2,6},{1,3},{5,1},... | collective-permute-start | bytes 393224 | tf_op jit(solution)/shard_map/ppermute | solution.py:371
  22.5 6.9 %collective-permute-start.5 = (bf16[4,16,1024]{2,1,0:T(8,128)(2,1)S(1)}, bf16[4,16,1024]{2,1,0:T(8,128)(2,1)S(1)}, u32[]{:S(2)}, u32[]{:S(2)}) collective-permute-start(bf16[4,16,1024]{2,1,0:T(8,128)(2,1)S(1)} %collective-permute-done.4.refs_8_), channel_id=1, source_target_pairs={{0,4},{4,8},{8,12},{12,14},{14,10},{10,6},{6,2},{2,0},{1,5},{5,9},... | collective-permute-start | bytes 393224 | tf_op jit(solution)/shard_map/ppermute | solution.py:371
  26.2 10.2 %collective-permute-start.26 = (bf16[520,128]{1,0:T(8,128)(2,1)S(1)}, bf16[520,128]{1,0:T(8,128)(2,1)}, u32[]{:S(2)}, u32[]{:S(2)}) collective-permute-start(bf16[520,128]{1,0:T(8,128)(2,1)S(1)} %get-tuple-element.45), channel_id=1, source_target_pairs={{0,2},{4,0},{8,4},{12,8},{14,12},{10,14},{6,10},{2,6},{1,3},{5,1},... | collective-permute-start | bytes 399368 | tf_op jit(solution)/shard_map/ppermute | solution.py:371
  27.9 6.4 %collective-permute-start.2 = (bf16[4,16,1024]{2,1,0:T(8,128)(2,1)S(1)}, bf16[4,16,1024]{2,1,0:T(8,128)(2,1)S(1)}, u32[]{:S(2)}, u32[]{:S(2)}) collective-permute-start(bf16[4,16,1024]{2,1,0:T(8,128)(2,1)S(1)} %collective-permute-done.1.refs_2_), channel_id=1, source_target_pairs={{0,2},{4,0},{8,4},{12,8},{14,12},{10,14},{6,10},{2,6},{1,3},{5,1},... | collective-permute-start | bytes 393224 | tf_op jit(solution)/shard_map/ppermute | solution.py:371
  29.4 6.5 %collective-permute-start.6 = (bf16[4,16,1024]{2,1,0:T(8,128)(2,1)S(1)}, bf16[4,16,1024]{2,1,0:T(8,128)(2,1)}, u32[]{:S(2)}, u32[]{:S(2)}) collective-permute-start(bf16[4,16,1024]{2,1,0:T(8,128)(2,1)S(1)} %collective-permute-done.5.refs_7_), channel_id=1, source_target_pairs={{0,4},{4,8},{8,12},{12,14},{14,10},{10,6},{6,2},{2,0},{1,5},{5,9},... | collective-permute-start | bytes 393224 | tf_op jit(solution)/shard_map/ppermute | solution.py:371
  29.9 9.1 %collective-permute-start.23 = (bf16[520,128]{1,0:T(8,128)(2,1)S(1)}, bf16[520,128]{1,0:T(8,128)(2,1)S(1)}, u32[]{:S(2)}, u32[]{:S(2)}) collective-permute-start(bf16[520,128]{1,0:T(8,128)(2,1)S(1)} %get-tuple-element.41), channel_id=1, source_target_pairs={{0,4},{4,8},{8,12},{12,14},{14,10},{10,6},{6,2},{2,0},{1,5},{5,9},... | collective-permute-start | bytes 399368 | tf_op jit(solution)/shard_map/ppermute | solution.py:371
  34.2 5.3 %collective-permute-start.3 = (bf16[4,16,1024]{2,1,0:T(8,128)(2,1)S(1)}, bf16[4,16,1024]{2,1,0:T(8,128)(2,1)S(1)}, u32[]{:S(2)}, u32[]{:S(2)}) collective-permute-start(bf16[4,16,1024]{2,1,0:T(8,128)(2,1)S(1)} %collective-permute-done.2.refs_3_), channel_id=1, source_target_pairs={{0,2},{4,0},{8,4},{12,8},{14,12},{10,14},{6,10},{2,6},{1,3},{5,1},... | collective-permute-start | bytes 393224 | tf_op jit(solution)/shard_map/ppermute | solution.py:371
  35.9 5.5 %collective-permute-start.7 = (bf16[4,16,1024]{2,1,0:T(8,128)(2,1)}, bf16[4,16,1024]{2,1,0:T(8,128)(2,1)S(1)}, u32[]{:S(2)}, u32[]{:S(2)}) collective-permute-start(bf16[4,16,1024]{2,1,0:T(8,128)(2,1)} %collective-permute-done.6.refs_6_), channel_id=1, source_target_pairs={{0,4},{4,8},{8,12},{12,14},{14,10},{10,6},{6,2},{2,0},{1,5},{5,9},... | collective-permute-start | bytes 393224 | tf_op jit(solution)/shard_map/ppermute | solution.py:371
  37.3 9.0 %collective-permute-start.27 = (bf16[520,128]{1,0:T(8,128)(2,1)S(1)}, bf16[520,128]{1,0:T(8,128)(2,1)S(1)}, u32[]{:S(2)}, u32[]{:S(2)}) collective-permute-start(bf16[520,128]{1,0:T(8,128)(2,1)S(1)} %add_convert_fusion.2), channel_id=1, source_target_pairs={{0,2},{4,0},{8,4},{12,8},{14,12},{10,14},{6,10},{2,6},{1,3},{5,1},... | collective-permute-start | bytes 399368 | tf_op jit(solution)/shard_map/ppermute | solution.py:371
  39.0 9.0 %collective-permute-start.24 = (bf16[520,128]{1,0:T(8,128)(2,1)S(1)}, bf16[520,128]{1,0:T(8,128)(2,1)S(1)}, u32[]{:S(2)}, u32[]{:S(2)}) collective-permute-start(bf16[520,128]{1,0:T(8,128)(2,1)S(1)} %add_convert_fusion.4), channel_id=1, source_target_pairs={{0,4},{4,8},{8,12},{12,14},{14,10},{10,6},{6,2},{2,0},{1,5},{5,9},... | collective-permute-start | bytes 399368 | tf_op jit(solution)/shard_map/ppermute | solution.py:371
  44.3 5.0 %collective-permute-start.8 = (bf16[520,128]{1,0:T(8,128)(2,1)S(1)}, bf16[520,128]{1,0:T(8,128)(2,1)S(1)}, u32[]{:S(2)}, u32[]{:S(2)}) collective-permute-start(bf16[520,128]{1,0:T(8,128)(2,1)S(1)} %get-tuple-element.33), channel_id=1, source_target_pairs={{0,4},{4,8},{8,12},{12,14},{14,10},{10,6},{6,2},{2,0},{1,5},{5,9},... | collective-permute-start | bytes 399368 | tf_op jit(solution)/shard_map/ppermute | solution.py:371
  44.5 5.2 %collective-permute-start.12 = (bf16[520,128]{1,0:T(8,128)(2,1)S(1)}, bf16[520,128]{1,0:T(8,128)(2,1)S(1)}, u32[]{:S(2)}, u32[]{:S(2)}) collective-permute-start(bf16[520,128]{1,0:T(8,128)(2,1)S(1)} %get-tuple-element.36), channel_id=1, source_target_pairs={{0,2},{4,0},{8,4},{12,8},{14,12},{10,14},{6,10},{2,6},{1,3},{5,1},... | collective-permute-start | bytes 399368 | tf_op jit(solution)/shard_map/ppermute | solution.py:371
  46.4 20.5 %copy-start = (s32[16]{0:T(128)S(1)}, s32[16]{0:T(128)}, u32[]{:S(2)}) copy-start(s32[16]{0:T(128)} %parents_ref.1) | copy-start | bytes 196
  46.4 20.5 %copy-start.1 = (s32[8]{0:T(128)S(1)}, s32[8]{0:T(128)}, u32[]{:S(2)}) copy-start(s32[8]{0:T(128)} %counts_ref.1) | copy-start | bytes 100
  46.4 14.6 %collective-permute-start.28 = (bf16[520,128]{1,0:T(8,128)(2,1)S(1)}, bf16[520,128]{1,0:T(8,128)(2,1)S(1)}, u32[]{:S(2)}, u32[]{:S(2)}) collective-permute-start(bf16[520,128]{1,0:T(8,128)(2,1)S(1)} %add_convert_fusion.1), channel_id=1, source_target_pairs={{0,2},{4,0},{8,4},{12,8},{14,12},{10,14},{6,10},{2,6},{1,3},{5,1},... | collective-permute-start | bytes 399368 | tf_op jit(solution)/shard_map/ppermute | solution.py:371
  48.1 17.6 %collective-permute-start.25 = (bf16[520,128]{1,0:T(8,128)(2,1)S(1)}, bf16[520,128]{1,0:T(8,128)(2,1)S(1)}, u32[]{:S(2)}, u32[]{:S(2)}) collective-permute-start(bf16[520,128]{1,0:T(8,128)(2,1)S(1)} %add_convert_fusion.3), channel_id=1, source_target_pairs={{0,4},{4,8},{8,12},{12,14},{14,10},{10,6},{6,2},{2,0},{1,5},{5,9},... | collective-permute-start | bytes 399368 | tf_op jit(solution)/shard_map/ppermute | solution.py:371
  49.3 6.1 %collective-permute-start.9 = (bf16[520,128]{1,0:T(8,128)(2,1)S(1)}, bf16[520,128]{1,0:T(8,128)(2,1)S(1)}, u32[]{:S(2)}, u32[]{:S(2)}) collective-permute-start(bf16[520,128]{1,0:T(8,128)(2,1)S(1)} %add_convert_fusion.9), channel_id=1, source_target_pairs={{0,4},{4,8},{8,12},{12,14},{14,10},{10,6},{6,2},{2,0},{1,5},{5,9},... | collective-permute-start | bytes 399368 | tf_op jit(solution)/shard_map/ppermute | solution.py:371
  49.7 6.2 %collective-permute-start.13 = (bf16[520,128]{1,0:T(8,128)(2,1)S(1)}, bf16[520,128]{1,0:T(8,128)(2,1)S(1)}, u32[]{:S(2)}, u32[]{:S(2)}) collective-permute-start(bf16[520,128]{1,0:T(8,128)(2,1)S(1)} %add_convert_fusion.6), channel_id=1, source_target_pairs={{0,2},{4,0},{8,4},{12,8},{14,12},{10,14},{6,10},{2,6},{1,3},{5,1},... | collective-permute-start | bytes 399368 | tf_op jit(solution)/shard_map/ppermute | solution.py:371
  55.5 5.0 %collective-permute-start.10 = (bf16[520,128]{1,0:T(8,128)(2,1)S(1)}, bf16[520,128]{1,0:T(8,128)(2,1)S(1)}, u32[]{:S(2)}, u32[]{:S(2)}) collective-permute-start(bf16[520,128]{1,0:T(8,128)(2,1)S(1)} %add_convert_fusion.8), channel_id=1, source_target_pairs={{0,4},{4,8},{8,12},{12,14},{14,10},{10,6},{6,2},{2,0},{1,5},{5,9},... | collective-permute-start | bytes 399368 | tf_op jit(solution)/shard_map/ppermute | solution.py:371
  55.9 6.8 %collective-permute-start.14 = (bf16[520,128]{1,0:T(8,128)(2,1)S(1)}, bf16[520,128]{1,0:T(8,128)(2,1)S(1)}, u32[]{:S(2)}, u32[]{:S(2)}) collective-permute-start(bf16[520,128]{1,0:T(8,128)(2,1)S(1)} %add_convert_fusion.5), channel_id=1, source_target_pairs={{0,2},{4,0},{8,4},{12,8},{14,12},{10,14},{6,10},{2,6},{1,3},{5,1},... | collective-permute-start | bytes 399368 | tf_op jit(solution)/shard_map/ppermute | solution.py:371
  60.6 5.0 %collective-permute-start.11 = (bf16[520,128]{1,0:T(8,128)(2,1)S(1)}, bf16[520,128]{1,0:T(8,128)(2,1)S(1)}, u32[]{:S(2)}, u32[]{:S(2)}) collective-permute-start(bf16[520,128]{1,0:T(8,128)(2,1)S(1)} %add_convert_fusion.7), channel_id=1, source_target_pairs={{0,4},{4,8},{8,12},{12,14},{14,10},{10,6},{6,2},{2,0},{1,5},{5,9},... | collective-permute-start | bytes 399368 | tf_op jit(solution)/shard_map/ppermute | solution.py:371
  61.0 5.0 %collective-permute-start.29 = (bf16[520,128]{1,0:T(8,128)(2,1)S(1)}, bf16[520,128]{1,0:T(8,128)(2,1)S(1)}, u32[]{:S(2)}, u32[]{:S(2)}) collective-permute-start(bf16[520,128]{1,0:T(8,128)(2,1)S(1)} %add_convert_fusion), channel_id=1, source_target_pairs={{0,2},{4,0},{8,4},{12,8},{14,12},{10,14},{6,10},{2,6},{1,3},{5,1},... | collective-permute-start | bytes 399368 | tf_op jit(solution)/shard_map/ppermute | solution.py:371
  65.6 1.3 %collective-permute-start.15 = (bf16[128,128]{1,0:T(8,128)(2,1)S(1)}, bf16[128,128]{1,0:T(8,128)(2,1)S(1)}, u32[]{:S(2)}, u32[]{:S(2)}) collective-permute-start(bf16[128,128]{1,0:T(8,128)(2,1)S(1)} %add_convert_fusion.10), channel_id=1, source_target_pairs={{0,1},{1,0},{2,3},{3,2},{4,5},{5,4},{6,7},{7,6},{8,9},{9,8},{10,11... | collective-permute-start | bytes 98312 | tf_op jit(solution)/shard_map/ppermute | solution.py:343
